TPU v7x, 128 devices: a whole 4x4x4 slice. The times are simulated.
128 devices in a mesh: row: 8 (over z, y_lo), col: 16 (over x, y_hi, core).
Axes of the slice: x: 4, y: 4 (y_hi: 2, y_lo: 2; y = y_hi * 2 + y_lo), z: 4, core: 2. Of those that a mesh axis runs over, the one named last changes fastest.
Arguments:
- covariance: float32 [16384, 16384], P('row', 'col'), may hold values from -1 to 3, as said below
- center: float32 [16384], replicated, may hold values from 0.4 to 1
- links: float32 [4, 16384], replicated, may hold values from 0.05 to 0.25
- process: float32 [16384], replicated, may hold values from 0.1 to 1
- wells: int32 [1, 256], replicated, may hold values from 0 to 16383, as said below
- noise: float32 [1, 256], replicated, may hold values from 0.05 to 0.5
Outputs:
- updated: float32 [16384, 16384], P('row', 'col')
Inputs may be any that keep to these rules, and one draw needn't show every extreme that they name: `covariance`: symmetric positive definite. `wells`: each row holds 256 distinct cells; at most 32 of them lie in one aligned block of 1024 cells, and exactly 32 in some block.
All inputs are finite; a program needn't handle non-finite values.
Results may differ from a plain program's by a relative error of at most 0.0001.
Values sent between devices are 32-bit elements; how exact they have to be, the bound alone decides.
No kernel may reach another device: no remote copies, remote signals or barrier semaphores. Data moves between devices by JAX's collectives and lax.ppermute only.
A program may use at most 128 MiB of HBM per device.

v0:
```python
import jax
import jax.numpy as jnp
from jax import lax
from jax.sharding import PartitionSpec as P

NGY = 128
M = 256
WMAX = 32


def extended(cells, sides, width):
    for axis, dim in sides:
        count = lax.axis_size(axis)
        ends = count - 1
        head = lax.slice_in_dim(cells, 0, width, axis=dim)
        tail = lax.slice_in_dim(cells, cells.shape[dim] - width, cells.shape[dim], axis=dim)
        cells = jnp.concatenate(
            [
                lax.ppermute(tail, axis, [(i, (i + 1) % count) for i in range(ends)]),
                cells,
                lax.ppermute(head, axis, [((i + 1) % count, i) for i in range(ends)]),
            ],
            axis=dim,
        )
    return cells


def rows_first(arrays, axis, dims):
    turned = [jnp.moveaxis(a, dim, 0) for a, dim in zip(arrays, dims)]
    widths = [t[0].size for t in turned]
    both = jnp.concatenate([t.reshape(-1, w) for t, w in zip(turned, widths)], axis=1)
    result = lax.all_gather(both, axis, axis=0, tiled=True)
    blocks = jnp.split(result, [sum(widths[:k]) for k in range(1, len(widths))], axis=1)
    return tuple(
        (
            jnp.moveaxis(b.reshape(-1, *t.shape[1:]), 0, dim)
            for b, t, dim in zip(blocks, turned, dims)
        )
    )


def shards(covariance, center, links, process, wells, noise):
    row_id = lax.axis_index("row")
    col_id = lax.axis_index("col")
    row_count, col_count = covariance.shape
    grid_rows = row_count // NGY
    grid_cols = col_count // NGY
    row_start = row_id * row_count
    col_start = col_id * col_count
    own_rows = lax.dynamic_slice_in_dim(center, row_start, row_count).reshape(grid_rows, NGY, 1)
    link_rows = lax.dynamic_slice_in_dim(links, row_start, row_count, 1).reshape(
        4, grid_rows, NGY, 1
    )
    own_cols = lax.dynamic_slice_in_dim(center, col_start, col_count).reshape(1, grid_cols, NGY)
    link_cols = lax.dynamic_slice_in_dim(links, col_start, col_count, 1).reshape(
        4, 1, grid_cols, NGY
    )
    noise_rows = lax.dynamic_slice_in_dim(process, row_start, row_count)
    local_rows = jnp.arange(row_count, dtype=jnp.int32)
    diag_cols = row_start + local_rows - col_start
    diag_valid = (diag_cols >= 0) & (diag_cols < col_count)
    diag_clip = jnp.clip(diag_cols, 0, col_count - 1)
    diag_values = jnp.where(diag_valid, noise_rows, 0.0)
    current = covariance
    field = current.reshape(grid_rows, NGY, col_count)
    rimmed = extended(field, (("row", 0),), 1)
    padded = jnp.pad(rimmed, ((0, 0), (1, 1), (0, 0)))
    left = own_rows * field + link_rows[0] * padded[:-2, 1:-1] + link_rows[1] * padded[2:, 1:-1]
    left = left + link_rows[2] * padded[1:-1, :-2] + link_rows[3] * padded[1:-1, 2:]
    field = left.reshape(row_count, grid_cols, NGY)
    rimmed = extended(field, (("col", 1),), 1)
    padded = jnp.pad(rimmed, ((0, 0), (0, 0), (1, 1)))
    right = (
        own_cols * field + link_cols[0] * padded[:, :-2, 1:-1] + link_cols[1] * padded[:, 2:, 1:-1]
    )
    right = right + link_cols[2] * padded[:, 1:-1, :-2] + link_cols[3] * padded[:, 1:-1, 2:]
    predicted = right.reshape(row_count, col_count).at[local_rows, diag_clip].add(diag_values)
    chosen = wells[0]
    col_local = chosen - col_start
    in_col = (col_local >= 0) & (col_local < col_count)
    col_clip = jnp.clip(col_local, 0, col_count - 1)
    order = jnp.argsort(jnp.where(in_col, 0, 1).astype(jnp.int32), stable=True)[:WMAX]
    valid = in_col[order]
    compact = jnp.where(valid[None, :], jnp.take(predicted, col_clip[order], axis=1), 0.0)
    numbers = jnp.where(valid, order, -1).astype(jnp.float32)
    all_cols, all_numbers = rows_first((compact, numbers), "col", (1, 0))
    onehot = (all_numbers[:, None] == jnp.arange(M, dtype=jnp.float32)[None, :]).astype(jnp.float32)
    strip = jnp.dot(all_cols, onehot, precision=lax.Precision.HIGHEST)
    row_local = chosen - row_start
    in_row = (row_local >= 0) & (row_local < row_count)
    row_clip = jnp.clip(row_local, 0, row_count - 1)
    rows_part = jnp.where(in_row[:, None], jnp.take(predicted, row_clip, axis=0), 0.0)
    gram_part = jnp.where(in_row[:, None], jnp.take(strip, row_clip, axis=0), 0.0)
    across, gram = lax.psum((rows_part, gram_part), "row")
    innovation = gram + jnp.diag(noise[0])
    factor = jnp.linalg.cholesky(innovation)
    solved = jax.scipy.linalg.cho_solve((factor, True), across)
    current = predicted - jnp.dot(strip, solved, precision=lax.Precision.HIGHEST)
    return current


def solution(mesh):
    in_specs = (P("row", "col"), P(), P(), P(), P(), P())
    out_specs = P("row", "col")
    return jax.shard_map(shards, mesh=mesh, in_specs=in_specs, out_specs=out_specs, check_vma=False)
```

profile of v0, /device:TPU:0, one launch (start us, length us, event | category | flops | bytes accessed | tf_op | source)
XLA Modules:
  0.0 419.2 jit_solution(4098314979119295900)
XLA Ops:
  7.8 3.6 collective-permute-start
  14.9 3.2 sort.17
  22.6 13.5 %collective-permute-done.1 = f32[1,128,1024]{2,1,0:T(8,128)S(1)} collective-permute-done((f32[1,128,1024]{2,1,0:T(8,128)S(1)}, f32[1,128,1024]{2,1,0:T(8,128)S(1)}, u32[]{:S(2)}, u32[]{:S(2)}) %collective-permute-start.1) | collective-permute-done | bytes 524320 | tf_op jit(solution)/shard_map/ppermute | solution.py:21
  36.1 4.3 %select_maximum_fusion.2 = f32[18,130,1024]{2,1,0:T(8,128)S(1)} fusion(f32[1,128,1024]{2,1,0:T(8,128)S(1)} %collective-permute-done.1, f32[16,128,1024]{2,1,0:T(8,128)} %bitcast.73, f32[1,128,1024]{2,1,0:T(8,128)S(1)} %collective-permute-done), kind=kLoop, calls=%fused_computation.15 | loop fusion | flops 19169280 | bytes 19021824 | tf_op jit(solution)/shard_map/concatenate | solution.py:17
  40.3 9.5 %fusion.9 = f32[16,128,1024]{2,1,0:T(8,128)S(1)} fusion(f32[18,130,1024]{2,1,0:T(8,128)S(1)} %select_maximum_fusion.2, f32[1,128,1024]{2,1,0:T(8,128)S(1)} %collective-permute-done.1, f32[16,128,1024]{2,1,0:T(8,128)} %bitcast.74, f32[1,128,1024]{2,1,0:T(8,128)S(1)} %collective-permute-done, f32[16,128]{1,0:T(8,128)S(1)} %bitcast.79, ...), kind=kLoop, calls=%fused_computation.30 | loop fusion | flops 23068672 | bytes 34643968 | tf_op jit(solution)/shard_map/add | solution.py:69
  49.9 2.1 copy.32
  52.0 3.4 copy-done.2
  62.0 4.8 %collective-permute-done.3 = f32[2048,1,128]{2,1,0:T(1,128)S(1)} collective-permute-done((f32[2048,1,128]{2,1,0:T(1,128)S(1)}, f32[2048,1,128]{2,1,0:T(1,128)S(1)}, u32[]{:S(2)}, u32[]{:S(2)}) %collective-permute-start.3) | collective-permute-done | bytes 1048608 | tf_op jit(solution)/shard_map/ppermute | solution.py:21
  66.8 23.3 %select_maximum_fusion = f32[2048,10,130]{2,1,0:T(8,128)} fusion(f32[2048,1,128]{2,1,0:T(1,128)S(1)} %collective-permute-done.3, f32[2048,8,128]{2,1,0:T(8,128)} %bitcast.71, f32[2048,1,128]{2,1,0:T(1,128)S(1)} %collective-permute-done.2), kind=kLoop, calls=%fused_computation.10 | loop fusion | flops 21299200 | bytes 21135360 | tf_op jit(solution)/shard_map/concatenate | solution.py:17
  90.0 32.2 %fusion.3 = f32[2097152]{0:T(1024)} fusion(f32[2048,10,130]{2,1,0:T(8,128)} %select_maximum_fusion, f32[2048,1,128]{2,1,0:T(1,128)S(1)} %collective-permute-done.3, f32[2048,8,128]{2,1,0:T(8,128)} %bitcast.72, f32[2048,1,128]{2,1,0:T(1,128)S(1)} %collective-permute-done.2, f32[8,128]{1,0:T(8,128)S(1)} %bitcast.83, f32[8,128]{1,0:T(8,128)S(1)} %bitcast.81, ...), kind=kLoop, calls=%fused_computation.20 | loop fusion | flops 23068672 | bytes 35672064
  122.3 16.9 %scatter_fusion = f32[2097152]{0:T(1024)} fusion(f32[2097152]{0:T(1024)} %fusion.3, s32[2048]{0:T(1024)S(1)} %broadcast_select_fusion, f32[2048]{0:T(1024)S(1)} %dynamic-slice_select_fusion), kind=kCustom, calls=%fused_computation.5 | custom fusion | flops 2048 | bytes 32768
  139.1 9.2 %reshape.178 = f32[2048,1024]{1,0:T(8,128)} reshape(f32[2097152]{0:T(1024)} %scatter_fusion) | data formatting | bytes 16777216 | tf_op jit(solution)/shard_map/scatter-add | solution.py:77
  148.4 9.1 %copy.23 = f32[2048,1024]{0,1:T(8,128)} copy(f32[2048,1024]{1,0:T(8,128)} %reshape.178) | data formatting | bytes 16777216 | tf_op jit(solution)/shard_map/scatter-add | solution.py:77
  157.5 4.2 gather_fusion.2
  162.8 5.0 %gather_fusion.4 = f32[256,1024]{1,0:T(8,128)S(1)} fusion(f32[2048,1024]{1,0:T(8,128)} %reshape.178, s32[1024]{0:T(1024)S(1)} %pad_clamp_fusion), kind=kCustom, calls=%fused_computation.4 | custom fusion | bytes 2098176 | tf_op jit(solution)/shard_map/jit(_take)/gather | solution.py:92
  168.9 72.6 %all-gather.2.cloned.1.call-done = f32[512,2049]{1,0:T(8,128)} async-done(((f32[32,2049]{1,0:T(8,128)}), f32[512,2049]{1,0:T(8,128)}) %all-gather.2.cloned.1.call-update) | async-done | bytes 4196368 | tf_op jit(solution)/shard_map/all_gather | solution.py:32
  242.7 5.7 %fusion.15 = f32[2048,256]{1,0:T(8,128)S(1)} fusion(f32[512,2049]{1,0:T(8,128)} %all-gather.2.cloned.1.call-done, f32[512]{0:T(512)S(1)} %slice_reduce_fusion), kind=kOutput, calls=%fused_computation.40 | convolution fusion | flops 3221356544 | bytes 6293504 | tf_op jit(solution)/shard_map/dot_general | solution.py:88
  250.3 82.6 %all-reduce.6.cloned.1.call-done = (f32[256,1024]{1,0:T(8,128)}, f32[256,256]{0,1:T(8,128)}) async-done(((f32[256,1024]{1,0:T(8,128)}, f32[256,256]{0,1:T(8,128)}), (f32[256,1024]{1,0:T(8,128)}, f32[256,256]{0,1:T(8,128)})) %all-reduce.6.cloned.1.call-update) | async-done | bytes 1310736 | tf_op jit(solution)/shard_map/psum | solution.py:94
  334.9 11.7 %cholesky.48 = f32[128,128]{1,0:T(8,128)S(1)} custom-call(f32[128,128]{1,0:T(8,128)S(1)} %cholesky.112), custom_call_target="Cholesky" | custom-call | tf_op jit(solution)/shard_map/jit(cholesky)/cholesky | solution.py:96
  346.7 9.8 %custom-call.18 = f32[1,128,128]{1,2,0:T(8,128)S(1)} custom-call(f32[1,128,128]{2,1,0:T(8,128)S(1)} %get-tuple-element.56), custom_call_target="InvertDiagBlocksLowerTriangular" | custom-call | tf_op jit(solution)/shard_map/jit(cholesky)/cholesky | solution.py:96
  357.0 11.9 %cholesky.101 = f32[128,128]{1,0:T(8,128)S(1)} custom-call(f32[128,128]{1,0:T(8,128)S(1)} %convolution_subtract_fusion.3), custom_call_target="Cholesky" | custom-call | tf_op jit(solution)/shard_map/jit(cholesky)/cholesky | solution.py:96
  371.4 4.3 %while.1 = (s32[]{:T(128)}, f32[256,256]{0,1:T(8,128)S(1)}, s32[2,2]{1,0:T(2,128)S(1)}, f32[2,128,128]{2,1,0:T(8,128)S(1)}, s32[]{:T(128)}) while((s32[]{:T(128)}, f32[256,256]{0,1:T(8,128)S(1)}, s32[2,2]{1,0:T(2,128)S(1)}, f32[2,128,128]{2,1,0:T(8,128)S(1)}, s32[]{:T(128)}) %tuple.34), condition=%wide.while_cond, body=%wide.while_body.sunk | while | flops 2 | bytes 393321 | solution.py:97
  375.7 19.7 %custom-call.19 = f32[2,128,128]{1,2,0:T(8,128)S(1)} custom-call(f32[2,128,128]{2,1,0:T(8,128)S(1)} %get-tuple-element.14), custom_call_target="InvertDiagBlocksLowerTriangular" | custom-call | tf_op jit(solution)/shard_map/jit(_cho_solve)/triangular_solve | solution.py:97
  401.1 11.0 %convolution_subtract_fusion = f32[2048,1024]{1,0:T(8,128)} fusion(f32[2048,1024]{1,0:T(8,128)} %reshape.178, f32[2048,256]{1,0:T(8,128)S(1)} %fusion.15, f32[128,1024]{1,0:T(8,128)S(1)} %fusion.28, f32[128,1024]{1,0:T(8,128)S(1)} %fusion.27), kind=kOutput, calls=%fused_computation.39 | convolution fusion | flops 6444810240 | bytes 19922944 | tf_op jit(solution)/shard_map/dot_general | solution.py:98
  (92 shorter events, 34.6 us)
Async XLA Ops:
  6.5 7.6 %copy-start = (f32[16384]{0:T(1024)S(1)}, f32[16384]{0:T(1024)}, u32[]{:S(2)}) copy-start(f32[16384]{0:T(1024)} %param.7) | copy-start | bytes 196612
  6.5 235.0 %all-gather.2.cloned.1.call-start = ((), (), s32[]{:S(2)}) async-start(), calls=%async_computation | async-start | bytes 4734976 | tf_op jit(solution)/shard_map/all_gather | solution.py:32
  7.8 14.7 %collective-permute-start = (f32[1,128,1024]{2,1,0:T(8,128)S(1)}, f32[1,128,1024]{2,1,0:T(8,128)S(1)}, u32[]{:S(2)}, u32[]{:S(2)}) collective-permute-start(f32[1,128,1024]{2,1,0:T(8,128)S(1)} %get-tuple-element.45), channel_id=1, source_target_pairs={{0,16},{16,32},{32,48},{48,64},{64,80},{80,96},{96,112},{1,17},{17... | collective-permute-start | bytes 1572872 | tf_op jit(solution)/shard_map/ppermute | solution.py:19
  11.4 24.6 %collective-permute-start.1 = (f32[1,128,1024]{2,1,0:T(8,128)S(1)}, f32[1,128,1024]{2,1,0:T(8,128)S(1)}, u32[]{:S(2)}, u32[]{:S(2)}) collective-permute-start(f32[1,128,1024]{2,1,0:T(8,128)S(1)} %get-tuple-element.46), channel_id=1, source_target_pairs={{16,0},{32,16},{48,32},{64,48},{80,64},{96,80},{112,96},{17,1},{33... | collective-permute-start | bytes 1572872 | tf_op jit(solution)/shard_map/ppermute | solution.py:21
  49.9 11.8 %copy-start.6 = (s32[2]{0:T(128)S(1)}, s32[2]{0:T(128)}, u32[]{:S(2)}) copy-start(s32[2]{0:T(128)} %constant.169) | copy-start | bytes 28
  49.9 11.9 %copy-start.5 = (s32[2]{0:T(128)S(1)}, s32[2]{0:T(128)}, u32[]{:S(2)}) copy-start(s32[2]{0:T(128)} %constant.172) | copy-start | bytes 28
  52.0 3.4 copy-start.2
  57.5 4.5 %collective-permute-start.2 = (f32[2048,1,128]{2,1,0:T(1,128)}, f32[2048,1,128]{2,1,0:T(1,128)S(1)}, u32[]{:S(2)}, u32[]{:S(2)}) collective-permute-start(f32[2048,1,128]{2,1,0:T(1,128)} %get-tuple-element.43), channel_id=1, source_target_pairs={{0,1},{1,2},{2,3},{3,4},{4,5},{5,6},{6,7},{7,8},{8,9},{9,10},{10,1... | collective-permute-start | bytes 3145736 | tf_op jit(solution)/shard_map/ppermute | solution.py:19
  58.8 7.9 %collective-permute-start.3 = (f32[2048,1,128]{2,1,0:T(1,128)S(1)}, f32[2048,1,128]{2,1,0:T(1,128)S(1)}, u32[]{:S(2)}, u32[]{:S(2)}) collective-permute-start(f32[2048,1,128]{2,1,0:T(1,128)S(1)} %get-tuple-element.44), channel_id=1, source_target_pairs={{1,0},{2,1},{3,2},{4,3},{5,4},{6,5},{7,6},{8,7},{9,8},{10,9},{11,1... | collective-permute-start | bytes 3145736 | tf_op jit(solution)/shard_map/ppermute | solution.py:21
  157.5 5.3 %copy-start.3 = (s32[1,256]{1,0:T(1,128)S(1)}, s32[1,256]{1,0:T(1,128)}, u32[]{:S(2)}) copy-start(s32[1,256]{1,0:T(1,128)} %param.10) | copy-start | bytes 3076
  162.5 170.3 %all-reduce.6.cloned.1.call-start = ((), (), s32[]{:S(2)}) async-start(), calls=%async_computation.1 | async-start | bytes 2621440 | tf_op jit(solution)/shard_map/psum | solution.py:94
  167.8 165.1 %copy-start.4 = (f32[1,256]{1,0:T(1,128)S(1)}, f32[1,256]{1,0:T(1,128)}, u32[]{:S(2)}) copy-start(f32[1,256]{1,0:T(1,128)} %param.11) | copy-start | bytes 3076
  400.5 11.6 %copy-start.1 = (f32[16384]{0:T(1024)S(1)}, f32[16384]{0:T(1024)}, u32[]{:S(2)}) copy-start(f32[16384]{0:T(1024)} %param.7) | copy-start | bytes 196612
Sparse Core Ops, SparseCore 0:
  162.7 78.8 all-gather.1
  250.4 82.4 all-reduce.5
where the time goes:
time: 425 us; the launch traced here: 419 us
  waiting for transfers between devices  176 us (41%)
  other arithmetic  150 us (35%)
  local copies, waits for them, and re-layouts  46.8 us (11%)
  matrix products  22.9 us (5%)
  between operations  15.3 us (4%)
  starting transfers between devices  8.21 us (2%)
    psum x1, waiting for transfers between devices, shards(): across, gram = lax.psum((rows_part, gram_part), 'row')  82.6 us
    all_gather x1, waiting for transfers between devices, rows_first(): result = lax.all_gather(both, axis, axis=0, tiled=True)  72.6 us
    unnamed x6, other arithmetic  49.3 us
    another operation x6, other arithmetic, shards(): factor = jnp.linalg.cholesky(innovation)  34.2 us
    concatenate x2, other arithmetic, extended(): jnp.concatenate([lax.ppermute(tail, axis, [(i, (i + 1) % count) for i in...  27.6 us
    another operation x3, other arithmetic, shards(): solved = jax.scipy.linalg.cho_solve((factor, True), across)  19.7 us
    scatter-add x2, local copies, waits for them, and re-layouts, shards(): right.reshape(row_count, col_count).at[local_rows, diag_clip]  18.4 us
    ppermute x2, waiting for transfers between devices, extended(): lax.ppermute(head, axis, [((i + 1) % count, i) for i in range(ends)])  18.3 us
  transfers between devices with their start and end apart: 6, of which 5 were waited for; matrix products, arithmetic and copies ran while one was open for 4% of the time, Pallas kernels for 0%

commit v1 on v0

v1 whole, which is shorter than its diff:
```python
import functools

import jax
import jax.numpy as jnp
from jax import lax
from jax.experimental import pallas as pl
from jax.experimental.pallas import tpu as pltpu
from jax.sharding import PartitionSpec as P

NGY = 128
M = 256
WMAX = 32
ROWS = 8
COLS = 16
HALF = 2 * WMAX
SLOTS = ROWS * HALF
F32 = jnp.float32
BF16 = jnp.bfloat16
HI = lax.Precision.HIGHEST


def cost(flops, size):
    return pl.CostEstimate(flops=flops, bytes_accessed=size, transcendentals=0)


def vmem(count):
    return [pl.BlockSpec(memory_space=pltpu.VMEM)] * count


def rows_kernel(idx, coef, send, p_ref, z_ref, up_ref, dn_ref):
    def one(s, carry):
        i = idx[0, s]
        total = coef[0, s] * p_ref[pl.ds(i, 1), :]
        for k in range(1, 5):
            total = total + coef[k, s] * p_ref[pl.ds(idx[k, s], 1), :]
        z_ref[pl.ds(s, 1), :] = total
        return carry

    lax.fori_loop(0, HALF, one, 0)

    def two(s, carry):
        up_ref[pl.ds(s, 1), :] = p_ref[pl.ds(send[0, s], 1), :]
        dn_ref[pl.ds(s, 1), :] = p_ref[pl.ds(send[1, s], 1), :]
        return carry

    lax.fori_loop(0, WMAX, two, 0)


def well_rows(idx, coef, send, block):
    cols = block.shape[1]
    smem = pl.BlockSpec(memory_space=pltpu.SMEM)
    return pl.pallas_call(
        rows_kernel,
        out_shape=(
            jax.ShapeDtypeStruct((HALF, cols), F32),
            jax.ShapeDtypeStruct((WMAX, cols), F32),
            jax.ShapeDtypeStruct((WMAX, cols), F32),
        ),
        in_specs=[smem, smem, smem] + vmem(1),
        out_specs=tuple(vmem(3)),
        compiler_params=pltpu.CompilerParams(vmem_limit_bytes=24 << 20),
        cost_estimate=cost(10 * HALF * cols, block.size * 4),
        name="well_rows",
    )(idx, coef, send, block)


def across_lanes(parts, coef, lo, hi):
    out = []
    for t in range(lo, hi):
        left, mid, right = parts[t], parts[t + 1], parts[t + 2]
        c = coef[:, t * NGY : (t + 1) * NGY]
        total = c[0:1] * mid + c[1:2] * left + c[2:3] * right
        total = total + c[3:4] * pltpu.roll(mid, 1, 1) + c[4:5] * pltpu.roll(mid, NGY - 1, 1)
        out.append(total)
    return out


def cols_kernel(z_ref, zl_ref, zr_ref, coef_ref, diag_ref, proc_ref, target_ref, x_ref, g_ref):
    cols = z_ref.shape[1]
    tiles = cols // NGY
    parts = [zl_ref[...]] + [z_ref[:, t * NGY : (t + 1) * NGY] for t in range(tiles)] + [zr_ref[...]]
    out = across_lanes(parts, coef_ref[...], 0, tiles)
    x = jnp.concatenate(out, axis=1)
    lane = lax.broadcasted_iota(jnp.int32, x.shape, 1)
    x = x + jnp.where(lane == diag_ref[...], proc_ref[...], 0.0)
    x_ref[...] = x
    pick = lax.broadcasted_iota(jnp.int32, (cols, NGY), 0) == target_ref[...]
    g_ref[...] = jnp.dot(x, pick.astype(F32), precision=HI, preferred_element_type=F32)


def well_cols(z, zl, zr, coef, diag, proc, target):
    cols = z.shape[1]
    return pl.pallas_call(
        cols_kernel,
        out_shape=(
            jax.ShapeDtypeStruct((HALF, cols), F32),
            jax.ShapeDtypeStruct((HALF, NGY), F32),
        ),
        in_specs=vmem(7),
        out_specs=tuple(vmem(2)),
        cost_estimate=cost(12 * HALF * cols * NGY, 4 * HALF * cols * 4),
        name="well_cols",
    )(z, zl, zr, coef, diag, proc, target)


def predict_kernel(start, p_ref, up_ref, dn_ref, el_ref, er_ref, rc_ref, cc_ref, proc_ref, o_ref):
    g = pl.program_id(0)
    last = pl.num_programs(0) - 1
    cols = p_ref.shape[1]
    tiles = cols // NGY
    here = pl.multiple_of(g * NGY, NGY)
    before = pl.multiple_of(jnp.maximum(g - 1, 0) * NGY, NGY)
    after = pl.multiple_of(jnp.minimum(g + 1, last) * NGY, NGY)
    wide = (NGY, NGY)
    rc = [jnp.broadcast_to(rc_ref[:, k : k + 1], wide) for k in range(5)]

    def left_tile(mid, above, below):
        total = rc[0] * mid + rc[1] * above + rc[2] * below
        return total + rc[3] * pltpu.roll(mid, 1, 0) + rc[4] * pltpu.roll(mid, NGY - 1, 0)

    parts = []
    for ref, t in [(el_ref, None)] + [(p_ref, t) for t in range(tiles)] + [(er_ref, None)]:
        if t is None:
            mid = ref[pl.ds(here + NGY, NGY), :]
            above = ref[pl.ds(here, NGY), :]
            below = ref[pl.ds(here + 2 * NGY, NGY), :]
        else:
            lanes = slice(t * NGY, (t + 1) * NGY)
            mid = p_ref[pl.ds(here, NGY), lanes]
            above = jnp.where(g == 0, up_ref[:, lanes], p_ref[pl.ds(before, NGY), lanes])
            below = jnp.where(g == last, dn_ref[:, lanes], p_ref[pl.ds(after, NGY), lanes])
        parts.append(left_tile(mid, above, below))
        if len(parts) >= 3:
            k = len(parts) - 3
            o_ref[:, k * NGY : (k + 1) * NGY] = across_lanes(parts, cc_ref[...], k, k + 1)[0]
    hit = start[0] + g
    eye = lax.broadcasted_iota(jnp.int32, wide, 0) == lax.broadcasted_iota(jnp.int32, wide, 1)
    for t in range(tiles):

        @pl.when(hit == t)
        def _():
            lanes = slice(t * NGY, (t + 1) * NGY)
            o_ref[:, lanes] = o_ref[:, lanes] + jnp.where(eye, proc_ref[:, lanes], 0.0)


def predict(start, block, up, dn, el, er, row_coef, col_coef, proc):
    rows, cols = block.shape
    steps = rows // NGY
    return pl.pallas_call(
        predict_kernel,
        out_shape=jax.ShapeDtypeStruct((rows, cols), F32),
        grid_spec=pltpu.PrefetchScalarGridSpec(
            num_scalar_prefetch=1,
            grid=(steps,),
            in_specs=vmem(5)
            + [pl.BlockSpec((NGY, 8), lambda g, s: (g, 0))]
            + vmem(2),
            out_specs=pl.BlockSpec((NGY, cols), lambda g, s: (g, 0)),
        ),
        compiler_params=pltpu.CompilerParams(vmem_limit_bytes=32 << 20),
        cost_estimate=cost(22 * rows * cols, 8 * rows * cols),
        name="predict",
    )(start, block, up, dn, el, er, row_coef, col_coef, proc)


BLK = 32


def small_inverse(d):
    size = d.shape[0]
    sub = lax.broadcasted_iota(jnp.int32, d.shape, 0)
    lane = lax.broadcasted_iota(jnp.int32, d.shape, 1)
    for j in range(size):
        row = d[j : j + 1, :]
        col = d[:, j : j + 1]
        inv = 1.0 / d[j : j + 1, j : j + 1]
        row = jnp.where(lane[0:1] == j, 1.0, row) * inv
        col = jnp.where(sub[:, 0:1] == j, -1.0, col)
        d = jnp.where((sub == j) | (lane == j), 0.0, d) - col * row
    return d


def dot(a, b):
    return jnp.dot(a, b, precision=HI, preferred_element_type=F32)


def inverse_kernel(own_ref, other_ref, rslot_ref, cslot_ref, noise_ref, o_ref, s_ref):
    rows_in = ROWS * HALF
    pick_rows = (lax.broadcasted_iota(jnp.int32, (M, rows_in), 1) == rslot_ref[...]).astype(F32)
    total = jnp.zeros((M, M), F32)
    for k, ref in enumerate((own_ref, other_ref)):
        for h in range(2):
            piece = ref[:, h].reshape(rows_in, NGY)
            some = dot(pick_rows, piece)
            base = (2 * k + h) * NGY
            pick = lax.broadcasted_iota(jnp.int32, (NGY, M), 0) + base == cslot_ref[...]
            total = total + dot(some, pick.astype(F32))
    i0 = lax.broadcasted_iota(jnp.int32, (M, M), 0)
    i1 = lax.broadcasted_iota(jnp.int32, (M, M), 1)
    s_ref[...] = total + jnp.where(i0 == i1, noise_ref[...], 0.0)
    sub = lax.broadcasted_iota(jnp.int32, (M, BLK), 0)
    for b in range(M // BLK):
        lo = b * BLK
        inv = small_inverse(s_ref[lo : lo + BLK, lo : lo + BLK])
        panel = s_ref[lo : lo + BLK, :]
        col = s_ref[:, lo : lo + BLK]
        here = (i1[0:BLK] >= lo) & (i1[0:BLK] < lo + BLK)
        scaled = dot(inv, panel)
        inside = (sub >= lo) & (sub < lo + BLK)
        upd = dot(jnp.where(inside, 0.0, col), scaled)
        down = dot(col, inv)
        s_ref[...] = s_ref[...] - upd
        s_ref[:, lo : lo + BLK] = -down
        s_ref[lo : lo + BLK, :] = scaled
        s_ref[lo : lo + BLK, lo : lo + BLK] = inv
    o_ref[...] = s_ref[...]


def inverse(own, other, rslot, cslot, noise):
    return pl.pallas_call(
        inverse_kernel,
        out_shape=jax.ShapeDtypeStruct((M, M), F32),
        in_specs=vmem(5),
        out_specs=vmem(1)[0],
        scratch_shapes=[pltpu.VMEM((M, M), F32)],
        compiler_params=pltpu.CompilerParams(vmem_limit_bytes=24 << 20),
        cost_estimate=cost(2 * 1153000000 * 8, 4 << 20),
        name="inverse",
    )(own, other, rslot, cslot, noise)


def split(x):
    high = x.astype(BF16)
    return high, (x - high.astype(F32)).astype(BF16)


def bdot(a, b, dims=((1,), (0,))):
    return lax.dot_general(a, b, (dims, ((), ())), preferred_element_type=F32)


def update_kernel(pred_ref, xc_ref, xr_ref, inv_ref, cslot_ref, rslot_ref, o_ref, uh, ul, sh, sl):
    j = pl.program_id(1)

    @pl.when((pl.program_id(0) == 0) & (j == 0))
    def _():
        pick = (lax.broadcasted_iota(jnp.int32, (M, SLOTS), 1) == cslot_ref[...]).astype(F32)
        across = dot(pick, xc_ref[...])
        high, low = split(dot(inv_ref[...], across))
        uh[...] = high
        ul[...] = low

    @pl.when(j == 0)
    def _():
        size = xr_ref.shape[-1]
        strip = xr_ref[...].reshape(SLOTS, size)
        pick = (lax.broadcasted_iota(jnp.int32, (SLOTS, M), 0) == rslot_ref[...]).astype(BF16)
        high, low = split(strip)
        sh[...] = bdot(high, pick, ((0,), (0,))).astype(BF16)
        sl[...] = bdot(low, pick, ((0,), (0,))).astype(BF16)

    size = o_ref.shape[0]
    rows = pl.ds(pl.multiple_of(j * size, size), size)
    a, b = sh[rows, :], sl[rows, :]
    o_ref[...] = pred_ref[...] - (bdot(a, uh[...]) + (bdot(a, ul[...]) + bdot(b, uh[...])))


def update(pred, xc, xr, inv, cslot, rslot):
    rows, cols = pred.shape
    tile = 256
    half = rows // 2
    steps = half // tile
    return pl.pallas_call(
        update_kernel,
        out_shape=jax.ShapeDtypeStruct((rows, cols), F32),
        grid=(2, steps),
        in_specs=[
            pl.BlockSpec((tile, cols), lambda k, j: (k * steps + j, 0)),
            pl.BlockSpec(memory_space=pltpu.VMEM),
            pl.BlockSpec((ROWS, None, HALF, half), lambda k, j: (0, k, 0, 0)),
        ]
        + vmem(3),
        out_specs=pl.BlockSpec((tile, cols), lambda k, j: (k * steps + j, 0)),
        scratch_shapes=[
            pltpu.VMEM((M, cols), BF16),
            pltpu.VMEM((M, cols), BF16),
            pltpu.VMEM((half, M), BF16),
            pltpu.VMEM((half, M), BF16),
        ],
        compiler_params=pltpu.CompilerParams(vmem_limit_bytes=40 << 20),
        cost_estimate=cost(6 * rows * cols * M, 8 * rows * cols),
        name="update",
    )(pred, xc, xr, inv, cslot, rslot)


def shift(x, axis, count, back):
    return lax.ppermute(x, axis, [((i + back) % count, i) for i in range(count)])


def flip(x, axis, count, bit):
    return lax.ppermute(x, axis, [(i, i ^ bit) for i in range(count)])


def shards(covariance, center, links, process, wells, noise):
    r = lax.axis_index("row")
    c = lax.axis_index("col")
    rows, cols = covariance.shape
    cells = center.shape[0]
    row_start, col_start = r * rows, c * cols
    block = covariance

    w = wells[0]
    part = w // cols
    slot_i = jnp.arange(M, dtype=jnp.int32)
    same = (part[:, None] == part[None, :]) & (slot_i[None, :] < slot_i[:, None])
    rank = jnp.sum(same.astype(jnp.int32), axis=1)
    slot = part * WMAX + rank
    hits = slot[None, :] == jnp.arange(SLOTS, dtype=jnp.int32)[:, None]
    slot_cell = jnp.max(jnp.where(hits, w[None, :], -1), axis=1)

    gy = jnp.arange(cells, dtype=jnp.int32) % NGY
    coef = jnp.concatenate(
        [
            center[None],
            links[0:2],
            jnp.where(gy == 0, 0.0, links[2])[None],
            jnp.where(gy == NGY - 1, 0.0, links[3])[None],
            process[None],
        ]
    )
    col_coef = lax.dynamic_slice_in_dim(coef, col_start, cols, 1)
    row_coef = jnp.concatenate(
        [lax.dynamic_slice_in_dim(coef, row_start, rows, 1), jnp.zeros((2, rows), F32)]
    ).T

    mine = lax.dynamic_slice_in_dim(slot_cell, r * HALF, HALF)
    valid = mine >= 0
    safe = jnp.maximum(mine, 0)
    at = jnp.take(coef, safe, axis=1)
    at = jnp.where(valid[None, :], at, 0.0)
    local = jnp.where(valid, mine - row_start, 0)
    first = local < NGY
    final = local >= rows - NGY
    five = jnp.stack([local, local - NGY, local + NGY, local - 1, local + 1])
    idx = jnp.clip(five, 0, rows - 1)
    inside = jnp.stack([valid, ~first, ~final, valid, valid])
    row_scale = jnp.where(inside, at[:5], 0.0)
    above = jnp.where(first, at[1], 0.0)[:, None]
    below = jnp.where(final, at[2], 0.0)[:, None]
    padded = jnp.concatenate([jnp.zeros((WMAX,), jnp.int32), slot_cell, jnp.zeros((WMAX,), jnp.int32)])
    next_cells = lax.dynamic_slice_in_dim(padded, (r + 1) * HALF + WMAX, WMAX)
    prev_cells = lax.dynamic_slice_in_dim(padded, r * HALF, WMAX)
    send = jnp.clip(
        jnp.stack([next_cells - NGY, prev_cells + NGY]) - row_start, 0, rows - 1
    )

    z, send_up, send_dn = well_rows(idx, row_scale, send, block)
    got_up = lax.ppermute(send_up, "row", [(i, i + 1) for i in range(ROWS - 1)])
    got_dn = lax.ppermute(send_dn, "row", [(i + 1, i) for i in range(ROWS - 1)])
    z = jnp.concatenate(
        [z[:WMAX] + above[:WMAX] * got_up, z[WMAX:] + below[WMAX:] * got_dn]
    )
    zl = lax.ppermute(z[:, cols - NGY :], "col", [(i, i + 1) for i in range(COLS - 1)])
    zr = lax.ppermute(z[:, :NGY], "col", [(i + 1, i) for i in range(COLS - 1)])
    here = lax.dynamic_slice_in_dim(slot_cell, c * WMAX, WMAX) - col_start
    lane = jnp.arange(NGY, dtype=jnp.int32)
    xq = c // 4
    target = jnp.where(lane // WMAX == xq, jnp.tile(here, NGY // WMAX), -1)[None]
    x, g = well_cols(
        z, zl, zr, col_coef[:5], (mine - col_start)[:, None], at[5][:, None], target
    )

    xc = lax.all_gather(x, "row", axis=0, tiled=True)
    turn = [
        (a * COLS + 2 * b + k, b * COLS + 2 * a + k)
        for a in range(ROWS)
        for b in range(ROWS)
        for k in range(2)
    ]
    turned = lax.ppermute(x, ("row", "col"), turn)
    xr = lax.all_gather(turned, "col", axis=0, tiled=False).reshape(ROWS, 2, HALF, cols)

    g = g + shift(g, "col", COLS, 4) + shift(g, "col", COLS, 8) + shift(g, "col", COLS, 12)
    g = jnp.stack([g, flip(g, "col", COLS, 2)])
    g = jnp.stack([g, flip(g, "row", ROWS, 1)])
    g = jnp.stack([g] + [shift(g, "row", ROWS, 2 * d) for d in range(1, 4)])
    g = g.reshape(ROWS, 2, HALF, NGY)
    g_other = flip(g, "col", COLS, 1)
    wr, wc = slot // HALF, slot // WMAX
    z_rel = (wr // 2 - r // 2) % 4
    row_slot = (z_rel * 2 + (wr % 2 ^ r % 2)) * HALF + slot % HALF
    col_slot = (
        (wc % 2 ^ c % 2) * (2 * NGY)
        + ((wc // 2) % 2 ^ (c // 2) % 2) * NGY
        + (wc // 4) * WMAX
        + slot % WMAX
    )
    inv = inverse(g, g_other, row_slot[:, None], col_slot[None], noise)

    up = lax.ppermute(block[rows - NGY :], "row", [(i, i + 1) for i in range(ROWS - 1)])
    dn = lax.ppermute(block[:NGY], "row", [(i + 1, i) for i in range(ROWS - 1)])
    right_edge = jnp.concatenate([a[:, cols - NGY :] for a in (up, block, dn)])
    left_edge = jnp.concatenate([a[:, :NGY] for a in (up, block, dn)])
    el = lax.ppermute(right_edge, "col", [(i, i + 1) for i in range(COLS - 1)])
    er = lax.ppermute(left_edge, "col", [(i + 1, i) for i in range(COLS - 1)])
    start = ((row_start - col_start) // NGY)[None]
    pred = predict(start, block, up, dn, el, er, row_coef, col_coef[:5], col_coef[5:6])

    return update(pred, xc, xr, inv, slot[:, None], slot[None])


def solution(mesh):
    in_specs = (P("row", "col"), P(), P(), P(), P(), P())
    out_specs = P("row", "col")
    return jax.shard_map(shards, mesh=mesh, in_specs=in_specs, out_specs=out_specs, check_vma=False)
```

time: 425 us -> 233 us (0.55)
  the two profiles are of different devices: /device:TPU:0 before, /device:TPU:3 now
where the time goes in v1:
time: 233 us; the launch traced here: 232 us
  starting transfers between devices  81.4 us (35%)
  Pallas kernels  61.1 us (26%)
  waiting for transfers between devices  35.5 us (15%)
  local copies, waits for them, and re-layouts  31.7 us (14%)
  between operations  13.8 us (6%)
  other arithmetic  8.27 us (4%)
    pallas_call x1, Pallas kernels, inverse(): pl.pallas_call(inverse_kernel, out_shape=jax.ShapeDtypeStruct((M, M), F32...  29.7 us
    ppermute x6, starting transfers between devices, shift(): lax.ppermute(x, axis, [((i + back) % count, i) for i in range(count)])  25.4 us
    ppermute x3, starting transfers between devices, flip(): return lax.ppermute(x, axis, [(i, i ^ bit) for i in range(count)])  24.8 us
    pallas_call x1, Pallas kernels, update(): pl.pallas_call(update_kernel, out_shape=jax.ShapeDtypeStruct((rows, cols)...  14.8 us
    ppermute x3, waiting for transfers between devices, flip(): return lax.ppermute(x, axis, [(i, i ^ bit) for i in range(count)])  13.7 us
    unnamed x28, local copies, waits for them, and re-layouts  12.1 us
    pallas_call x1, Pallas kernels, predict(): pl.pallas_call(predict_kernel, out_shape=jax.ShapeDtypeStruct((rows, cols...  12.1 us
    ppermute x1, starting transfers between devices, shards(): lax.ppermute(block[rows - NGY:], 'row', [(i, i + 1) for i in range(ROWS -...  8.19 us
  transfers between devices with their start and end apart: 20, of which 9 were waited for; matrix products, arithmetic and copies ran while one was open for 5% of the time, Pallas kernels for 18%

profile of v1, /device:TPU:3, one launch (start us, length us, event | category | flops | bytes accessed | tf_op | source)
XLA Modules:
  0.0 231.8 jit_solution(17202901909979448953)
XLA Ops:
  13.3 5.3 %copy.23 = f32[6,16384]{0,1:T(8,128)} copy(f32[6,16384]{1,0:T(8,128)S(1)} %concatenate.20) | data formatting | bytes 786432 | tf_op jit(solution)/shard_map/concatenate | solution.py:321
  18.6 4.0 %gather_fusion = f32[64,6]{1,0:T(8,128)S(1)} fusion(f32[6,16384]{0,1:T(8,128)} %copy.23, s32[1024]{0:T(1024)S(1)} %pad_clamp_fusion), kind=kCustom, calls=%fused_computation | custom fusion | bytes 3328 | tf_op jit(solution)/shard_map/jit(_take)/gather | solution.py:338
  22.9 3.4 %copy-done = f32[2048,1024]{1,0:T(8,128)S(1)} copy-done((f32[2048,1024]{1,0:T(8,128)S(1)}, f32[2048,1024]{1,0:T(8,128)}, u32[]{:S(2)}) %copy-start) | copy-done | bytes 8388632
  28.6 3.2 %collective-permute-start.4 = (f32[32,1024]{1,0:T(8,128)S(1)}, f32[32,1024]{1,0:T(8,128)S(1)}, u32[]{:S(2)}, u32[]{:S(2)}) collective-permute-start(f32[32,1024]{1,0:T(8,128)S(1)} %get-tuple-element.11), channel_id=1, source_target_pairs={{0,16},{16,32},{32,48},{48,64},{64,80},{80,96},{96,112},{1,17},{17... | collective-permute-start | bytes 393224 | tf_op jit(solution)/shard_map/ppermute | solution.py:357
  36.0 3.3 %collective-permute-done.5 = f32[32,1024]{1,0:T(8,128)S(1)} collective-permute-done((f32[32,1024]{1,0:T(8,128)S(1)}, f32[32,1024]{1,0:T(8,128)S(1)}, u32[]{:S(2)}, u32[]{:S(2)}) %collective-permute-start.5) | collective-permute-done | bytes 131104 | tf_op jit(solution)/shard_map/ppermute | solution.py:358
  39.4 3.2 %collective-permute-start.7 = (f32[64,128]{1,0:T(8,128)S(1)}, f32[64,128]{1,0:T(8,128)S(1)}, u32[]{:S(2)}, u32[]{:S(2)}) collective-permute-start(f32[64,128]{1,0:T(8,128)S(1)} %get-tuple-element.31), channel_id=1, source_target_pairs={{1,0},{2,1},{3,2},{4,3},{5,4},{6,5},{7,6},{8,7},{9,8},{10,9},{11,1... | collective-permute-start | bytes 98312 | tf_op jit(solution)/shard_map/ppermute | solution.py:363
  42.6 4.7 %collective-permute-start.6 = (f32[64,128]{1,0:T(8,128)S(1)}, f32[64,128]{1,0:T(8,128)S(1)}, u32[]{:S(2)}, u32[]{:S(2)}) collective-permute-start(f32[64,128]{1,0:T(8,128)S(1)} %get-tuple-element.32), channel_id=1, source_target_pairs={{0,1},{1,2},{2,3},{3,4},{4,5},{5,6},{6,7},{7,8},{8,9},{9,10},{10,1... | collective-permute-start | bytes 98312 | tf_op jit(solution)/shard_map/ppermute | solution.py:362
  51.5 3.5 %collective-permute-start.8 = (f32[64,1024]{1,0:T(8,128)}, f32[64,1024]{1,0:T(8,128)S(1)}, u32[]{:S(2)}, u32[]{:S(2)}) collective-permute-start(f32[64,1024]{1,0:T(8,128)} %get-tuple-element.13), channel_id=1, source_target_pairs={{0,0},{1,1},{2,16},{3,17},{4,32},{5,33},{6,48},{7,49},{8,64},{9,65... | collective-permute-start | bytes 786440 | tf_op jit(solution)/shard_map/ppermute | solution.py:379
  55.0 4.7 %collective-permute-done.8 = f32[64,1024]{1,0:T(8,128)S(1)} collective-permute-done((f32[64,1024]{1,0:T(8,128)}, f32[64,1024]{1,0:T(8,128)S(1)}, u32[]{:S(2)}, u32[]{:S(2)}) %collective-permute-start.8) | collective-permute-done | bytes 262176 | tf_op jit(solution)/shard_map/ppermute | solution.py:379
  64.1 8.2 %collective-permute-start = (f32[128,1024]{1,0:T(8,128)}, f32[128,1024]{1,0:T(8,128)S(1)}, u32[]{:S(2)}, u32[]{:S(2)}) collective-permute-start(f32[128,1024]{1,0:T(8,128)} %get-tuple-element.26), channel_id=1, source_target_pairs={{0,16},{16,32},{32,48},{48,64},{64,80},{80,96},{96,112},{1,17},{17... | collective-permute-start | bytes 1572872 | tf_op jit(solution)/shard_map/ppermute | solution.py:399
  72.3 7.1 %collective-permute-start.11 = (f32[64,128]{1,0:T(8,128)S(1)}, f32[64,128]{1,0:T(8,128)S(1)}, u32[]{:S(2)}, u32[]{:S(2)}) collective-permute-start(f32[64,128]{1,0:T(8,128)S(1)} %copy-done.8), channel_id=1, source_target_pairs={{12,0},{13,1},{14,2},{15,3},{0,4},{1,5},{2,6},{3,7},{4,8},{5,9},{6... | collective-permute-start | bytes 98312 | tf_op jit(solution)/shard_map/ppermute | solution.py:296
  79.4 8.8 %collective-permute-start.10 = (f32[64,128]{1,0:T(8,128)S(1)}, f32[64,128]{1,0:T(8,128)S(1)}, u32[]{:S(2)}, u32[]{:S(2)}) collective-permute-start(f32[64,128]{1,0:T(8,128)S(1)} %copy-done.8), channel_id=1, source_target_pairs={{8,0},{9,1},{10,2},{11,3},{12,4},{13,5},{14,6},{15,7},{0,8},{1,9},... | collective-permute-start | bytes 98312 | tf_op jit(solution)/shard_map/ppermute | solution.py:296
  92.5 10.8 %collective-permute-done.12 = f32[64,128]{1,0:T(8,128)S(1)} collective-permute-done((f32[64,128]{1,0:T(8,128)S(1)}, f32[64,128]{1,0:T(8,128)S(1)}, u32[]{:S(2)}, u32[]{:S(2)}) %collective-permute-start.12) | collective-permute-done | bytes 32800 | tf_op jit(solution)/shard_map/ppermute | solution.py:300
  103.9 20.2 %collective-permute-start.13 = (f32[2,64,128]{2,1,0:T(8,128)}, f32[2,64,128]{2,1,0:T(8,128)}, u32[]{:S(2)}, u32[]{:S(2)}) collective-permute-start(f32[2,64,128]{2,1,0:T(8,128)} %get-tuple-element.40), channel_id=1, source_target_pairs={{0,16},{16,0},{32,48},{48,32},{64,80},{80,64},{96,112},{112,96},{1... | collective-permute-start | bytes 196616 | tf_op jit(solution)/shard_map/ppermute | solution.py:300
  128.6 5.7 %collective-permute-start.15 = (f32[2,2,64,128]{3,2,1,0:T(8,128)S(1)}, f32[2,2,64,128]{3,2,1,0:T(8,128)S(1)}, u32[]{:S(2)}, u32[]{:S(2)}) collective-permute-start(f32[2,2,64,128]{3,2,1,0:T(8,128)S(1)} %get-tuple-element.38), channel_id=1, source_target_pairs={{64,0},{80,16},{96,32},{112,48},{0,64},{16,80},{32,96},{48,112},{6... | collective-permute-start | bytes 393224 | tf_op jit(solution)/shard_map/ppermute | solution.py:296
  139.4 3.4 %collective-permute-done.16 = f32[2,2,64,128]{3,2,1,0:T(8,128)S(1)} collective-permute-done((f32[2,2,64,128]{3,2,1,0:T(8,128)S(1)}, f32[2,2,64,128]{3,2,1,0:T(8,128)S(1)}, u32[]{:S(2)}, u32[]{:S(2)}) %collective-permute-start.16) | collective-permute-done | bytes 131104 | tf_op jit(solution)/shard_map/ppermute | solution.py:296
  142.9 3.7 %collective-permute-start.17 = (f32[8,2,64,128]{3,2,1,0:T(8,128)S(1)}, f32[8,2,64,128]{3,2,1,0:T(8,128)S(1)}, u32[]{:S(2)}, u32[]{:S(2)}) collective-permute-start(f32[8,2,64,128]{3,2,1,0:T(8,128)S(1)} %bitcast.56), channel_id=1, source_target_pairs={{0,1},{1,0},{2,3},{3,2},{4,5},{5,4},{6,7},{7,6},{8,9},{9,8},{10,11... | collective-permute-start | bytes 1572872 | tf_op jit(solution)/shard_map/ppermute | solution.py:300
  146.7 3.6 %collective-permute-start.2 = (f32[2304,128]{1,0:T(8,128)S(1)}, f32[2304,128]{1,0:T(8,128)S(1)}, u32[]{:S(2)}, u32[]{:S(2)}) collective-permute-start(f32[2304,128]{1,0:T(8,128)S(1)} %pad_maximum_fusion), channel_id=1, source_target_pairs={{0,1},{1,2},{2,3},{3,4},{4,5},{5,6},{6,7},{7,8},{8,9},{9,10},{10,1... | collective-permute-start | bytes 3538952 | tf_op jit(solution)/shard_map/ppermute | solution.py:403
  152.6 29.7 %inverse.1.inv_ref = f32[256,256]{1,0:T(8,128)S(1)} custom-call(f32[8,2,64,128]{3,2,1,0:T(8,128)S(1)} %bitcast.57, f32[8,2,64,128]{3,2,1,0:T(8,128)S(1)} %collective-permute-done.17.other_ref, s32[256,1]{1,0:T(8,128)S(1)} %get-tuple-element.17.rslot_ref, s32[1,256]{1,0:T(1,128)S(1)} %get-tuple-element.15.cslot_ref, f32[1,256]{1,0:T(1,128)S(1)} %copy-done.5), custom_call_target="tpu_custom_call" | custom-call | flops 18447998976 | bytes 4194304 | tf_op jit(solution)/shard_map/inverse/pallas_call | solution.py:220
  182.4 5.0 %collective-permute-done.2.el_ref = f32[2304,128]{1,0:T(8,128)S(1)} collective-permute-done((f32[2304,128]{1,0:T(8,128)S(1)}, f32[2304,128]{1,0:T(8,128)S(1)}, u32[]{:S(2)}, u32[]{:S(2)}) %collective-permute-start.2) | collective-permute-done | bytes 1179680 | tf_op jit(solution)/shard_map/ppermute | solution.py:403
  187.4 3.5 %collective-permute-done.3.er_ref = f32[2304,128]{1,0:T(8,128)S(1)} collective-permute-done((f32[2304,128]{1,0:T(8,128)S(1)}, f32[2304,128]{1,0:T(8,128)S(1)}, u32[]{:S(2)}, u32[]{:S(2)}) %collective-permute-start.3) | collective-permute-done | bytes 1179680 | tf_op jit(solution)/shard_map/ppermute | solution.py:404
  190.9 12.1 %predict.1.pred_ref = f32[2048,1024]{1,0:T(8,128)S(1)} custom-call(s32[1]{0:T(128)} %bitcast.start, f32[2048,1024]{1,0:T(8,128)S(1)} %bitcast.54, f32[128,1024]{1,0:T(8,128)S(1)} %collective-permute-done.up_ref, f32[128,1024]{1,0:T(8,128)S(1)} %collective-permute-done.1.dn_ref, f32[2304,128]{1,0:T(8,128)S(1)} %collective-permute-done.2.el_ref, ...), custom_call_target="tpu_custom_call" | custom-call | flops 46137344 | bytes 16777216 | tf_op jit(solution)/shard_map/predict/pallas_call | solution.py:149
  203.1 3.3 %copy-done.1 = f32[2048,1024]{1,0:T(8,128)} copy-done((f32[2048,1024]{1,0:T(8,128)}, f32[2048,1024]{1,0:T(8,128)S(1)}, u32[]{:S(2)}) %copy-start.1) | copy-done | bytes 8388632
  210.1 14.8 %update.1 = f32[2048,1024]{1,0:T(8,128)} custom-call(f32[2048,1024]{1,0:T(8,128)} %copy-done.1, f32[512,1024]{1,0:T(8,128)S(1)} %copy-done.3, f32[8,2,64,1024]{3,2,1,0:T(8,128)S(1)} %bitcast.55, f32[256,256]{1,0:T(8,128)S(1)} %inverse.1.inv_ref, s32[256,1]{1,0:T(8,128)S(1)} %get-tuple-element.18.cslot_ref, s32[1,256]{1,0:T(1,128)S(1)} %get-tuple-element.16.rslot_ref), custom_call_target="tpu_custom_call" | custom-call | flops 3221225472 | bytes 16777216 | tf_op jit(solution)/shard_map/update/pallas_call | solution.py:272
  (109 shorter events, 42.5 us)
Async XLA Ops:
  6.5 199.8 %all-gather.4.cloned.1.call-start = ((), (), s32[]{:S(2)}) async-start(), calls=%async_computation | async-start | bytes 2359296 | tf_op jit(solution)/shard_map/all_gather | solution.py:372
  28.6 7.3 %collective-permute-start.4 = (f32[32,1024]{1,0:T(8,128)S(1)}, f32[32,1024]{1,0:T(8,128)S(1)}, u32[]{:S(2)}, u32[]{:S(2)}) collective-permute-start(f32[32,1024]{1,0:T(8,128)S(1)} %get-tuple-element.11), channel_id=1, source_target_pairs={{0,16},{16,32},{32,48},{48,64},{64,80},{80,96},{96,112},{1,17},{17... | collective-permute-start | bytes 393224 | tf_op jit(solution)/shard_map/ppermute | solution.py:357
  31.8 7.4 %collective-permute-start.5 = (f32[32,1024]{1,0:T(8,128)S(1)}, f32[32,1024]{1,0:T(8,128)S(1)}, u32[]{:S(2)}, u32[]{:S(2)}) collective-permute-start(f32[32,1024]{1,0:T(8,128)S(1)} %get-tuple-element.12), channel_id=1, source_target_pairs={{16,0},{32,16},{48,32},{64,48},{80,64},{96,80},{112,96},{17,1},{33... | collective-permute-start | bytes 393224 | tf_op jit(solution)/shard_map/ppermute | solution.py:358
  39.4 8.7 %collective-permute-start.7 = (f32[64,128]{1,0:T(8,128)S(1)}, f32[64,128]{1,0:T(8,128)S(1)}, u32[]{:S(2)}, u32[]{:S(2)}) collective-permute-start(f32[64,128]{1,0:T(8,128)S(1)} %get-tuple-element.31), channel_id=1, source_target_pairs={{1,0},{2,1},{3,2},{4,3},{5,4},{6,5},{7,6},{8,7},{9,8},{10,9},{11,1... | collective-permute-start | bytes 98312 | tf_op jit(solution)/shard_map/ppermute | solution.py:363
  42.6 5.7 %collective-permute-start.6 = (f32[64,128]{1,0:T(8,128)S(1)}, f32[64,128]{1,0:T(8,128)S(1)}, u32[]{:S(2)}, u32[]{:S(2)}) collective-permute-start(f32[64,128]{1,0:T(8,128)S(1)} %get-tuple-element.32), channel_id=1, source_target_pairs={{0,1},{1,2},{2,3},{3,4},{4,5},{5,6},{6,7},{7,8},{8,9},{9,10},{10,1... | collective-permute-start | bytes 98312 | tf_op jit(solution)/shard_map/ppermute | solution.py:362
  51.5 154.9 %all-gather.6.cloned.1.call-start = ((), (), s32[]{:S(2)}) async-start(), calls=%async_computation.1 | async-start | bytes 4456448 | tf_op jit(solution)/shard_map/all_gather | solution.py:380
  51.5 8.2 %collective-permute-start.8 = (f32[64,1024]{1,0:T(8,128)}, f32[64,1024]{1,0:T(8,128)S(1)}, u32[]{:S(2)}, u32[]{:S(2)}) collective-permute-start(f32[64,1024]{1,0:T(8,128)} %get-tuple-element.13), channel_id=1, source_target_pairs={{0,0},{1,1},{2,16},{3,17},{4,32},{5,33},{6,48},{7,49},{8,64},{9,65... | collective-permute-start | bytes 786440 | tf_op jit(solution)/shard_map/ppermute | solution.py:379
  62.8 83.8 %collective-permute-start.1 = (f32[128,1024]{1,0:T(8,128)}, f32[128,1024]{1,0:T(8,128)S(1)}, u32[]{:S(2)}, u32[]{:S(2)}) collective-permute-start(f32[128,1024]{1,0:T(8,128)} %get-tuple-element.25), channel_id=1, source_target_pairs={{16,0},{32,16},{48,32},{64,48},{80,64},{96,80},{112,96},{17,1},{33... | collective-permute-start | bytes 1572872 | tf_op jit(solution)/shard_map/ppermute | solution.py:400
  64.1 82.5 %collective-permute-start = (f32[128,1024]{1,0:T(8,128)}, f32[128,1024]{1,0:T(8,128)S(1)}, u32[]{:S(2)}, u32[]{:S(2)}) collective-permute-start(f32[128,1024]{1,0:T(8,128)} %get-tuple-element.26), channel_id=1, source_target_pairs={{0,16},{16,32},{32,48},{48,64},{64,80},{80,96},{96,112},{1,17},{17... | collective-permute-start | bytes 1572872 | tf_op jit(solution)/shard_map/ppermute | solution.py:399
  72.3 52.0 %copy-start.11 = (s32[1,256]{1,0:T(1,128)S(1)}, s32[1,256]{1,0:T(1,128)}, u32[]{:S(2)}) copy-start(s32[1,256]{1,0:T(1,128)} %param.10) | copy-start | bytes 3076
  72.3 19.3 %collective-permute-start.11 = (f32[64,128]{1,0:T(8,128)S(1)}, f32[64,128]{1,0:T(8,128)S(1)}, u32[]{:S(2)}, u32[]{:S(2)}) collective-permute-start(f32[64,128]{1,0:T(8,128)S(1)} %copy-done.8), channel_id=1, source_target_pairs={{12,0},{13,1},{14,2},{15,3},{0,4},{1,5},{2,6},{3,7},{4,8},{5,9},{6... | collective-permute-start | bytes 98312 | tf_op jit(solution)/shard_map/ppermute | solution.py:296
  79.4 12.1 %collective-permute-start.10 = (f32[64,128]{1,0:T(8,128)S(1)}, f32[64,128]{1,0:T(8,128)S(1)}, u32[]{:S(2)}, u32[]{:S(2)}) collective-permute-start(f32[64,128]{1,0:T(8,128)S(1)} %copy-done.8), channel_id=1, source_target_pairs={{8,0},{9,1},{10,2},{11,3},{12,4},{13,5},{14,6},{15,7},{0,8},{1,9},... | collective-permute-start | bytes 98312 | tf_op jit(solution)/shard_map/ppermute | solution.py:296
  88.3 3.3 %collective-permute-start.9 = (f32[64,128]{1,0:T(8,128)S(1)}, f32[64,128]{1,0:T(8,128)S(1)}, u32[]{:S(2)}, u32[]{:S(2)}) collective-permute-start(f32[64,128]{1,0:T(8,128)S(1)} %copy-done.8), channel_id=1, source_target_pairs={{4,0},{5,1},{6,2},{7,3},{8,4},{9,5},{10,6},{11,7},{12,8},{13,9},{1... | collective-permute-start | bytes 98312 | tf_op jit(solution)/shard_map/ppermute | solution.py:296
  91.6 11.7 %collective-permute-start.12 = (f32[64,128]{1,0:T(8,128)S(1)}, f32[64,128]{1,0:T(8,128)S(1)}, u32[]{:S(2)}, u32[]{:S(2)}) collective-permute-start(f32[64,128]{1,0:T(8,128)S(1)} %add_add_fusion), channel_id=1, source_target_pairs={{0,2},{1,3},{2,0},{3,1},{4,6},{5,7},{6,4},{7,5},{8,10},{9,11},{10,... | collective-permute-start | bytes 98312 | tf_op jit(solution)/shard_map/ppermute | solution.py:300
  103.9 23.8 %collective-permute-start.13 = (f32[2,64,128]{2,1,0:T(8,128)}, f32[2,64,128]{2,1,0:T(8,128)}, u32[]{:S(2)}, u32[]{:S(2)}) collective-permute-start(f32[2,64,128]{2,1,0:T(8,128)} %get-tuple-element.40), channel_id=1, source_target_pairs={{0,16},{16,0},{32,48},{48,32},{64,80},{80,64},{96,112},{112,96},{1... | collective-permute-start | bytes 196616 | tf_op jit(solution)/shard_map/ppermute | solution.py:300
  128.6 9.2 %collective-permute-start.15 = (f32[2,2,64,128]{3,2,1,0:T(8,128)S(1)}, f32[2,2,64,128]{3,2,1,0:T(8,128)S(1)}, u32[]{:S(2)}, u32[]{:S(2)}) collective-permute-start(f32[2,2,64,128]{3,2,1,0:T(8,128)S(1)} %get-tuple-element.38), channel_id=1, source_target_pairs={{64,0},{80,16},{96,32},{112,48},{0,64},{16,80},{32,96},{48,112},{6... | collective-permute-start | bytes 393224 | tf_op jit(solution)/shard_map/ppermute | solution.py:296
  134.3 5.1 %collective-permute-start.14 = (f32[2,2,64,128]{3,2,1,0:T(8,128)S(1)}, f32[2,2,64,128]{3,2,1,0:T(8,128)S(1)}, u32[]{:S(2)}, u32[]{:S(2)}) collective-permute-start(f32[2,2,64,128]{3,2,1,0:T(8,128)S(1)} %get-tuple-element.38), channel_id=1, source_target_pairs={{32,0},{48,16},{64,32},{80,48},{96,64},{112,80},{0,96},{16,112},{3... | collective-permute-start | bytes 393224 | tf_op jit(solution)/shard_map/ppermute | solution.py:296
  137.4 5.4 %collective-permute-start.16 = (f32[2,2,64,128]{3,2,1,0:T(8,128)S(1)}, f32[2,2,64,128]{3,2,1,0:T(8,128)S(1)}, u32[]{:S(2)}, u32[]{:S(2)}) collective-permute-start(f32[2,2,64,128]{3,2,1,0:T(8,128)S(1)} %get-tuple-element.38), channel_id=1, source_target_pairs={{96,0},{112,16},{0,32},{16,48},{32,64},{48,80},{64,96},{80,112},{9... | collective-permute-start | bytes 393224 | tf_op jit(solution)/shard_map/ppermute | solution.py:296
  142.9 9.7 %collective-permute-start.17 = (f32[8,2,64,128]{3,2,1,0:T(8,128)S(1)}, f32[8,2,64,128]{3,2,1,0:T(8,128)S(1)}, u32[]{:S(2)}, u32[]{:S(2)}) collective-permute-start(f32[8,2,64,128]{3,2,1,0:T(8,128)S(1)} %bitcast.56), channel_id=1, source_target_pairs={{0,1},{1,0},{2,3},{3,2},{4,5},{5,4},{6,7},{7,6},{8,9},{9,8},{10,11... | collective-permute-start | bytes 1572872 | tf_op jit(solution)/shard_map/ppermute | solution.py:300
  146.7 40.6 %collective-permute-start.2 = (f32[2304,128]{1,0:T(8,128)S(1)}, f32[2304,128]{1,0:T(8,128)S(1)}, u32[]{:S(2)}, u32[]{:S(2)}) collective-permute-start(f32[2304,128]{1,0:T(8,128)S(1)} %pad_maximum_fusion), channel_id=1, source_target_pairs={{0,1},{1,2},{2,3},{3,4},{4,5},{5,6},{6,7},{7,8},{8,9},{9,10},{10,1... | collective-permute-start | bytes 3538952 | tf_op jit(solution)/shard_map/ppermute | solution.py:403
  150.5 40.5 %collective-permute-start.3 = (f32[2304,128]{1,0:T(8,128)S(1)}, f32[2304,128]{1,0:T(8,128)S(1)}, u32[]{:S(2)}, u32[]{:S(2)}) collective-permute-start(f32[2304,128]{1,0:T(8,128)S(1)} %pad_maximum_fusion.1), channel_id=1, source_target_pairs={{1,0},{2,1},{3,2},{4,3},{5,4},{6,5},{7,6},{8,7},{9,8},{10,9},{11,1... | collective-permute-start | bytes 3538952 | tf_op jit(solution)/shard_map/ppermute | solution.py:404
  152.6 38.3 %slice-start = ((s8[8388608]{0:T(1024)(128)(4,1)}), s8[4194304]{0:T(1024)(128)(4,1)S(1)}, s32[]{:S(2)}) async-start(s8[8388608]{0:T(1024)(128)(4,1)} %bitcast.53), calls=%async_computation.2 | async-start | bytes 8388608
  152.6 38.3 %slice-start.1 = ((s8[8388608]{0:T(1024)(128)(4,1)}), s8[4194304]{0:T(1024)(128)(4,1)S(1)}, s32[]{:S(2)}) async-start(s8[8388608]{0:T(1024)(128)(4,1)} %bitcast.53), calls=%async_computation.3 | async-start | bytes 8388608
  152.6 38.3 %copy-start.4 = (f32[5,1024]{1,0:T(8,128)S(1)}, f32[5,1024]{1,0:T(8,128)}, u32[]{:S(2)}) copy-start(f32[5,1024]{1,0:T(8,128)} %constant_dynamic-slice_fusion.cc_ref.coef_ref) | copy-start | bytes 61444
  (10 other events, 46.1 us)
Sparse Core Ops, SparseCore 0:
  51.6 76.4 all-gather.3
  130.5 63.0 all-gather.5

commit v2 on v1

v2 whole, which is shorter than its diff:
```python
import functools

import jax
import jax.numpy as jnp
from jax import lax
from jax.experimental import pallas as pl
from jax.experimental.pallas import tpu as pltpu
from jax.sharding import PartitionSpec as P

NGY = 128
M = 256
WMAX = 32
ROWS = 8
COLS = 16
HALF = 2 * WMAX
SLOTS = ROWS * HALF
F32 = jnp.float32
BF16 = jnp.bfloat16
HI = lax.Precision.HIGHEST


def cost(flops, size):
    return pl.CostEstimate(flops=flops, bytes_accessed=size, transcendentals=0)


def vmem(count):
    return [pl.BlockSpec(memory_space=pltpu.VMEM)] * count


def rows_kernel(
    place, wells, center, links, process, block,
    z_ref, dn_ref, aux_ref, target_ref, local_ref,
    p_ref, own, side, noise, cell, count, sems,
):
    rows, cols = p_ref.shape
    r, c = place[0], place[1]
    row_start, col_start = pl.multiple_of(r * rows, rows), c * cols
    part = pl.ds(row_start, rows)
    copies = [
        pltpu.make_async_copy(block, p_ref, sems.at[0]),
        pltpu.make_async_copy(center.at[part], own, sems.at[1]),
        pltpu.make_async_copy(links.at[:, part], side, sems.at[2]),
        pltpu.make_async_copy(process.at[part], noise, sems.at[3]),
    ]
    for copy in copies:
        copy.start()

    for i in range(SLOTS // WMAX):
        count[i] = 0

    def none(i, carry):
        for k in range(16):
            cell[i * 16 + k] = -1
        return carry

    lax.fori_loop(0, SLOTS // 16, none, 0)

    def put(m, carry):
        w = wells[0, m]
        home = w // cols
        n = count[home]
        cell[home * WMAX + n] = w
        count[home] = n + 1
        return carry

    lax.fori_loop(0, M, put, 0, unroll=8)
    for copy in copies:
        copy.wait()

    lane = lax.broadcasted_iota(jnp.int32, (1, NGY), 1)
    top = ROWS - 1

    def one(s, carry):
        w = cell[r * HALF + s]
        good = w >= 0
        i = jnp.where(good, w - row_start, 0)
        first, final = i < NGY, i >= rows - NGY
        gy = i % NGY
        gate = jnp.where(good, 1.0, 0.0)
        k0, k1, k2 = own[i] * gate, side[0, i] * gate, side[1, i] * gate
        k3 = jnp.where(gy == 0, 0.0, side[2, i] * gate)
        k4 = jnp.where(gy == NGY - 1, 0.0, side[3, i] * gate)
        total = k0 * p_ref[pl.ds(i, 1), :]
        above = p_ref[pl.ds(jnp.maximum(i - NGY, 0), 1), :]
        below = p_ref[pl.ds(jnp.minimum(i + NGY, rows - 1), 1), :]
        total = total + jnp.where(first, 0.0, k1) * above + jnp.where(final, 0.0, k2) * below
        before = p_ref[pl.ds(jnp.maximum(i - 1, 0), 1), :]
        after = p_ref[pl.ds(jnp.minimum(i + 1, rows - 1), 1), :]
        z_ref[pl.ds(s, 1), :] = total + k3 * before + k4 * after
        row = jnp.where(lane == 0, jnp.where(first & (r > 0), k1, 0.0), 0.0)
        row = jnp.where(lane == 1, jnp.where(final & (r < top), k2, 0.0), row)
        row = jnp.where(lane == 2, noise[i] * gate, row)
        col = jnp.where(good, w - col_start, -1)
        row = jnp.where(lane == 3, jnp.full((1, NGY), col, jnp.int32).astype(F32), row)
        aux_ref[pl.ds(s, 1), :] = row
        return carry

    lax.fori_loop(0, HALF, one, 0, unroll=4)

    def two(s, carry):
        dn = cell[jnp.maximum(r * HALF - WMAX + s, 0)] + NGY - row_start
        dn_ref[pl.ds(s, 1), :] = p_ref[pl.ds(jnp.clip(dn, 0, rows - 1), 1), :]
        local_ref[s] = jnp.clip(cell[r * HALF + s] - row_start, 0, NGY - 1)
        return carry

    lax.fori_loop(0, WMAX, two, 0, unroll=4)

    base = (c // 4) * WMAX

    def three(t, row):
        return jnp.where(lane == base + t, cell[c * WMAX + t] - col_start, row)

    target_ref[...] = lax.fori_loop(0, WMAX, three, jnp.full((1, NGY), -1, jnp.int32), unroll=4)


def well_rows(place, wells, center, links, process, block):
    rows, cols = block.shape
    smem = pl.BlockSpec(memory_space=pltpu.SMEM)
    hbm = pl.BlockSpec(memory_space=pltpu.HBM)
    return pl.pallas_call(
        rows_kernel,
        out_shape=(
            jax.ShapeDtypeStruct((HALF, cols), F32),
            jax.ShapeDtypeStruct((WMAX, cols), F32),
            jax.ShapeDtypeStruct((HALF, NGY), F32),
            jax.ShapeDtypeStruct((1, NGY), jnp.int32),
            jax.ShapeDtypeStruct((WMAX,), jnp.int32),
        ),
        in_specs=[smem, smem, hbm, hbm, hbm, hbm],
        out_specs=tuple(vmem(4)) + (smem,),
        scratch_shapes=[
            pltpu.VMEM((rows, cols), F32),
            pltpu.SMEM((rows,), F32),
            pltpu.SMEM((4, rows), F32),
            pltpu.SMEM((rows,), F32),
            pltpu.SMEM((SLOTS,), jnp.int32),
            pltpu.SMEM((SLOTS // WMAX,), jnp.int32),
            pltpu.SemaphoreType.DMA((4,)),
        ],
        compiler_params=pltpu.CompilerParams(vmem_limit_bytes=24 << 20),
        cost_estimate=cost(10 * HALF * cols, block.size * 4),
        name="well_rows",
    )(place, wells, center, links, process, block)


def merge_kernel(local, z_ref, aux_ref, up_ref, dn_ref, o_ref, left_ref, right_ref):
    cols = z_ref.shape[1]
    scale = aux_ref[...]

    def one(s, carry):
        o_ref[pl.ds(s, 1), :] = up_ref[pl.ds(local[s], 1), :]
        return carry

    lax.fori_loop(0, WMAX, one, 0, unroll=4)
    o_ref[0:WMAX] = z_ref[0:WMAX] + scale[0:WMAX, 0:1] * o_ref[0:WMAX]
    o_ref[WMAX:] = z_ref[WMAX:] + scale[WMAX:, 1:2] * dn_ref[...]
    left_ref[...] = o_ref[:, 0:NGY]
    right_ref[...] = o_ref[:, cols - NGY :]


def merge(local, z, aux, up, dn):
    cols = z.shape[1]
    return pl.pallas_call(
        merge_kernel,
        out_shape=(
            jax.ShapeDtypeStruct((HALF, cols), F32),
            jax.ShapeDtypeStruct((HALF, NGY), F32),
            jax.ShapeDtypeStruct((HALF, NGY), F32),
        ),
        in_specs=[pl.BlockSpec(memory_space=pltpu.SMEM)] + vmem(4),
        out_specs=tuple(vmem(3)),
        cost_estimate=cost(4 * HALF * cols, 4 * HALF * cols * 4),
        name="merge",
    )(local, z, aux, up, dn)


def across_lanes(parts, coef, lo, hi):
    out = []
    for t in range(lo, hi):
        left, mid, right = parts[t], parts[t + 1], parts[t + 2]
        c = coef[:, t * NGY : (t + 1) * NGY]
        total = c[0:1] * mid
        if left is not None:
            total = total + c[1:2] * left
        if right is not None:
            total = total + c[2:3] * right
        total = total + c[3:4] * pltpu.roll(mid, 1, 1) + c[4:5] * pltpu.roll(mid, NGY - 1, 1)
        out.append(total)
    return out


def cols_kernel(z_ref, zl_ref, zr_ref, coef_ref, aux_ref, target_ref, x_ref, g_ref):
    cols = z_ref.shape[1]
    tiles = cols // NGY
    parts = [zl_ref[...]] + [z_ref[:, t * NGY : (t + 1) * NGY] for t in range(tiles)] + [zr_ref[...]]
    out = across_lanes(parts, coef_ref[...], 0, tiles)
    x = jnp.concatenate(out, axis=1)
    lane = lax.broadcasted_iota(jnp.int32, x.shape, 1)
    x = x + jnp.where(lane.astype(F32) == aux_ref[:, 3:4], aux_ref[:, 2:3], 0.0)
    x_ref[...] = x
    pick = lax.broadcasted_iota(jnp.int32, (cols, NGY), 0) == target_ref[...]
    g_ref[...] = jnp.dot(x, pick.astype(F32), precision=HI, preferred_element_type=F32)


def well_cols(z, zl, zr, coef, aux, target):
    cols = z.shape[1]
    return pl.pallas_call(
        cols_kernel,
        out_shape=(
            jax.ShapeDtypeStruct((HALF, cols), F32),
            jax.ShapeDtypeStruct((HALF, NGY), F32),
        ),
        in_specs=vmem(6),
        out_specs=tuple(vmem(2)),
        cost_estimate=cost(12 * HALF * cols * NGY, 4 * HALF * cols * 4),
        name="well_cols",
    )(z, zl, zr, coef, aux, target)


def left_tile(rc, mid, above, below):
    total = rc[0] * mid + rc[1] * above + rc[2] * below
    return total + rc[3] * pltpu.roll(mid, 1, 0) + rc[4] * pltpu.roll(mid, NGY - 1, 0)


def predict_kernel(start, p_ref, rc_ref, cc_ref, proc_ref, o_ref):
    g = pl.program_id(0)
    last = pl.num_programs(0) - 1
    cols = p_ref.shape[1]
    tiles = cols // NGY
    here = pl.ds(pl.multiple_of(g * NGY, NGY), NGY)
    before = pl.ds(pl.multiple_of(jnp.maximum(g - 1, 0) * NGY, NGY), NGY)
    after = pl.ds(pl.multiple_of(jnp.minimum(g + 1, last) * NGY, NGY), NGY)
    wide = (NGY, NGY)
    rc = [jnp.broadcast_to(rc_ref[:, k : k + 1], wide) for k in range(5)]
    rc[1] = jnp.where(g == 0, 0.0, rc[1])
    rc[2] = jnp.where(g == last, 0.0, rc[2])
    parts = [None]
    for t in range(tiles + 1):
        if t < tiles:
            lanes = slice(t * NGY, (t + 1) * NGY)
            parts.append(left_tile(rc, p_ref[here, lanes], p_ref[before, lanes], p_ref[after, lanes]))
        else:
            parts.append(None)
        if t >= 1:
            o_ref[:, (t - 1) * NGY : t * NGY] = across_lanes(parts, cc_ref[...], t - 1, t)[0]
    hit = start[0] + g
    eye = lax.broadcasted_iota(jnp.int32, wide, 0) == lax.broadcasted_iota(jnp.int32, wide, 1)
    for t in range(tiles):

        @pl.when(hit == t)
        def _():
            lanes = slice(t * NGY, (t + 1) * NGY)
            o_ref[:, lanes] = o_ref[:, lanes] + jnp.where(eye, proc_ref[:, lanes], 0.0)


def predict(start, block, row_coef, col_coef, proc):
    rows, cols = block.shape
    steps = rows // NGY
    return pl.pallas_call(
        predict_kernel,
        out_shape=jax.ShapeDtypeStruct((rows, cols), F32),
        grid_spec=pltpu.PrefetchScalarGridSpec(
            num_scalar_prefetch=1,
            grid=(steps,),
            in_specs=vmem(1) + [pl.BlockSpec((NGY, 8), lambda g, s: (g, 0))] + vmem(2),
            out_specs=pl.BlockSpec((NGY, cols), lambda g, s: (g, 0)),
        ),
        compiler_params=pltpu.CompilerParams(vmem_limit_bytes=24 << 20),
        cost_estimate=cost(22 * rows * cols, 8 * rows * cols),
        name="predict",
    )(start, block, row_coef, col_coef, proc)


BLK = 128
STEP = 4


def inverse_two(a, b, c):
    q = 1.0 / (a * c - b * b)
    return c * q, -b * q, a * q


def inverse_four(e):
    a, b, c = inverse_two(e[0][0], e[0][1], e[1][1])
    two = range(2)
    side = [[e[i][2 + k] for k in two] for i in two]
    w = [
        [a * side[0][k] + b * side[1][k] for k in two],
        [b * side[0][k] + c * side[1][k] for k in two],
    ]
    s = [
        [e[2 + i][2 + k] - (side[0][i] * w[0][k] + side[1][i] * w[1][k]) for k in two] for i in two
    ]
    p, q, t = inverse_two(s[0][0], s[0][1], s[1][1])
    v = [[w[i][0] * p + w[i][1] * q, w[i][0] * q + w[i][1] * t] for i in two]
    t00 = a + v[0][0] * w[0][0] + v[0][1] * w[0][1]
    t01 = b + v[0][0] * w[1][0] + v[0][1] * w[1][1]
    t11 = c + v[1][0] * w[1][0] + v[1][1] * w[1][1]
    return [
        [t00, t01, -v[0][0], -v[0][1]],
        [t01, t11, -v[1][0], -v[1][1]],
        [-v[0][0], -v[1][0], p, q],
        [-v[0][1], -v[1][1], q, t],
    ]


def small_inverse(d):
    size = d.shape[0]
    wide = (8, size)
    chunks = [d[8 * q : 8 * q + 8] for q in range(size // 8)]
    sub = lax.broadcasted_iota(jnp.int32, wide, 0)
    lane = lax.broadcasted_iota(jnp.int32, wide, 1)
    four = range(STEP)
    for j in range(0, size, STEP):
        home, o = divmod(j, 8)
        row = [jnp.broadcast_to(chunks[home][o + a : o + a + 1], wide) for a in four]
        e = [[None] * STEP for _ in four]
        for a in four:
            for b in range(a, STEP):
                e[a][b] = e[b][a] = jnp.broadcast_to(row[a][:, j + b : j + b + 1], wide)
        piv = inverse_four(e)
        inside = (lane >= j) & (lane < j + STEP)
        row = [jnp.where(lane == j + a, 1.0, jnp.where(inside, 0.0, row[a])) for a in four]
        new = [
            (piv[a][0] * row[0] + piv[a][1] * row[1]) + (piv[a][2] * row[2] + piv[a][3] * row[3])
            for a in four
        ]
        out = []
        for q, chunk in enumerate(chunks):
            col = [jnp.broadcast_to(chunk[:, j + a : j + a + 1], wide) for a in four]
            less = (col[0] * new[0] + col[1] * new[1]) + (col[2] * new[2] + col[3] * new[3])
            rest = jnp.where(inside, 0.0, chunk) - less
            if q == home:
                for a in four:
                    rest = jnp.where(sub == o + a, new[a], rest)
            out.append(rest)
        chunks = out
    return jnp.concatenate(chunks, axis=0)


def dot(a, b):
    return jnp.dot(a, b, precision=HI, preferred_element_type=F32)


def inverse_kernel(own_ref, other_ref, rslot_ref, cslot_ref, noise_ref, o_ref, s_ref):
    rows_in = ROWS * HALF
    pick_rows = (lax.broadcasted_iota(jnp.int32, (M, rows_in), 1) == rslot_ref[...]).astype(F32)
    total = jnp.zeros((M, M), F32)
    for k, ref in enumerate((own_ref, other_ref)):
        for h in range(2):
            piece = ref[:, h].reshape(rows_in, NGY)
            some = dot(pick_rows, piece)
            base = (2 * k + h) * NGY
            pick = lax.broadcasted_iota(jnp.int32, (NGY, M), 0) + base == cslot_ref[...]
            total = total + dot(some, pick.astype(F32))
    i0 = lax.broadcasted_iota(jnp.int32, (M, M), 0)
    i1 = lax.broadcasted_iota(jnp.int32, (M, M), 1)
    s_ref[...] = total + jnp.where(i0 == i1, noise_ref[...], 0.0)
    sub = lax.broadcasted_iota(jnp.int32, (M, BLK), 0)
    for b in range(M // BLK):
        lo = b * BLK
        inv = small_inverse(s_ref[lo : lo + BLK, lo : lo + BLK])
        panel = s_ref[lo : lo + BLK, :]
        col = s_ref[:, lo : lo + BLK]
        here = (i1[0:BLK] >= lo) & (i1[0:BLK] < lo + BLK)
        scaled = dot(inv, panel)
        inside = (sub >= lo) & (sub < lo + BLK)
        upd = dot(jnp.where(inside, 0.0, col), scaled)
        down = dot(col, inv)
        s_ref[...] = s_ref[...] - upd
        s_ref[:, lo : lo + BLK] = -down
        s_ref[lo : lo + BLK, :] = scaled
        s_ref[lo : lo + BLK, lo : lo + BLK] = inv
    o_ref[...] = s_ref[...]


def inverse(own, other, rslot, cslot, noise):
    return pl.pallas_call(
        inverse_kernel,
        out_shape=jax.ShapeDtypeStruct((M, M), F32),
        in_specs=vmem(5),
        out_specs=vmem(1)[0],
        scratch_shapes=[pltpu.VMEM((M, M), F32)],
        compiler_params=pltpu.CompilerParams(vmem_limit_bytes=24 << 20),
        cost_estimate=cost(2 * 1153000000 * 8, 4 << 20),
        name="inverse",
    )(own, other, rslot, cslot, noise)


def split(x):
    high = x.astype(BF16)
    return high, (x - high.astype(F32)).astype(BF16)


def bdot(a, b, dims=((1,), (0,))):
    return lax.dot_general(a, b, (dims, ((), ())), preferred_element_type=F32)


def three(x):
    high, low = split(x)
    return high, low, (x - high.astype(F32) - low.astype(F32)).astype(BF16)


def joined(refs):
    return jnp.concatenate([p[...].reshape(-1, p.shape[-1]) for p in refs], axis=0)


def across_kernel(slot_ref, *refs):
    pick = (lax.broadcasted_iota(jnp.int32, (M, SLOTS), 1) == slot_ref[...]).astype(BF16)
    high, mid, low = three(joined(refs[:-1]))
    refs[-1][...] = bdot(pick, high) + (bdot(pick, mid) + bdot(pick, low))


def across(slot, parts):
    cols = parts[0].shape[-1]
    return pl.pallas_call(
        across_kernel,
        out_shape=jax.ShapeDtypeStruct((M, cols), F32),
        in_specs=vmem(1 + len(parts)),
        out_specs=vmem(1)[0],
        compiler_params=pltpu.CompilerParams(vmem_limit_bytes=24 << 20),
        cost_estimate=cost(6 * M * SLOTS * cols, 3 * SLOTS * cols * 4),
        name="across",
    )(slot, *parts)


def strip_kernel(slot_ref, *refs):
    pick = (lax.broadcasted_iota(jnp.int32, (SLOTS, M), 0) == slot_ref[...]).astype(BF16)
    high, low = split(joined(refs[:-2]))
    refs[-2][...] = bdot(high, pick, ((0,), (0,))).astype(BF16)
    refs[-1][...] = bdot(low, pick, ((0,), (0,))).astype(BF16)


def strip(slot, parts):
    size = parts[0].shape[-1]
    return pl.pallas_call(
        strip_kernel,
        out_shape=(jax.ShapeDtypeStruct((size, M), BF16), jax.ShapeDtypeStruct((size, M), BF16)),
        in_specs=vmem(1 + len(parts)),
        out_specs=tuple(vmem(2)),
        compiler_params=pltpu.CompilerParams(vmem_limit_bytes=24 << 20),
        cost_estimate=cost(4 * M * SLOTS * size, 2 * SLOTS * size * 4),
        name="strip",
    )(slot, *parts)


def update_kernel(
    core, pred_ref, inv_ref, xc_ref, rc_ref, cc_ref, up_ref, dn_ref, el_ref, er_ref,
    oh_ref, ol_ref, ph_ref, pl_ref, o_ref, uh, ul,
):
    h, j = pl.program_id(0), pl.program_id(1)
    steps = pl.num_programs(1)
    g = (h ^ core[0]) * steps + j
    last = 2 * steps - 1

    @pl.when((h == 0) & (j == 0))
    def _():
        high, low = split(dot(inv_ref[...], xc_ref[...]))
        uh[...] = high
        ul[...] = low

    size, cols = o_ref.shape
    rows = pl.ds(pl.multiple_of(j * size, size), size)
    for half, (hi_ref, lo_ref) in enumerate(((oh_ref, ol_ref), (ph_ref, pl_ref))):

        @pl.when(h == half)
        def _():
            a, b = hi_ref[rows, :], lo_ref[rows, :]
            o_ref[...] = pred_ref[...] - (bdot(a, uh[...]) + (bdot(a, ul[...]) + bdot(b, uh[...])))

    rc = [jnp.broadcast_to(rc_ref[:, k : k + 1], (NGY, NGY)) for k in range(5)]
    above = pl.ds(pl.multiple_of(g * NGY, NGY), NGY)
    here = pl.ds(pl.multiple_of(g * NGY + NGY, NGY), NGY)
    below = pl.ds(pl.multiple_of(g * NGY + 2 * NGY, NGY), NGY)
    for ref, lo, k in ((el_ref, 0, 1), (er_ref, cols - NGY, 2)):
        rim = left_tile(rc, ref[here, :], ref[above, :], ref[below, :])
        lanes = slice(lo, lo + NGY)
        o_ref[:, lanes] = o_ref[:, lanes] + cc_ref[k : k + 1, lanes] * rim
    for at, ref, k in ((0, up_ref, 1), (last, dn_ref, 2)):

        @pl.when(g == at)
        def _():
            tiles = cols // NGY
            parts = [None] + [rc[k] * ref[:, t * NGY : (t + 1) * NGY] for t in range(tiles)] + [None]
            rim = across_lanes(parts, cc_ref[...], 0, tiles)
            o_ref[...] = o_ref[...] + jnp.concatenate(rim, axis=1)


def update(core, pred, inv, xc, row_coef, col_coef, rims, own, other):
    rows, cols = pred.shape
    half = rows // 2
    steps = half // NGY
    tile = pl.BlockSpec((NGY, cols), lambda h, j, k: ((h ^ k[0]) * steps + j, 0))
    few = pl.BlockSpec((NGY, 8), lambda h, j, k: ((h ^ k[0]) * steps + j, 0))
    return pl.pallas_call(
        update_kernel,
        out_shape=jax.ShapeDtypeStruct((rows, cols), F32),
        grid_spec=pltpu.PrefetchScalarGridSpec(
            num_scalar_prefetch=1,
            grid=(2, steps),
            in_specs=[tile] + vmem(2) + [few] + vmem(9),
            out_specs=tile,
            scratch_shapes=[pltpu.VMEM((M, cols), BF16), pltpu.VMEM((M, cols), BF16)],
        ),
        compiler_params=pltpu.CompilerParams(vmem_limit_bytes=32 << 20),
        cost_estimate=cost(6 * rows * cols * M, 8 * rows * cols),
        name="update",
    )(core, pred, inv, xc, row_coef, col_coef, *rims, *own, *other)


def shift(x, axis, count, back):
    return lax.ppermute(x, axis, [((i + back) % count, i) for i in range(count)])


def flip(x, axis, count, bit):
    return lax.ppermute(x, axis, [(i, i ^ bit) for i in range(count)])


def ring(x, axis, count, near, step):
    pair = jnp.stack([x, flip(x, axis, count, near)])
    more = shift(pair, axis, count, step)
    less = shift(pair, axis, count, count - step)
    far = shift(more[0], axis, count, step), shift(less[1], axis, count, count - step)
    return pair, more, far, less


def after(x, *others):
    return lax.optimization_barrier((x,) + others)[0]


def shards(covariance, center, links, process, wells, noise):
    r = lax.axis_index("row")
    c = lax.axis_index("col")
    rows, cols = covariance.shape
    cells = center.shape[0]
    row_start, col_start = r * rows, c * cols
    block = covariance

    up = shift(block[rows - NGY :], "row", ROWS, ROWS - 1)
    z, send_dn, aux, target, local = well_rows(
        jnp.stack([r, c]), wells, center, links, process, block
    )
    got_dn = shift(send_dn, "row", ROWS, 1)
    z, left, right = merge(local, z, aux, up, got_dn)
    zl = shift(right, "col", COLS, COLS - 1)
    zr = shift(left, "col", COLS, 1)

    cell = jnp.arange(cells, dtype=jnp.int32)
    gx, gy = cell // NGY, cell % NGY
    coef = jnp.concatenate(
        [
            center[None],
            jnp.where(gx == 0, 0.0, links[0])[None],
            jnp.where(gx == cells // NGY - 1, 0.0, links[1])[None],
            jnp.where(gy == 0, 0.0, links[2])[None],
            jnp.where(gy == NGY - 1, 0.0, links[3])[None],
            process[None],
        ]
    )
    coef = after(coef, send_dn)
    col_coef = lax.dynamic_slice_in_dim(coef, col_start, cols, 1)
    row_part = lax.dynamic_slice_in_dim(coef, row_start, rows, 1)
    x, g = well_cols(z, zl, zr, col_coef[:5], aux, target)

    g = g + shift(g, "col", COLS, 4) + shift(g, "col", COLS, 8) + shift(g, "col", COLS, 12)
    g = jnp.stack([g, flip(g, "col", COLS, 2)])
    g = jnp.stack([g, flip(g, "row", ROWS, 1)])
    g = jnp.stack([g] + [shift(g, "row", ROWS, 2 * d) for d in range(1, 4)])
    g = g.reshape(ROWS, 2, HALF, NGY)
    g_other = flip(g, "col", COLS, 1)

    turn = [
        (a * COLS + 2 * b + k, b * COLS + 2 * a + k)
        for a in range(ROWS)
        for b in range(ROWS)
        for k in range(2)
    ]
    turned = lax.ppermute(x, ("row", "col"), turn)
    pair, more, far, less = ring(x, "row", ROWS, 1, 2)
    x_parts = [pair, more, *far, less]
    pair, more, far, less = ring(turned, "col", COLS, 2, 4)
    own = [pair, more, *far, less]
    far = jnp.stack(far)
    other = [flip(a, "col", COLS, 1) for a in (pair, more, far, less)]

    dn = shift(after(block[:NGY], x), "row", ROWS, 1)
    right = jnp.concatenate([a[:, cols - NGY :] for a in (up, block, dn)])
    left = jnp.concatenate([a[:, :NGY] for a in (up, block, dn)])
    el = shift(after(right, turned), "col", COLS, COLS - 1)
    er = shift(after(left, turned), "col", COLS, 1)

    start = ((row_start - col_start) // NGY)[None]
    row_coef = jnp.concatenate([after(row_part, x), jnp.zeros((2, rows), F32)]).T
    pred = predict(start, block, row_coef, col_coef[:5], col_coef[5:6])

    w = after(wells, z)[0]
    part = w // cols
    number = jnp.arange(M, dtype=jnp.int32)
    same = (part[:, None] == part[None, :]) & (number[None, :] < number[:, None])
    rank = jnp.sum(same.astype(jnp.int32), axis=1)
    wr, wc = part // 2, part
    in_row = (wc % 2) * WMAX + rank
    row_slot = ((wr // 2 - r // 2) % 4 * 2 + (wr % 2 ^ r % 2)) * HALF + in_row
    strip_slot = ((wr // 2 - c // 4) % 4 * 2 + (wr % 2 ^ (c // 2) % 2)) * HALF + in_row
    col_slot = (
        (wc % 2 ^ c % 2) * (2 * NGY)
        + ((wc // 2) % 2 ^ (c // 2) % 2) * NGY
        + (wc // 4) * WMAX
        + rank
    )
    xc = across(row_slot[:, None], x_parts)
    own = strip(strip_slot[None], own)
    other = strip(strip_slot[None], other)
    inv = inverse(g, g_other, row_slot[:, None], col_slot[None], noise)
    rims = (up, dn, el, er)
    return update((c % 2)[None], pred, inv, xc, row_coef, col_coef[:5], rims, own, other)


def solution(mesh):
    in_specs = (P("row", "col"), P(), P(), P(), P(), P())
    out_specs = P("row", "col")
    return jax.shard_map(shards, mesh=mesh, in_specs=in_specs, out_specs=out_specs, check_vma=False)
```

time: 233 us -> 179 us (0.77)
  starting transfers between devices: 81.4 us -> 52.7 us
  local copies, waits for them, and re-layouts: 31.7 us -> 18.2 us
  between operations: 13.8 us -> 0.59 us
  waiting for transfers between devices: 35.5 us -> 46.1 us
  Pallas kernels: 61.1 us -> 54.7 us
  other arithmetic: 8.27 us -> 3.79 us
    ppermute x6 -> x21, waiting for transfers between devices: 5 us -> 35.6 us  [shift(): lax.ppermute(x, axis, [((i + back) % count, i) for i in range(count)])]
    ppermute x8 -> x0, starting transfers between devices: 27.6 us -> none  [the longest x1 8.19 us: shards(): lax.ppermute(block[rows - NGY:], 'row', [(i, i + 1) for i in range(ROWS -...]
    ppermute x6 -> x21, starting transfers between devices: 25.4 us -> 37.9 us  [shift(): lax.ppermute(x, axis, [((i + back) % count, i) for i in range(count)])]
    ppermute x8 -> x0, waiting for transfers between devices: 12.1 us -> none  [the longest x1 5 us: shards(): el = lax.ppermute(right_edge, 'col', [(i, i + 1) for i in range(COLS - 1)])]
    ppermute x3 -> x9, waiting for transfers between devices: 13.7 us -> 1.54 us  [flip(): return lax.ppermute(x, axis, [(i, i ^ bit) for i in range(count)])]
    ppermute x3 -> x9, starting transfers between devices: 24.8 us -> 12.9 us  [flip(): return lax.ppermute(x, axis, [(i, i ^ bit) for i in range(count)])]
    pallas_call x1, Pallas kernels: 29.7 us -> 18.9 us  [inverse(): pl.pallas_call(inverse_kernel, out_shape=jax.ShapeDtypeStruct((M, M), F32...]
    concatenate x2 -> x1, local copies, waits for them, and re-layouts: 6.56 us -> 0.64 us  [shards(): jnp.concatenate([center[None], jnp.where(gx == 0, 0.0, links[0])[None], j...]
  transfers between devices with their start and end apart: 20 -> 31, of which waited for: 9 -> 10; matrix products, arithmetic and copies ran while one was open for 5% -> 6% of each run, Pallas kernels for 18% -> 17%
where the time goes in v2:
time: 179 us; the launch traced here: 176 us
  Pallas kernels  54.7 us (31%)
  starting transfers between devices  52.7 us (29%)
  waiting for transfers between devices  46.1 us (26%)
  local copies, waits for them, and re-layouts  18.2 us (10%)
  other arithmetic  3.79 us (2%)
    ppermute x21, starting transfers between devices, shift(): lax.ppermute(x, axis, [((i + back) % count, i) for i in range(count)])  37.9 us
    ppermute x21, waiting for transfers between devices, shift(): lax.ppermute(x, axis, [((i + back) % count, i) for i in range(count)])  35.6 us
    pallas_call x1, Pallas kernels, inverse(): pl.pallas_call(inverse_kernel, out_shape=jax.ShapeDtypeStruct((M, M), F32...  18.9 us
    pallas_call x1, Pallas kernels, update(): pl.pallas_call(update_kernel, out_shape=jax.ShapeDtypeStruct((rows, cols)...  13.1 us
    ppermute x9, starting transfers between devices, flip(): return lax.ppermute(x, axis, [(i, i ^ bit) for i in range(count)])  12.9 us
    unnamed x56, local copies, waits for them, and re-layouts  11.6 us
    pallas_call x1, Pallas kernels, predict(): pl.pallas_call(predict_kernel, out_shape=jax.ShapeDtypeStruct((rows, cols...  9.18 us
    ppermute x1, waiting for transfers between devices, shards(): turned = lax.ppermute(x, ('row', 'col'), turn)  8.99 us
  transfers between devices with their start and end apart: 31, of which 10 were waited for; matrix products, arithmetic and copies ran while one was open for 6% of the time, Pallas kernels for 17%

profile of v2, /device:TPU:3, one launch (start us, length us, event | category | flops | bytes accessed | tf_op | source)
XLA Modules:
  0.0 176.1 jit_solution(9200938519243804887)
XLA Ops:
  0.1 3.4 %copy-done = f32[2048,1024]{1,0:T(8,128)S(1)} copy-done((f32[2048,1024]{1,0:T(8,128)S(1)}, f32[2048,1024]{1,0:T(8,128)}, u32[]{:S(2)}) %copy-start) | copy-done | bytes 8388632
  6.8 6.5 %well_rows.1 = (f32[64,1024]{1,0:T(8,128)S(1)}, f32[32,1024]{1,0:T(8,128)S(1)}, f32[64,128]{1,0:T(8,128)S(1)}, s32[1,128]{1,0:T(1,128)S(1)}, s32[32]{0:T(128)S(1)}) custom-call(s32[2]{0:T(128)S(1)} %pad_add_fusion.place, s32[1,256]{1,0:T(1,128)S(1)} %copy-done.12, f32[16384]{0:T(1024)S(1)} %copy-done.6, f32[4,16384]{1,0:T(4,128)S(1)} %copy-done.4, ...), custom_call_target="tpu_custom_call" | custom-call | flops 655360 | bytes 8388608 | tf_op jit(solution)/shard_map/well_rows/pallas_call | solution.py:120
  13.3 4.8 %collective-permute-start.1 = (f32[32,1024]{1,0:T(8,128)S(1)}, f32[32,1024]{1,0:T(8,128)S(1)}, u32[]{:S(2)}, u32[]{:S(2)}) collective-permute-start(f32[32,1024]{1,0:T(8,128)S(1)} %get-tuple-element.25), channel_id=1, source_target_pairs={{16,0},{32,16},{48,32},{64,48},{80,64},{96,80},{112,96},{0,112},{1... | collective-permute-start | bytes 393224 | tf_op jit(solution)/shard_map/ppermute | solution.py:512
  21.6 11.2 %collective-permute-done.up_ref = f32[128,1024]{1,0:T(8,128)S(1)} collective-permute-done((f32[128,1024]{1,0:T(8,128)S(1)}, f32[128,1024]{1,0:T(8,128)S(1)}, u32[]{:S(2)}, u32[]{:S(2)}) %collective-permute-start) | collective-permute-done | bytes 524320 | tf_op jit(solution)/shard_map/ppermute | solution.py:512
  35.8 4.4 %collective-permute-start.2 = (f32[64,128]{1,0:T(8,128)}, f32[64,128]{1,0:T(8,128)S(1)}, u32[]{:S(2)}, u32[]{:S(2)}) collective-permute-start(f32[64,128]{1,0:T(8,128)} %get-tuple-element.31), channel_id=1, source_target_pairs={{15,0},{0,1},{1,2},{2,3},{3,4},{4,5},{5,6},{6,7},{7,8},{8,9},{9,10... | collective-permute-start | bytes 98312 | tf_op jit(solution)/shard_map/ppermute | solution.py:512
  41.6 3.7 %collective-permute-done.3.zr_ref = f32[64,128]{1,0:T(8,128)S(1)} collective-permute-done((f32[64,128]{1,0:T(8,128)}, f32[64,128]{1,0:T(8,128)S(1)}, u32[]{:S(2)}, u32[]{:S(2)}) %collective-permute-start.3) | collective-permute-done | bytes 32800 | tf_op jit(solution)/shard_map/ppermute | solution.py:512
  56.2 2.5 %collective-permute-start.7 = (f32[64,128]{1,0:T(8,128)S(1)}, f32[64,128]{1,0:T(8,128)S(1)}, u32[]{:S(2)}, u32[]{:S(2)}) collective-permute-start(f32[64,128]{1,0:T(8,128)S(1)} %add_add_fusion), channel_id=1, source_target_pairs={{0,2},{1,3},{2,0},{3,1},{4,6},{5,7},{6,4},{7,5},{8,10},{9,11},{10,... | collective-permute-start | bytes 98312 | tf_op jit(solution)/shard_map/ppermute | solution.py:516
  61.0 9.0 %collective-permute-done.19 = f32[64,1024]{1,0:T(8,128)S(1)} collective-permute-done((f32[64,1024]{1,0:T(8,128)}, f32[64,1024]{1,0:T(8,128)S(1)}, u32[]{:S(2)}, u32[]{:S(2)}) %collective-permute-start.19) | collective-permute-done | bytes 262176 | tf_op jit(solution)/shard_map/ppermute | solution.py:578
  70.0 6.5 %collective-permute-start.22 = (f32[64,1024]{1,0:T(8,128)S(1)}, f32[64,1024]{1,0:T(8,128)S(1)}, u32[]{:S(2)}, u32[]{:S(2)}) collective-permute-start(f32[64,1024]{1,0:T(8,128)S(1)} %collective-permute-done.19), channel_id=1, source_target_pairs={{0,2},{1,3},{2,0},{3,1},{4,6},{5,7},{6,4},{7,5},{8,10},{9,11},{10,... | collective-permute-start | bytes 786440 | tf_op jit(solution)/shard_map/ppermute | solution.py:516
  77.2 3.9 %collective-permute-start.10 = (f32[2,2,64,128]{3,2,1,0:T(8,128)}, f32[2,2,64,128]{3,2,1,0:T(8,128)}, u32[]{:S(2)}, u32[]{:S(2)}) collective-permute-start(f32[2,2,64,128]{3,2,1,0:T(8,128)} %get-tuple-element.60), channel_id=1, source_target_pairs={{64,0},{80,16},{96,32},{112,48},{0,64},{16,80},{32,96},{48,112},{6... | collective-permute-start | bytes 393224 | tf_op jit(solution)/shard_map/ppermute | solution.py:512
  83.3 3.1 %collective-permute-start.16 = (f32[2,64,1024]{2,1,0:T(8,128)S(1)}, f32[2,64,1024]{2,1,0:T(8,128)S(1)}, u32[]{:S(2)}, u32[]{:S(2)}) collective-permute-start(f32[2,64,1024]{2,1,0:T(8,128)S(1)} %pad_maximum_fusion.3.refs_0_), channel_id=1, source_target_pairs={{96,0},{112,16},{0,32},{16,48},{32,64},{48,80},{64,96},{80,112},{9... | collective-permute-start | bytes 1572872 | tf_op jit(solution)/shard_map/ppermute | solution.py:512
  88.2 3.4 %copy-done.1 = f32[2048,1024]{1,0:T(8,128)S(1)} copy-done((f32[2048,1024]{1,0:T(8,128)S(1)}, f32[2048,1024]{1,0:T(8,128)}, u32[]{:S(2)}) %copy-start.1) | copy-done | bytes 8388632
  91.6 9.2 %predict.1.pred_ref = f32[2048,1024]{1,0:T(8,128)S(1)} custom-call(s32[1]{0:T(128)} %bitcast.1.start, f32[2048,1024]{1,0:T(8,128)S(1)} %copy-done.1, f32[2048,8]{1,0:T(8,128)S(1)} %copy.16.rc_ref, f32[5,1024]{1,0:T(8,128)S(1)} %copy-done.5, f32[1,1024]{1,0:T(1,128)S(1)} %dynamic-slice.1.proc_ref), custom_call_target="tpu_custom_call" | custom-call | flops 46137344 | bytes 16777216 | tf_op jit(solution)/shard_map/predict/pallas_call | solution.py:259
  102.9 2.5 %collective-permute-start.12 = (f32[8,2,64,128]{3,2,1,0:T(8,128)S(1)}, f32[8,2,64,128]{3,2,1,0:T(8,128)S(1)}, u32[]{:S(2)}, u32[]{:S(2)}) collective-permute-start(f32[8,2,64,128]{3,2,1,0:T(8,128)S(1)} %bitcast.40), channel_id=1, source_target_pairs={{0,1},{1,0},{2,3},{3,2},{4,5},{5,4},{6,7},{7,6},{8,9},{9,8},{10,11... | collective-permute-start | bytes 1572872 | tf_op jit(solution)/shard_map/ppermute | solution.py:516
  105.6 4.3 %collective-permute-start.23 = (f32[2,64,1024]{2,1,0:T(8,128)S(1)}, f32[2,64,1024]{2,1,0:T(8,128)S(1)}, u32[]{:S(2)}, u32[]{:S(2)}) collective-permute-start(f32[2,64,1024]{2,1,0:T(8,128)S(1)} %pad_maximum_fusion.4.refs_0_), channel_id=1, source_target_pairs={{4,0},{5,1},{6,2},{7,3},{8,4},{9,5},{10,6},{11,7},{12,8},{13,9},{1... | collective-permute-start | bytes 1572872 | tf_op jit(solution)/shard_map/ppermute | solution.py:512
  109.9 6.9 %collective-permute-done.25.refs_4_ = f32[2,64,1024]{2,1,0:T(8,128)S(1)} collective-permute-done((f32[2,64,1024]{2,1,0:T(8,128)S(1)}, f32[2,64,1024]{2,1,0:T(8,128)S(1)}, u32[]{:S(2)}, u32[]{:S(2)}) %collective-permute-start.25) | collective-permute-done | bytes 524320 | tf_op jit(solution)/shard_map/ppermute | solution.py:512
  116.9 3.9 %collective-permute-done.23.refs_1_ = f32[2,64,1024]{2,1,0:T(8,128)S(1)} collective-permute-done((f32[2,64,1024]{2,1,0:T(8,128)S(1)}, f32[2,64,1024]{2,1,0:T(8,128)S(1)}, u32[]{:S(2)}, u32[]{:S(2)}) %collective-permute-start.23) | collective-permute-done | bytes 524320 | tf_op jit(solution)/shard_map/ppermute | solution.py:512
  123.0 2.7 %collective-permute-start.24 = (f32[64,1024]{1,0:T(8,128)S(1)}, f32[64,1024]{1,0:T(8,128)S(1)}, u32[]{:S(2)}, u32[]{:S(2)}) collective-permute-start(f32[64,1024]{1,0:T(8,128)S(1)} %slice_bitcast_fusion.1), channel_id=1, source_target_pairs={{4,0},{5,1},{6,2},{7,3},{8,4},{9,5},{10,6},{11,7},{12,8},{13,9},{1... | collective-permute-start | bytes 786440 | tf_op jit(solution)/shard_map/ppermute | solution.py:512
  125.9 3.1 %collective-permute-done.24.refs_2_ = f32[64,1024]{1,0:T(8,128)S(1)} collective-permute-done((f32[64,1024]{1,0:T(8,128)S(1)}, f32[64,1024]{1,0:T(8,128)S(1)}, u32[]{:S(2)}, u32[]{:S(2)}) %collective-permute-start.24) | collective-permute-done | bytes 262176 | tf_op jit(solution)/shard_map/ppermute | solution.py:512
  129.0 4.9 %collective-permute-start.21 = (f32[2304,128]{1,0:T(8,128)S(1)}, f32[2304,128]{1,0:T(8,128)S(1)}, u32[]{:S(2)}, u32[]{:S(2)}) collective-permute-start(f32[2304,128]{1,0:T(8,128)S(1)} %get-tuple-element.40), channel_id=1, source_target_pairs={{1,0},{2,1},{3,2},{4,3},{5,4},{6,5},{7,6},{8,7},{9,8},{10,9},{11,1... | collective-permute-start | bytes 3538952 | tf_op jit(solution)/shard_map/ppermute | solution.py:512
  134.0 2.6 %collective-permute-start.20 = (f32[2304,128]{1,0:T(8,128)S(1)}, f32[2304,128]{1,0:T(8,128)S(1)}, u32[]{:S(2)}, u32[]{:S(2)}) collective-permute-start(f32[2304,128]{1,0:T(8,128)S(1)} %get-tuple-element.39), channel_id=1, source_target_pairs={{15,0},{0,1},{1,2},{2,3},{3,4},{4,5},{5,6},{6,7},{7,8},{8,9},{9,10... | collective-permute-start | bytes 3538952 | tf_op jit(solution)/shard_map/ppermute | solution.py:512
  137.2 18.9 %inverse.1.inv_ref = f32[256,256]{1,0:T(8,128)S(1)} custom-call(f32[8,2,64,128]{3,2,1,0:T(8,128)S(1)} %bitcast.41, f32[8,2,64,128]{3,2,1,0:T(8,128)S(1)} %collective-permute-done.12.other_ref, s32[256,1]{1,0:T(8,128)S(1)} %fusion.7.rslot_ref.slot_ref, s32[1,256]{1,0:T(1,128)S(1)} %add_add_fusion.2.cslot_ref, f32[1,256]{1,0:T(1,128)S(1)} %copy-done.16), custom_call_target="tpu_custom_call" | custom-call | flops 18447998976 | bytes 4194304 | tf_op jit(solution)/shard_map/inverse/pallas_call | solution.py:378
  158.9 4.1 %collective-permute-done.21.er_ref = f32[2304,128]{1,0:T(8,128)S(1)} collective-permute-done((f32[2304,128]{1,0:T(8,128)S(1)}, f32[2304,128]{1,0:T(8,128)S(1)}, u32[]{:S(2)}, u32[]{:S(2)}) %collective-permute-start.21) | collective-permute-done | bytes 1179680 | tf_op jit(solution)/shard_map/ppermute | solution.py:512
  163.0 13.1 %update.1 = f32[2048,1024]{1,0:T(8,128)} custom-call(s32[1]{0:T(128)} %bitcast.core, f32[2048,1024]{1,0:T(8,128)S(1)} %predict.1.pred_ref, f32[256,256]{1,0:T(8,128)S(1)} %inverse.1.inv_ref, f32[256,1024]{1,0:T(8,128)S(1)} %across.1.xc_ref, f32[2048,8]{1,0:T(8,128)S(1)} %copy.16.rc_ref, f32[5,1024]{1,0:T(8,128)S(1)} %copy-done.5, f32[128,1024]{1,0:T(8,128)S(1)} %copy-done.3, ...), custom_call_target="tpu_custom_call" | custom-call | flops 3221225472 | bytes 16777216 | tf_op jit(solution)/shard_map/update/pallas_call | solution.py:495
  (135 shorter events, 37.0 us)
Async XLA Ops:
  13.3 8.3 %collective-permute-start.1 = (f32[32,1024]{1,0:T(8,128)S(1)}, f32[32,1024]{1,0:T(8,128)S(1)}, u32[]{:S(2)}, u32[]{:S(2)}) collective-permute-start(f32[32,1024]{1,0:T(8,128)S(1)} %get-tuple-element.25), channel_id=1, source_target_pairs={{16,0},{32,16},{48,32},{64,48},{80,64},{96,80},{112,96},{0,112},{1... | collective-permute-start | bytes 393224 | tf_op jit(solution)/shard_map/ppermute | solution.py:512
  18.2 14.7 %collective-permute-start = (f32[128,1024]{1,0:T(8,128)S(1)}, f32[128,1024]{1,0:T(8,128)S(1)}, u32[]{:S(2)}, u32[]{:S(2)}) collective-permute-start(f32[128,1024]{1,0:T(8,128)S(1)} %get-tuple-element.50), channel_id=1, source_target_pairs={{112,0},{0,16},{16,32},{32,48},{48,64},{64,80},{80,96},{96,112},{1... | collective-permute-start | bytes 1572872 | tf_op jit(solution)/shard_map/ppermute | solution.py:512
  48.1 7.3 %collective-permute-start.6 = (f32[64,128]{1,0:T(8,128)}, f32[64,128]{1,0:T(8,128)S(1)}, u32[]{:S(2)}, u32[]{:S(2)}) collective-permute-start(f32[64,128]{1,0:T(8,128)} %get-tuple-element.36), channel_id=1, source_target_pairs={{12,0},{13,1},{14,2},{15,3},{0,4},{1,5},{2,6},{3,7},{4,8},{5,9},{6... | collective-permute-start | bytes 98312 | tf_op jit(solution)/shard_map/ppermute | solution.py:512
  53.5 16.4 %collective-permute-start.19 = (f32[64,1024]{1,0:T(8,128)}, f32[64,1024]{1,0:T(8,128)S(1)}, u32[]{:S(2)}, u32[]{:S(2)}) collective-permute-start(f32[64,1024]{1,0:T(8,128)} %get-tuple-element.34), channel_id=1, source_target_pairs={{0,0},{1,1},{2,16},{3,17},{4,32},{5,33},{6,48},{7,49},{8,64},{9,65... | collective-permute-start | bytes 786440 | tf_op jit(solution)/shard_map/ppermute | solution.py:578
  58.7 24.4 %collective-permute-start.13 = (f32[64,1024]{1,0:T(8,128)}, f32[64,1024]{1,0:T(8,128)S(1)}, u32[]{:S(2)}, u32[]{:S(2)}) collective-permute-start(f32[64,1024]{1,0:T(8,128)} %get-tuple-element.34), channel_id=1, source_target_pairs={{0,16},{16,0},{32,48},{48,32},{64,80},{80,64},{96,112},{112,96},{1... | collective-permute-start | bytes 786440 | tf_op jit(solution)/shard_map/ppermute | solution.py:516
  60.9 15.7 %collective-permute-start.8 = (f32[2,64,128]{2,1,0:T(8,128)S(1)}, f32[2,64,128]{2,1,0:T(8,128)S(1)}, u32[]{:S(2)}, u32[]{:S(2)}) collective-permute-start(f32[2,64,128]{2,1,0:T(8,128)S(1)} %get-tuple-element.62), channel_id=1, source_target_pairs={{0,16},{16,0},{32,48},{48,32},{64,80},{80,64},{96,112},{112,96},{1... | collective-permute-start | bytes 196616 | tf_op jit(solution)/shard_map/ppermute | solution.py:516
  70.0 13.3 %collective-permute-start.22 = (f32[64,1024]{1,0:T(8,128)S(1)}, f32[64,1024]{1,0:T(8,128)S(1)}, u32[]{:S(2)}, u32[]{:S(2)}) collective-permute-start(f32[64,1024]{1,0:T(8,128)S(1)} %collective-permute-done.19), channel_id=1, source_target_pairs={{0,2},{1,3},{2,0},{3,1},{4,6},{5,7},{6,4},{7,5},{8,10},{9,11},{10,... | collective-permute-start | bytes 786440 | tf_op jit(solution)/shard_map/ppermute | solution.py:516
  76.5 29.0 %collective-permute-start.18 = (f32[128,1024]{1,0:T(8,128)S(1)}, f32[128,1024]{1,0:T(8,128)S(1)}, u32[]{:S(2)}, u32[]{:S(2)}) collective-permute-start(f32[128,1024]{1,0:T(8,128)S(1)} %get-tuple-element.38), channel_id=1, source_target_pairs={{16,0},{32,16},{48,32},{64,48},{80,64},{96,80},{112,96},{0,112},{1... | collective-permute-start | bytes 1572872 | tf_op jit(solution)/shard_map/ppermute | solution.py:512
  77.2 23.6 %collective-permute-start.10 = (f32[2,2,64,128]{3,2,1,0:T(8,128)}, f32[2,2,64,128]{3,2,1,0:T(8,128)}, u32[]{:S(2)}, u32[]{:S(2)}) collective-permute-start(f32[2,2,64,128]{3,2,1,0:T(8,128)} %get-tuple-element.60), channel_id=1, source_target_pairs={{64,0},{80,16},{96,32},{112,48},{0,64},{16,80},{32,96},{48,112},{6... | collective-permute-start | bytes 393224 | tf_op jit(solution)/shard_map/ppermute | solution.py:512
  81.1 20.0 %collective-permute-start.9 = (f32[2,2,64,128]{3,2,1,0:T(8,128)}, f32[2,2,64,128]{3,2,1,0:T(8,128)}, u32[]{:S(2)}, u32[]{:S(2)}) collective-permute-start(f32[2,2,64,128]{3,2,1,0:T(8,128)} %get-tuple-element.60), channel_id=1, source_target_pairs={{32,0},{48,16},{64,32},{80,48},{96,64},{112,80},{0,96},{16,112},{3... | collective-permute-start | bytes 393224 | tf_op jit(solution)/shard_map/ppermute | solution.py:512
  83.2 18.6 %collective-permute-start.11 = (f32[2,2,64,128]{3,2,1,0:T(8,128)}, f32[2,2,64,128]{3,2,1,0:T(8,128)}, u32[]{:S(2)}, u32[]{:S(2)}) collective-permute-start(f32[2,2,64,128]{3,2,1,0:T(8,128)} %get-tuple-element.60), channel_id=1, source_target_pairs={{96,0},{112,16},{0,32},{16,48},{32,64},{48,80},{64,96},{80,112},{9... | collective-permute-start | bytes 393224 | tf_op jit(solution)/shard_map/ppermute | solution.py:512
  83.3 22.3 %collective-permute-start.16 = (f32[2,64,1024]{2,1,0:T(8,128)S(1)}, f32[2,64,1024]{2,1,0:T(8,128)S(1)}, u32[]{:S(2)}, u32[]{:S(2)}) collective-permute-start(f32[2,64,1024]{2,1,0:T(8,128)S(1)} %pad_maximum_fusion.3.refs_0_), channel_id=1, source_target_pairs={{96,0},{112,16},{0,32},{16,48},{32,64},{48,80},{64,96},{80,112},{9... | collective-permute-start | bytes 1572872 | tf_op jit(solution)/shard_map/ppermute | solution.py:512
  100.8 16.0 %collective-permute-start.14 = (f32[2,64,1024]{2,1,0:T(8,128)S(1)}, f32[2,64,1024]{2,1,0:T(8,128)S(1)}, u32[]{:S(2)}, u32[]{:S(2)}) collective-permute-start(f32[2,64,1024]{2,1,0:T(8,128)S(1)} %pad_maximum_fusion.3.refs_0_), channel_id=1, source_target_pairs={{32,0},{48,16},{64,32},{80,48},{96,64},{112,80},{0,96},{16,112},{3... | collective-permute-start | bytes 1572872 | tf_op jit(solution)/shard_map/ppermute | solution.py:512
  101.2 15.6 %collective-permute-start.25 = (f32[2,64,1024]{2,1,0:T(8,128)S(1)}, f32[2,64,1024]{2,1,0:T(8,128)S(1)}, u32[]{:S(2)}, u32[]{:S(2)}) collective-permute-start(f32[2,64,1024]{2,1,0:T(8,128)S(1)} %pad_maximum_fusion.4.refs_0_), channel_id=1, source_target_pairs={{12,0},{13,1},{14,2},{15,3},{0,4},{1,5},{2,6},{3,7},{4,8},{5,9},{6... | collective-permute-start | bytes 1572872 | tf_op jit(solution)/shard_map/ppermute | solution.py:512
  102.9 31.1 %collective-permute-start.12 = (f32[8,2,64,128]{3,2,1,0:T(8,128)S(1)}, f32[8,2,64,128]{3,2,1,0:T(8,128)S(1)}, u32[]{:S(2)}, u32[]{:S(2)}) collective-permute-start(f32[8,2,64,128]{3,2,1,0:T(8,128)S(1)} %bitcast.40), channel_id=1, source_target_pairs={{0,1},{1,0},{2,3},{3,2},{4,5},{5,4},{6,7},{7,6},{8,9},{9,8},{10,11... | collective-permute-start | bytes 1572872 | tf_op jit(solution)/shard_map/ppermute | solution.py:516
  105.4 31.1 %collective-permute-start.27 = (f32[2,64,1024]{2,1,0:T(8,128)S(1)}, f32[2,64,1024]{2,1,0:T(8,128)S(1)}, u32[]{:S(2)}, u32[]{:S(2)}) collective-permute-start(f32[2,64,1024]{2,1,0:T(8,128)S(1)} %pad_maximum_fusion.4.refs_0_), channel_id=1, source_target_pairs={{0,1},{1,0},{2,3},{3,2},{4,5},{5,4},{6,7},{7,6},{8,9},{9,8},{10,11... | collective-permute-start | bytes 1572872 | tf_op jit(solution)/shard_map/ppermute | solution.py:516
  105.6 15.2 %collective-permute-start.23 = (f32[2,64,1024]{2,1,0:T(8,128)S(1)}, f32[2,64,1024]{2,1,0:T(8,128)S(1)}, u32[]{:S(2)}, u32[]{:S(2)}) collective-permute-start(f32[2,64,1024]{2,1,0:T(8,128)S(1)} %pad_maximum_fusion.4.refs_0_), channel_id=1, source_target_pairs={{4,0},{5,1},{6,2},{7,3},{8,4},{9,5},{10,6},{11,7},{12,8},{13,9},{1... | collective-permute-start | bytes 1572872 | tf_op jit(solution)/shard_map/ppermute | solution.py:512
  116.8 19.8 %collective-permute-start.17 = (f32[64,1024]{1,0:T(8,128)S(1)}, f32[64,1024]{1,0:T(8,128)S(1)}, u32[]{:S(2)}, u32[]{:S(2)}) collective-permute-start(f32[64,1024]{1,0:T(8,128)S(1)} %slice_bitcast_fusion.2), channel_id=1, source_target_pairs={{96,0},{112,16},{0,32},{16,48},{32,64},{48,80},{64,96},{80,112},{9... | collective-permute-start | bytes 786440 | tf_op jit(solution)/shard_map/ppermute | solution.py:512
  120.8 16.3 %collective-permute-start.15 = (f32[64,1024]{1,0:T(8,128)S(1)}, f32[64,1024]{1,0:T(8,128)S(1)}, u32[]{:S(2)}, u32[]{:S(2)}) collective-permute-start(f32[64,1024]{1,0:T(8,128)S(1)} %slice_bitcast_fusion.3), channel_id=1, source_target_pairs={{32,0},{48,16},{64,32},{80,48},{96,64},{112,80},{0,96},{16,112},{3... | collective-permute-start | bytes 786440 | tf_op jit(solution)/shard_map/ppermute | solution.py:512
  129.0 34.0 %collective-permute-start.21 = (f32[2304,128]{1,0:T(8,128)S(1)}, f32[2304,128]{1,0:T(8,128)S(1)}, u32[]{:S(2)}, u32[]{:S(2)}) collective-permute-start(f32[2304,128]{1,0:T(8,128)S(1)} %get-tuple-element.40), channel_id=1, source_target_pairs={{1,0},{2,1},{3,2},{4,3},{5,4},{6,5},{7,6},{8,7},{9,8},{10,9},{11,1... | collective-permute-start | bytes 3538952 | tf_op jit(solution)/shard_map/ppermute | solution.py:512
  134.0 29.0 %collective-permute-start.20 = (f32[2304,128]{1,0:T(8,128)S(1)}, f32[2304,128]{1,0:T(8,128)S(1)}, u32[]{:S(2)}, u32[]{:S(2)}) collective-permute-start(f32[2304,128]{1,0:T(8,128)S(1)} %get-tuple-element.39), channel_id=1, source_target_pairs={{15,0},{0,1},{1,2},{2,3},{3,4},{4,5},{5,6},{6,7},{7,8},{8,9},{9,10... | collective-permute-start | bytes 3538952 | tf_op jit(solution)/shard_map/ppermute | solution.py:512
  136.6 21.5 %collective-permute-start.30 = (f32[2,64,1024]{2,1,0:T(8,128)S(1)}, f32[2,64,1024]{2,1,0:T(8,128)S(1)}, u32[]{:S(2)}, u32[]{:S(2)}) collective-permute-start(f32[2,64,1024]{2,1,0:T(8,128)S(1)} %collective-permute-done.25.refs_4_), channel_id=1, source_target_pairs={{0,1},{1,0},{2,3},{3,2},{4,5},{5,4},{6,7},{7,6},{8,9},{9,8},{10,11... | collective-permute-start | bytes 1572872 | tf_op jit(solution)/shard_map/ppermute | solution.py:516
  136.6 21.5 %collective-permute-start.28 = (f32[2,64,1024]{2,1,0:T(8,128)S(1)}, f32[2,64,1024]{2,1,0:T(8,128)S(1)}, u32[]{:S(2)}, u32[]{:S(2)}) collective-permute-start(f32[2,64,1024]{2,1,0:T(8,128)S(1)} %collective-permute-done.23.refs_1_), channel_id=1, source_target_pairs={{0,1},{1,0},{2,3},{3,2},{4,5},{5,4},{6,7},{7,6},{8,9},{9,8},{10,11... | collective-permute-start | bytes 1572872 | tf_op jit(solution)/shard_map/ppermute | solution.py:516
  137.1 21.0 %collective-permute-start.29 = (f32[2,64,1024]{2,1,0:T(8,128)S(1)}, f32[2,64,1024]{2,1,0:T(8,128)S(1)}, u32[]{:S(2)}, u32[]{:S(2)}) collective-permute-start(f32[2,64,1024]{2,1,0:T(8,128)S(1)} %pad_maximum_fusion.5), channel_id=1, source_target_pairs={{0,1},{1,0},{2,3},{3,2},{4,5},{5,4},{6,7},{7,6},{8,9},{9,8},{10,11... | collective-permute-start | bytes 1572872 | tf_op jit(solution)/shard_map/ppermute | solution.py:516
  (35 other events, 271.2 us)

commit v3 on v2

--- a/solution.py
+++ b/solution.py
@@ -27,20 +27,22 @@
     return [pl.BlockSpec(memory_space=pltpu.VMEM)] * count
 
 
-def rows_kernel(
+def table_kernel(
     place, wells, center, links, process, block,
-    z_ref, dn_ref, aux_ref, target_ref, local_ref,
+    z_ref, up_ref, dn_ref, aux_ref, target_ref, top_ref, low_ref, left_ref, right_ref,
     p_ref, own, side, noise, cell, count, sems,
 ):
-    rows, cols = p_ref.shape
+    rows, cols = block.shape
     r, c = place[0], place[1]
     row_start, col_start = pl.multiple_of(r * rows, rows), c * cols
     part = pl.ds(row_start, rows)
     copies = [
-        pltpu.make_async_copy(block, p_ref, sems.at[0]),
-        pltpu.make_async_copy(center.at[part], own, sems.at[1]),
-        pltpu.make_async_copy(links.at[:, part], side, sems.at[2]),
-        pltpu.make_async_copy(process.at[part], noise, sems.at[3]),
+        pltpu.make_async_copy(block.at[pl.ds(0, NGY)], top_ref, sems.at[0]),
+        pltpu.make_async_copy(block.at[pl.ds(rows - NGY, NGY)], low_ref, sems.at[1]),
+        pltpu.make_async_copy(center.at[part], own, sems.at[2]),
+        pltpu.make_async_copy(links.at[:, part], side, sems.at[3]),
+        pltpu.make_async_copy(process.at[part], noise, sems.at[4]),
+        pltpu.make_async_copy(block, p_ref, sems.at[5]),
     ]
     for copy in copies:
         copy.start()
@@ -54,41 +56,51 @@
         return carry
 
     lax.fori_loop(0, SLOTS // 16, none, 0)
+    shift_by = cols.bit_length() - 1
 
     def put(m, carry):
         w = wells[0, m]
-        home = w // cols
+        home = w >> shift_by
         n = count[home]
         cell[home * WMAX + n] = w
         count[home] = n + 1
         return carry
 
-    lax.fori_loop(0, M, put, 0, unroll=8)
+    lax.fori_loop(0, M, put, 0, unroll=16)
     for copy in copies:
         copy.wait()
 
+    left_ref[NGY : rows + NGY, :] = p_ref[:, 0:NGY]
+    right_ref[NGY : rows + NGY, :] = p_ref[:, cols - NGY :]
     lane = lax.broadcasted_iota(jnp.int32, (1, NGY), 1)
-    top = ROWS - 1
+
+    def two(s, carry):
+        up = cell[jnp.minimum((r + 1) * HALF + s, SLOTS - 1)] - NGY - row_start - (rows - NGY)
+        dn = cell[jnp.maximum(r * HALF - WMAX + s, 0)] + NGY - row_start
+        up_ref[pl.ds(s, 1), :] = low_ref[pl.ds(jnp.clip(up, 0, NGY - 1), 1), :]
+        dn_ref[pl.ds(s, 1), :] = top_ref[pl.ds(jnp.clip(dn, 0, NGY - 1), 1), :]
+        return carry
+
+    lax.fori_loop(0, WMAX, two, 0, unroll=4)
 
     def one(s, carry):
         w = cell[r * HALF + s]
         good = w >= 0
         i = jnp.where(good, w - row_start, 0)
         first, final = i < NGY, i >= rows - NGY
-        gy = i % NGY
+        gy = i & (NGY - 1)
         gate = jnp.where(good, 1.0, 0.0)
-        k0, k1, k2 = own[i] * gate, side[0, i] * gate, side[1, i] * gate
+        k1, k2 = side[0, i] * gate, side[1, i] * gate
         k3 = jnp.where(gy == 0, 0.0, side[2, i] * gate)
         k4 = jnp.where(gy == NGY - 1, 0.0, side[3, i] * gate)
-        total = k0 * p_ref[pl.ds(i, 1), :]
-        above = p_ref[pl.ds(jnp.maximum(i - NGY, 0), 1), :]
-        below = p_ref[pl.ds(jnp.minimum(i + NGY, rows - 1), 1), :]
-        total = total + jnp.where(first, 0.0, k1) * above + jnp.where(final, 0.0, k2) * below
-        before = p_ref[pl.ds(jnp.maximum(i - 1, 0), 1), :]
-        after = p_ref[pl.ds(jnp.minimum(i + 1, rows - 1), 1), :]
-        z_ref[pl.ds(s, 1), :] = total + k3 * before + k4 * after
+        low, high = jnp.maximum(i - 1, 0), jnp.minimum(i + 1, rows - 1)
+        above, below = jnp.maximum(i - NGY, 0), jnp.minimum(i + NGY, rows - 1)
+        total = (own[i] * gate) * p_ref[pl.ds(i, 1), :]
+        total = total + jnp.where(first, 0.0, k1) * p_ref[pl.ds(above, 1), :]
+        total = total + jnp.where(final, 0.0, k2) * p_ref[pl.ds(below, 1), :]
+        z_ref[pl.ds(s, 1), :] = total + k3 * p_ref[pl.ds(low, 1), :] + k4 * p_ref[pl.ds(high, 1), :]
         row = jnp.where(lane == 0, jnp.where(first & (r > 0), k1, 0.0), 0.0)
-        row = jnp.where(lane == 1, jnp.where(final & (r < top), k2, 0.0), row)
+        row = jnp.where(lane == 1, jnp.where(final & (r < ROWS - 1), k2, 0.0), row)
         row = jnp.where(lane == 2, noise[i] * gate, row)
         col = jnp.where(good, w - col_start, -1)
         row = jnp.where(lane == 3, jnp.full((1, NGY), col, jnp.int32).astype(F32), row)
@@ -96,15 +108,6 @@
         return carry
 
     lax.fori_loop(0, HALF, one, 0, unroll=4)
-
-    def two(s, carry):
-        dn = cell[jnp.maximum(r * HALF - WMAX + s, 0)] + NGY - row_start
-        dn_ref[pl.ds(s, 1), :] = p_ref[pl.ds(jnp.clip(dn, 0, rows - 1), 1), :]
-        local_ref[s] = jnp.clip(cell[r * HALF + s] - row_start, 0, NGY - 1)
-        return carry
-
-    lax.fori_loop(0, WMAX, two, 0, unroll=4)
-
     base = (c // 4) * WMAX
 
     def three(t, row):
@@ -113,21 +116,25 @@
     target_ref[...] = lax.fori_loop(0, WMAX, three, jnp.full((1, NGY), -1, jnp.int32), unroll=4)
 
 
-def well_rows(place, wells, center, links, process, block):
+def tables(place, wells, center, links, process, block):
     rows, cols = block.shape
     smem = pl.BlockSpec(memory_space=pltpu.SMEM)
     hbm = pl.BlockSpec(memory_space=pltpu.HBM)
     return pl.pallas_call(
-        rows_kernel,
+        table_kernel,
         out_shape=(
             jax.ShapeDtypeStruct((HALF, cols), F32),
             jax.ShapeDtypeStruct((WMAX, cols), F32),
+            jax.ShapeDtypeStruct((WMAX, cols), F32),
             jax.ShapeDtypeStruct((HALF, NGY), F32),
             jax.ShapeDtypeStruct((1, NGY), jnp.int32),
-            jax.ShapeDtypeStruct((WMAX,), jnp.int32),
+            jax.ShapeDtypeStruct((NGY, cols), F32),
+            jax.ShapeDtypeStruct((NGY, cols), F32),
+            jax.ShapeDtypeStruct((rows + 2 * NGY, NGY), F32),
+            jax.ShapeDtypeStruct((rows + 2 * NGY, NGY), F32),
         ),
         in_specs=[smem, smem, hbm, hbm, hbm, hbm],
-        out_specs=tuple(vmem(4)) + (smem,),
+        out_specs=tuple(vmem(9)),
         scratch_shapes=[
             pltpu.VMEM((rows, cols), F32),
             pltpu.SMEM((rows,), F32),
@@ -135,30 +142,24 @@
             pltpu.SMEM((rows,), F32),
             pltpu.SMEM((SLOTS,), jnp.int32),
             pltpu.SMEM((SLOTS // WMAX,), jnp.int32),
-            pltpu.SemaphoreType.DMA((4,)),
+            pltpu.SemaphoreType.DMA((6,)),
         ],
-        compiler_params=pltpu.CompilerParams(vmem_limit_bytes=24 << 20),
-        cost_estimate=cost(10 * HALF * cols, block.size * 4),
-        name="well_rows",
+        compiler_params=pltpu.CompilerParams(vmem_limit_bytes=60 << 20),
+        cost_estimate=cost(1 << 20, 2 << 20),
+        name="tables",
     )(place, wells, center, links, process, block)
 
 
-def merge_kernel(local, z_ref, aux_ref, up_ref, dn_ref, o_ref, left_ref, right_ref):
+def merge_kernel(z_ref, aux_ref, up_ref, dn_ref, o_ref, left_ref, right_ref):
     cols = z_ref.shape[1]
     scale = aux_ref[...]
-
-    def one(s, carry):
-        o_ref[pl.ds(s, 1), :] = up_ref[pl.ds(local[s], 1), :]
-        return carry
-
-    lax.fori_loop(0, WMAX, one, 0, unroll=4)
-    o_ref[0:WMAX] = z_ref[0:WMAX] + scale[0:WMAX, 0:1] * o_ref[0:WMAX]
+    o_ref[0:WMAX] = z_ref[0:WMAX] + scale[0:WMAX, 0:1] * up_ref[...]
     o_ref[WMAX:] = z_ref[WMAX:] + scale[WMAX:, 1:2] * dn_ref[...]
     left_ref[...] = o_ref[:, 0:NGY]
     right_ref[...] = o_ref[:, cols - NGY :]
 
 
-def merge(local, z, aux, up, dn):
+def merge(z, aux, up, dn):
     cols = z.shape[1]
     return pl.pallas_call(
         merge_kernel,
@@ -167,11 +168,11 @@
             jax.ShapeDtypeStruct((HALF, NGY), F32),
             jax.ShapeDtypeStruct((HALF, NGY), F32),
         ),
-        in_specs=[pl.BlockSpec(memory_space=pltpu.SMEM)] + vmem(4),
+        in_specs=vmem(4),
         out_specs=tuple(vmem(3)),
         cost_estimate=cost(4 * HALF * cols, 4 * HALF * cols * 4),
         name="merge",
-    )(local, z, aux, up, dn)
+    )(z, aux, up, dn)
 
 
 def across_lanes(parts, coef, lo, hi):
@@ -220,55 +221,6 @@
 def left_tile(rc, mid, above, below):
     total = rc[0] * mid + rc[1] * above + rc[2] * below
     return total + rc[3] * pltpu.roll(mid, 1, 0) + rc[4] * pltpu.roll(mid, NGY - 1, 0)
-
-
-def predict_kernel(start, p_ref, rc_ref, cc_ref, proc_ref, o_ref):
-    g = pl.program_id(0)
-    last = pl.num_programs(0) - 1
-    cols = p_ref.shape[1]
-    tiles = cols // NGY
-    here = pl.ds(pl.multiple_of(g * NGY, NGY), NGY)
-    before = pl.ds(pl.multiple_of(jnp.maximum(g - 1, 0) * NGY, NGY), NGY)
-    after = pl.ds(pl.multiple_of(jnp.minimum(g + 1, last) * NGY, NGY), NGY)
-    wide = (NGY, NGY)
-    rc = [jnp.broadcast_to(rc_ref[:, k : k + 1], wide) for k in range(5)]
-    rc[1] = jnp.where(g == 0, 0.0, rc[1])
-    rc[2] = jnp.where(g == last, 0.0, rc[2])
-    parts = [None]
-    for t in range(tiles + 1):
-        if t < tiles:
-            lanes = slice(t * NGY, (t + 1) * NGY)
-            parts.append(left_tile(rc, p_ref[here, lanes], p_ref[before, lanes], p_ref[after, lanes]))
-        else:
-            parts.append(None)
-        if t >= 1:
-            o_ref[:, (t - 1) * NGY : t * NGY] = across_lanes(parts, cc_ref[...], t - 1, t)[0]
-    hit = start[0] + g
-    eye = lax.broadcasted_iota(jnp.int32, wide, 0) == lax.broadcasted_iota(jnp.int32, wide, 1)
-    for t in range(tiles):
-
-        @pl.when(hit == t)
-        def _():
-            lanes = slice(t * NGY, (t + 1) * NGY)
-            o_ref[:, lanes] = o_ref[:, lanes] + jnp.where(eye, proc_ref[:, lanes], 0.0)
-
-
-def predict(start, block, row_coef, col_coef, proc):
-    rows, cols = block.shape
-    steps = rows // NGY
-    return pl.pallas_call(
-        predict_kernel,
-        out_shape=jax.ShapeDtypeStruct((rows, cols), F32),
-        grid_spec=pltpu.PrefetchScalarGridSpec(
-            num_scalar_prefetch=1,
-            grid=(steps,),
-            in_specs=vmem(1) + [pl.BlockSpec((NGY, 8), lambda g, s: (g, 0))] + vmem(2),
-            out_specs=pl.BlockSpec((NGY, cols), lambda g, s: (g, 0)),
-        ),
-        compiler_params=pltpu.CompilerParams(vmem_limit_bytes=24 << 20),
-        cost_estimate=cost(22 * rows * cols, 8 * rows * cols),
-        name="predict",
-    )(start, block, row_coef, col_coef, proc)
 
 
 BLK = 128
@@ -381,7 +333,7 @@
         in_specs=vmem(5),
         out_specs=vmem(1)[0],
         scratch_shapes=[pltpu.VMEM((M, M), F32)],
-        compiler_params=pltpu.CompilerParams(vmem_limit_bytes=24 << 20),
+        compiler_params=pltpu.CompilerParams(vmem_limit_bytes=10 << 20),
         cost_estimate=cost(2 * 1153000000 * 8, 4 << 20),
         name="inverse",
     )(own, other, rslot, cslot, noise)
@@ -418,7 +370,7 @@
         out_shape=jax.ShapeDtypeStruct((M, cols), F32),
         in_specs=vmem(1 + len(parts)),
         out_specs=vmem(1)[0],
-        compiler_params=pltpu.CompilerParams(vmem_limit_bytes=24 << 20),
+        compiler_params=pltpu.CompilerParams(vmem_limit_bytes=14 << 20),
         cost_estimate=cost(6 * M * SLOTS * cols, 3 * SLOTS * cols * 4),
         name="across",
     )(slot, *parts)
@@ -438,20 +390,23 @@
         out_shape=(jax.ShapeDtypeStruct((size, M), BF16), jax.ShapeDtypeStruct((size, M), BF16)),
         in_specs=vmem(1 + len(parts)),
         out_specs=tuple(vmem(2)),
-        compiler_params=pltpu.CompilerParams(vmem_limit_bytes=24 << 20),
+        compiler_params=pltpu.CompilerParams(vmem_limit_bytes=14 << 20),
         cost_estimate=cost(4 * M * SLOTS * size, 2 * SLOTS * size * 4),
         name="strip",
     )(slot, *parts)
 
 
 def update_kernel(
-    core, pred_ref, inv_ref, xc_ref, rc_ref, cc_ref, up_ref, dn_ref, el_ref, er_ref,
-    oh_ref, ol_ref, ph_ref, pl_ref, o_ref, uh, ul,
+    place, p_ref, proc_ref, inv_ref, xc_ref, rc_ref, cc_ref, up_ref, dn_ref, el_ref, er_ref,
+    oh_ref, ol_ref, ph_ref, pl_ref, o_ref, uh, ul, sh, sl,
 ):
     h, j = pl.program_id(0), pl.program_id(1)
     steps = pl.num_programs(1)
-    g = (h ^ core[0]) * steps + j
-    last = 2 * steps - 1
+    g = (h ^ place[0]) * steps + j
+    final = 2 * steps - 1
+    size, cols = o_ref.shape
+    tiles, many = cols // NGY, size // NGY
+    last = 2 * steps * many - 1
 
     @pl.when((h == 0) & (j == 0))
     def _():
@@ -459,53 +414,80 @@
         uh[...] = high
         ul[...] = low
 
-    size, cols = o_ref.shape
     rows = pl.ds(pl.multiple_of(j * size, size), size)
     for half, (hi_ref, lo_ref) in enumerate(((oh_ref, ol_ref), (ph_ref, pl_ref))):
 
         @pl.when(h == half)
         def _():
-            a, b = hi_ref[rows, :], lo_ref[rows, :]
-            o_ref[...] = pred_ref[...] - (bdot(a, uh[...]) + (bdot(a, ul[...]) + bdot(b, uh[...])))
-
-    rc = [jnp.broadcast_to(rc_ref[:, k : k + 1], (NGY, NGY)) for k in range(5)]
-    above = pl.ds(pl.multiple_of(g * NGY, NGY), NGY)
-    here = pl.ds(pl.multiple_of(g * NGY + NGY, NGY), NGY)
-    below = pl.ds(pl.multiple_of(g * NGY + 2 * NGY, NGY), NGY)
-    for ref, lo, k in ((el_ref, 0, 1), (er_ref, cols - NGY, 2)):
-        rim = left_tile(rc, ref[here, :], ref[above, :], ref[below, :])
-        lanes = slice(lo, lo + NGY)
-        o_ref[:, lanes] = o_ref[:, lanes] + cc_ref[k : k + 1, lanes] * rim
-    for at, ref, k in ((0, up_ref, 1), (last, dn_ref, 2)):
+            sh[...] = hi_ref[rows, :]
+            sl[...] = lo_ref[rows, :]
+
+    less = bdot(sh[...], uh[...]) + (bdot(sh[...], ul[...]) + bdot(sl[...], uh[...]))
+    wide = (NGY, NGY)
+    eye = lax.broadcasted_iota(jnp.int32, wide, 0) == lax.broadcasted_iota(jnp.int32, wide, 1)
+    for n in range(many):
+        k = g * many + n
+        some = slice(n * NGY, (n + 1) * NGY)
+        rc = [jnp.broadcast_to(rc_ref[some, i : i + 1], wide) for i in range(5)]
+        inner = [rc[0], jnp.where(k == 0, 0.0, rc[1]), jnp.where(k == last, 0.0, rc[2]), rc[3], rc[4]]
+        a, b, d = (pl.ds(pl.multiple_of((k + i) * NGY, NGY), NGY) for i in range(3))
+        here = pl.ds(pl.multiple_of(k * NGY, NGY), NGY)
+        above = pl.ds(pl.multiple_of(jnp.maximum(k - 1, 0) * NGY, NGY), NGY)
+        below = pl.ds(pl.multiple_of(jnp.minimum(k + 1, last) * NGY, NGY), NGY)
+        parts = [left_tile(rc, el_ref[b, :], el_ref[a, :], el_ref[d, :])]
+        for t in range(tiles + 1):
+            lanes = slice(t * NGY, (t + 1) * NGY)
+            if t < tiles:
+                parts.append(left_tile(inner, p_ref[here, lanes], p_ref[above, lanes], p_ref[below, lanes]))
+            else:
+                parts.append(left_tile(rc, er_ref[b, :], er_ref[a, :], er_ref[d, :]))
+            if t >= 1:
+                lanes = slice((t - 1) * NGY, t * NGY)
+                o_ref[some, lanes] = across_lanes(parts, cc_ref[...], t - 1, t)[0] - less[some, lanes]
+        hit = place[1] + k
+
+        @pl.when((hit >= 0) & (hit < tiles))
+        def _():
+            lanes = pl.ds(pl.multiple_of(hit * NGY, NGY), NGY)
+            o_ref[some, lanes] = o_ref[some, lanes] + jnp.where(eye, proc_ref[:, lanes], 0.0)
+
+    for at, n, ref, k in ((0, 0, up_ref, 1), (final, many - 1, dn_ref, 2)):
 
         @pl.when(g == at)
         def _():
-            tiles = cols // NGY
-            parts = [None] + [rc[k] * ref[:, t * NGY : (t + 1) * NGY] for t in range(tiles)] + [None]
+            some = slice(n * NGY, (n + 1) * NGY)
+            scale = jnp.broadcast_to(rc_ref[some, k : k + 1], wide)
+            parts = [None] + [scale * ref[:, t * NGY : (t + 1) * NGY] for t in range(tiles)] + [None]
             rim = across_lanes(parts, cc_ref[...], 0, tiles)
-            o_ref[...] = o_ref[...] + jnp.concatenate(rim, axis=1)
-
-
-def update(core, pred, inv, xc, row_coef, col_coef, rims, own, other):
-    rows, cols = pred.shape
+            o_ref[some, :] = o_ref[some, :] + jnp.concatenate(rim, axis=1)
+
+
+def update(place, block, proc, inv, xc, row_coef, col_coef, rims, own, other):
+    rows, cols = block.shape
     half = rows // 2
-    steps = half // NGY
-    tile = pl.BlockSpec((NGY, cols), lambda h, j, k: ((h ^ k[0]) * steps + j, 0))
-    few = pl.BlockSpec((NGY, 8), lambda h, j, k: ((h ^ k[0]) * steps + j, 0))
+    size = 2 * NGY
+    steps = half // size
+    tile = pl.BlockSpec((size, cols), lambda h, j, k: ((h ^ k[0]) * steps + j, 0))
+    few = pl.BlockSpec((size, 8), lambda h, j, k: ((h ^ k[0]) * steps + j, 0))
     return pl.pallas_call(
         update_kernel,
         out_shape=jax.ShapeDtypeStruct((rows, cols), F32),
         grid_spec=pltpu.PrefetchScalarGridSpec(
             num_scalar_prefetch=1,
             grid=(2, steps),
-            in_specs=[tile] + vmem(2) + [few] + vmem(9),
+            in_specs=vmem(4) + [few] + vmem(9),
             out_specs=tile,
-            scratch_shapes=[pltpu.VMEM((M, cols), BF16), pltpu.VMEM((M, cols), BF16)],
+            scratch_shapes=[
+                pltpu.VMEM((M, cols), BF16),
+                pltpu.VMEM((M, cols), BF16),
+                pltpu.VMEM((size, M), BF16),
+                pltpu.VMEM((size, M), BF16),
+            ],
         ),
-        compiler_params=pltpu.CompilerParams(vmem_limit_bytes=32 << 20),
+        compiler_params=pltpu.CompilerParams(vmem_limit_bytes=30 << 20),
         cost_estimate=cost(6 * rows * cols * M, 8 * rows * cols),
         name="update",
-    )(core, pred, inv, xc, row_coef, col_coef, *rims, *own, *other)
+    )(place, block, proc, inv, xc, row_coef, col_coef, *rims, *own, *other)
 
 
 def shift(x, axis, count, back):
@@ -514,14 +496,6 @@
 
 def flip(x, axis, count, bit):
     return lax.ppermute(x, axis, [(i, i ^ bit) for i in range(count)])
-
-
-def ring(x, axis, count, near, step):
-    pair = jnp.stack([x, flip(x, axis, count, near)])
-    more = shift(pair, axis, count, step)
-    less = shift(pair, axis, count, count - step)
-    far = shift(more[0], axis, count, step), shift(less[1], axis, count, count - step)
-    return pair, more, far, less
 
 
 def after(x, *others):
@@ -536,14 +510,16 @@
     row_start, col_start = r * rows, c * cols
     block = covariance
 
-    up = shift(block[rows - NGY :], "row", ROWS, ROWS - 1)
-    z, send_dn, aux, target, local = well_rows(
+    z, send_up, send_dn, aux, target, top, low, left, right = tables(
         jnp.stack([r, c]), wells, center, links, process, block
     )
+    got_up = shift(send_up, "row", ROWS, ROWS - 1)
     got_dn = shift(send_dn, "row", ROWS, 1)
-    z, left, right = merge(local, z, aux, up, got_dn)
-    zl = shift(right, "col", COLS, COLS - 1)
-    zr = shift(left, "col", COLS, 1)
+    up = shift(low, "row", ROWS, ROWS - 1)
+    z, to_left, to_right = merge(z, aux, got_up, got_dn)
+    dn = shift(after(top, z), "row", ROWS, 1)
+    zl = shift(to_right, "col", COLS, COLS - 1)
+    zr = shift(to_left, "col", COLS, 1)
 
     cell = jnp.arange(cells, dtype=jnp.int32)
     gx, gy = cell // NGY, cell % NGY
@@ -560,38 +536,48 @@
     coef = after(coef, send_dn)
     col_coef = lax.dynamic_slice_in_dim(coef, col_start, cols, 1)
     row_part = lax.dynamic_slice_in_dim(coef, row_start, rows, 1)
+    start = ((row_start - col_start) // NGY)[None]
+    row_coef = jnp.concatenate([row_part, jnp.zeros((2, rows), F32)]).T
     x, g = well_cols(z, zl, zr, col_coef[:5], aux, target)
 
+    turn = []
+    for z_at in range(4):
+        for y in range(2):
+            for q in range(ROWS):
+                for k in range(2):
+                    to = (((z_at + q // 2) % 4) * 2 + y) * 2 + k
+                    turn.append(((z_at * 2 + y) * COLS + 2 * q + k, q * COLS + to))
+    first = lax.ppermute(x, ("row", "col"), turn)
+    mate = flip(x, "row", ROWS, 1)
+    second = lax.ppermute(mate, ("row", "col"), turn)
+
     g = g + shift(g, "col", COLS, 4) + shift(g, "col", COLS, 8) + shift(g, "col", COLS, 12)
+    g = after(g, mate, first, dn)
     g = jnp.stack([g, flip(g, "col", COLS, 2)])
     g = jnp.stack([g, flip(g, "row", ROWS, 1)])
+    gated = g
     g = jnp.stack([g] + [shift(g, "row", ROWS, 2 * d) for d in range(1, 4)])
     g = g.reshape(ROWS, 2, HALF, NGY)
     g_other = flip(g, "col", COLS, 1)
 
-    turn = [
-        (a * COLS + 2 * b + k, b * COLS + 2 * a + k)
-        for a in range(ROWS)
-        for b in range(ROWS)
-        for k in range(2)
-    ]
-    turned = lax.ppermute(x, ("row", "col"), turn)
-    pair, more, far, less = ring(x, "row", ROWS, 1, 2)
-    x_parts = [pair, more, *far, less]
-    pair, more, far, less = ring(turned, "col", COLS, 2, 4)
+    pair = after(jnp.stack([x, mate]), g)
+    more = shift(pair, "row", ROWS, 2)
+    less = shift(pair, "row", ROWS, ROWS - 2)
+    x_parts = [pair, more, shift(more[0], "row", ROWS, 2), shift(less[1], "row", ROWS, ROWS - 2), less]
+    pair = jnp.stack([first, second])
+    more = shift(pair, "col", COLS, 4)
+    less = shift(pair, "col", COLS, COLS - 4)
+    far = shift(more[0], "col", COLS, 4), shift(less[1], "col", COLS, COLS - 4)
     own = [pair, more, *far, less]
-    far = jnp.stack(far)
-    other = [flip(a, "col", COLS, 1) for a in (pair, more, far, less)]
-
-    dn = shift(after(block[:NGY], x), "row", ROWS, 1)
-    right = jnp.concatenate([a[:, cols - NGY :] for a in (up, block, dn)])
-    left = jnp.concatenate([a[:, :NGY] for a in (up, block, dn)])
-    el = shift(after(right, turned), "col", COLS, COLS - 1)
-    er = shift(after(left, turned), "col", COLS, 1)
-
-    start = ((row_start - col_start) // NGY)[None]
-    row_coef = jnp.concatenate([after(row_part, x), jnp.zeros((2, rows), F32)]).T
-    pred = predict(start, block, row_coef, col_coef[:5], col_coef[5:6])
+    other = [flip(a, "col", COLS, 1) for a in (pair, jnp.stack([more, less]), jnp.stack(far))]
+    other = [other[0], other[1][0], other[2], other[1][1]]
+
+    def cornered(edge, lanes):
+        edge = lax.dynamic_update_slice(edge, up[:, lanes], (0, 0))
+        return lax.dynamic_update_slice(edge, dn[:, lanes], (rows + NGY, 0))
+
+    el = shift(after(cornered(right, slice(cols - NGY, cols)), gated), "col", COLS, COLS - 1)
+    er = shift(after(cornered(left, slice(0, NGY)), gated), "col", COLS, 1)
 
     w = after(wells, z)[0]
     part = w // cols
@@ -601,7 +587,8 @@
     wr, wc = part // 2, part
     in_row = (wc % 2) * WMAX + rank
     row_slot = ((wr // 2 - r // 2) % 4 * 2 + (wr % 2 ^ r % 2)) * HALF + in_row
-    strip_slot = ((wr // 2 - c // 4) % 4 * 2 + (wr % 2 ^ (c // 2) % 2)) * HALF + in_row
+    gram_slot = ((wr // 2 - r // 2) % 4 * 2 + (wr % 2 ^ r % 2)) * HALF + in_row
+    strip_slot = ((wr // 2 + r // 2 - c // 4) % 4 * 2 + (wr % 2 ^ (c // 2) % 2)) * HALF + in_row
     col_slot = (
         (wc % 2 ^ c % 2) * (2 * NGY)
         + ((wc // 2) % 2 ^ (c // 2) % 2) * NGY
@@ -611,9 +598,10 @@
     xc = across(row_slot[:, None], x_parts)
     own = strip(strip_slot[None], own)
     other = strip(strip_slot[None], other)
-    inv = inverse(g, g_other, row_slot[:, None], col_slot[None], noise)
+    inv = inverse(g, g_other, gram_slot[:, None], col_slot[None], noise)
     rims = (up, dn, el, er)
-    return update((c % 2)[None], pred, inv, xc, row_coef, col_coef[:5], rims, own, other)
+    scalars = jnp.stack([c % 2, start[0]])
+    return update(scalars, block, col_coef[5:6], inv, xc, row_coef, col_coef[:5], rims, own, other)
 
 
 def solution(mesh):

time: 179 us -> 146 us (0.82); the launches traced: 176 us -> 145 us
  local copies, waits for them, and re-layouts: 18.2 us -> 3.48 us
  waiting for transfers between devices: 46.1 us -> 33.2 us
  Pallas kernels: 54.7 us -> 49.3 us
  starting transfers between devices: 52.7 us -> 54.6 us
    ppermute x21 -> x22, waiting for transfers between devices: 35.6 us -> 18.3 us  [shift(): lax.ppermute(x, axis, [((i + back) % count, i) for i in range(count)])]
    unnamed x56 -> x32, local copies, waits for them, and re-layouts: 11.6 us -> 1.32 us
    pallas_call x2 -> x1, Pallas kernels: 15.6 us -> 9.13 us  [tables(): pl.pallas_call(table_kernel, out_shape=(jax.ShapeDtypeStruct((HALF, cols)...]
    ppermute x21 -> x22, starting transfers between devices: 37.9 us -> 32.3 us  [shift(): lax.ppermute(x, axis, [((i + back) % count, i) for i in range(count)])]
    ppermute x1 -> x2, starting transfers between devices: 1.91 us -> 6.63 us  [the longest x1 3.52 us: shards(): first = lax.ppermute(x, ('row', 'col'), turn)]
    slice x5 -> x1, local copies, waits for them, and re-layouts: 3.23 us -> 0.08 us  [shards(): col_coef[5:6]]
    ppermute x9 -> x7, starting transfers between devices: 12.9 us -> 15.7 us  [flip(): return lax.ppermute(x, axis, [(i, i ^ bit) for i in range(count)])]
    ppermute x9 -> x7, waiting for transfers between devices: 1.54 us -> 4.24 us  [flip(): return lax.ppermute(x, axis, [(i, i ^ bit) for i in range(count)])]
  transfers between devices with their start and end apart: 31 -> 31, of which waited for: 10 -> 10; matrix products, arithmetic and copies ran while one was open for 6% -> 4% of each run, Pallas kernels for 17% -> 16%
where the time goes in v3:
time: 146 us; the launch traced here: 145 us
  starting transfers between devices  54.6 us (37%)
  Pallas kernels  49.3 us (34%)
  waiting for transfers between devices  33.2 us (23%)
  other arithmetic  3.8 us (3%)
  local copies, waits for them, and re-layouts  3.48 us (2%)
    ppermute x22, starting transfers between devices, shift(): lax.ppermute(x, axis, [((i + back) % count, i) for i in range(count)])  32.3 us
    pallas_call x1, Pallas kernels, inverse(): pl.pallas_call(inverse_kernel, out_shape=jax.ShapeDtypeStruct((M, M), F32...  18.9 us
    ppermute x22, waiting for transfers between devices, shift(): lax.ppermute(x, axis, [((i + back) % count, i) for i in range(count)])  18.3 us
    ppermute x7, starting transfers between devices, flip(): return lax.ppermute(x, axis, [(i, i ^ bit) for i in range(count)])  15.7 us
    pallas_call x1, Pallas kernels, update(): pl.pallas_call(update_kernel, out_shape=jax.ShapeDtypeStruct((rows, cols)...  14.5 us
    ppermute x1, waiting for transfers between devices, shards(): first = lax.ppermute(x, ('row', 'col'), turn)  10.7 us
    pallas_call x1, Pallas kernels, tables(): pl.pallas_call(table_kernel, out_shape=(jax.ShapeDtypeStruct((HALF, cols)...  9.13 us
    ppermute x7, waiting for transfers between devices, flip(): return lax.ppermute(x, axis, [(i, i ^ bit) for i in range(count)])  4.24 us
  transfers between devices with their start and end apart: 31, of which 10 were waited for; matrix products, arithmetic and copies ran while one was open for 4% of the time, Pallas kernels for 16%

profile of v3, /device:TPU:3, one launch (start us, length us, event | category | flops | bytes accessed | tf_op | source)
XLA Modules:
  0.0 144.9 jit_solution(12581778601123078507)
XLA Ops:
  0.6 9.1 %tables.1 = (f32[64,1024]{1,0:T(8,128)}, f32[32,1024]{1,0:T(8,128)}, f32[32,1024]{1,0:T(8,128)}, f32[64,128]{1,0:T(8,128)}, s32[1,128]{1,0:T(1,128)}, /*index=5*...) custom-call(s32[2]{0:T(128)} %pad_add_fusion.1.place, s32[1,256]{1,0:T(1,128)} %wells.1, ...), custom_call_target="tpu_custom_call" | custom-call | flops 1048576 | bytes 2097152 | tf_op jit(solution)/shard_map/tables/pallas_call | solution.py:123
  11.1 3.6 %collective-permute-start.1 = (f32[32,1024]{1,0:T(8,128)}, f32[32,1024]{1,0:T(8,128)S(1)}, u32[]{:S(2)}, u32[]{:S(2)}) collective-permute-start(f32[32,1024]{1,0:T(8,128)} %get-tuple-element.30), channel_id=1, source_target_pairs={{16,0},{32,16},{48,32},{64,48},{80,64},{96,80},{112,96},{0,112},{1... | collective-permute-start | bytes 393224 | tf_op jit(solution)/shard_map/ppermute | solution.py:494
  21.2 4.4 %collective-permute-start.2 = (f32[64,128]{1,0:T(8,128)}, f32[64,128]{1,0:T(8,128)S(1)}, u32[]{:S(2)}, u32[]{:S(2)}) collective-permute-start(f32[64,128]{1,0:T(8,128)} %get-tuple-element.36), channel_id=1, source_target_pairs={{15,0},{0,1},{1,2},{2,3},{3,4},{4,5},{5,6},{6,7},{7,8},{8,9},{9,10... | collective-permute-start | bytes 98312 | tf_op jit(solution)/shard_map/ppermute | solution.py:494
  28.4 2.2 %collective-permute-done.3.zr_ref = f32[64,128]{1,0:T(8,128)S(1)} collective-permute-done((f32[64,128]{1,0:T(8,128)}, f32[64,128]{1,0:T(8,128)S(1)}, u32[]{:S(2)}, u32[]{:S(2)}) %collective-permute-start.3) | collective-permute-done | bytes 32800 | tf_op jit(solution)/shard_map/ppermute | solution.py:494
  31.2 2.2 %well_cols.1 = (f32[64,1024]{1,0:T(8,128)}, f32[64,128]{1,0:T(8,128)}) custom-call(f32[64,1024]{1,0:T(8,128)} %get-tuple-element.35.z_ref, f32[64,128]{1,0:T(8,128)} %copy-done.8, f32[64,128]{1,0:T(8,128)} %copy-done.9, f32[5,1024]{1,0:T(8,128)} %constant_dynamic-slice_fusion.1.coef_ref.cc_ref, f32[64,128]{1,0:T(8,128)} %get-tuple-element.33.aux_ref, ...), custom_call_target="tpu_custom_call" | custom-call | flops 100663296 | bytes 1048576 | tf_op jit(solution)/shard_map/well_cols/pallas_call | solution.py:208
  38.3 3.5 %collective-permute-start.8 = (f32[64,1024]{1,0:T(8,128)}, f32[64,1024]{1,0:T(8,128)S(1)}, u32[]{:S(2)}, u32[]{:S(2)}) collective-permute-start(f32[64,1024]{1,0:T(8,128)} %get-tuple-element.40), channel_id=1, source_target_pairs={{0,0},{1,1},{2,16},{3,17},{4,36},{5,37},{6,52},{7,53},{8,72},{9,73... | collective-permute-start | bytes 786440 | tf_op jit(solution)/shard_map/ppermute | solution.py:550
  41.9 2.7 %collective-permute-start.20 = (f32[128,1024]{1,0:T(8,128)S(1)}, f32[128,1024]{1,0:T(8,128)S(1)}, u32[]{:S(2)}, u32[]{:S(2)}) collective-permute-start(f32[128,1024]{1,0:T(8,128)S(1)} %copy-done.12), channel_id=1, source_target_pairs={{112,0},{0,16},{16,32},{32,48},{48,64},{64,80},{80,96},{96,112},{1... | collective-permute-start | bytes 1572872 | tf_op jit(solution)/shard_map/ppermute | solution.py:494
  44.6 3.1 %collective-permute-start.23 = (f32[64,1024]{1,0:T(8,128)S(1)}, f32[64,1024]{1,0:T(8,128)S(1)}, u32[]{:S(2)}, u32[]{:S(2)}) collective-permute-start(f32[64,1024]{1,0:T(8,128)S(1)} %collective-permute-done.7), channel_id=1, source_target_pairs={{0,0},{1,1},{2,16},{3,17},{4,36},{5,37},{6,52},{7,53},{8,72},{9,73... | collective-permute-start | bytes 786440 | tf_op jit(solution)/shard_map/ppermute | solution.py:552
  48.5 10.7 %collective-permute-done.8 = f32[64,1024]{1,0:T(8,128)S(1)} collective-permute-done((f32[64,1024]{1,0:T(8,128)}, f32[64,1024]{1,0:T(8,128)S(1)}, u32[]{:S(2)}, u32[]{:S(2)}) %collective-permute-start.8) | collective-permute-done | bytes 262176 | tf_op jit(solution)/shard_map/ppermute | solution.py:550
  60.3 3.1 %collective-permute-done.10 = f32[64,128]{1,0:T(8,128)S(1)} collective-permute-done((f32[64,128]{1,0:T(8,128)S(1)}, f32[64,128]{1,0:T(8,128)S(1)}, u32[]{:S(2)}, u32[]{:S(2)}) %collective-permute-start.10) | collective-permute-done | bytes 32800 | tf_op jit(solution)/shard_map/ppermute | solution.py:498
  63.5 5.6 %collective-permute-start.11 = (f32[2,64,128]{2,1,0:T(8,128)S(1)}, f32[2,64,128]{2,1,0:T(8,128)S(1)}, u32[]{:S(2)}, u32[]{:S(2)}) collective-permute-start(f32[2,64,128]{2,1,0:T(8,128)S(1)} %get-tuple-element.70), channel_id=1, source_target_pairs={{0,16},{16,0},{32,48},{48,32},{64,80},{80,64},{96,112},{112,96},{1... | collective-permute-start | bytes 196616 | tf_op jit(solution)/shard_map/ppermute | solution.py:498
  71.4 4.1 %collective-permute-start.13 = (f32[2,2,64,128]{3,2,1,0:T(8,128)S(1)}, f32[2,2,64,128]{3,2,1,0:T(8,128)S(1)}, u32[]{:S(2)}, u32[]{:S(2)}) collective-permute-start(f32[2,2,64,128]{3,2,1,0:T(8,128)S(1)} %get-tuple-element.68), channel_id=1, source_target_pairs={{64,0},{80,16},{96,32},{112,48},{0,64},{16,80},{32,96},{48,112},{6... | collective-permute-start | bytes 393224 | tf_op jit(solution)/shard_map/ppermute | solution.py:494
  75.6 2.0 %collective-permute-start.12 = (f32[2,2,64,128]{3,2,1,0:T(8,128)S(1)}, f32[2,2,64,128]{3,2,1,0:T(8,128)S(1)}, u32[]{:S(2)}, u32[]{:S(2)}) collective-permute-start(f32[2,2,64,128]{3,2,1,0:T(8,128)S(1)} %get-tuple-element.68), channel_id=1, source_target_pairs={{32,0},{48,16},{64,32},{80,48},{96,64},{112,80},{0,96},{16,112},{3... | collective-permute-start | bytes 393224 | tf_op jit(solution)/shard_map/ppermute | solution.py:494
  77.7 3.5 %collective-permute-done.13 = f32[2,2,64,128]{3,2,1,0:T(8,128)S(1)} collective-permute-done((f32[2,2,64,128]{3,2,1,0:T(8,128)S(1)}, f32[2,2,64,128]{3,2,1,0:T(8,128)S(1)}, u32[]{:S(2)}, u32[]{:S(2)}) %collective-permute-start.13) | collective-permute-done | bytes 131104 | tf_op jit(solution)/shard_map/ppermute | solution.py:494
  81.3 2.7 %collective-permute-start.16 = (f32[2,64,1024]{2,1,0:T(8,128)S(1)}, f32[2,64,1024]{2,1,0:T(8,128)S(1)}, u32[]{:S(2)}, u32[]{:S(2)}) collective-permute-start(f32[2,64,1024]{2,1,0:T(8,128)S(1)} %pad_maximum_fusion.2.refs_0_), channel_id=1, source_target_pairs={{32,0},{48,16},{64,32},{80,48},{96,64},{112,80},{0,96},{16,112},{3... | collective-permute-start | bytes 1572872 | tf_op jit(solution)/shard_map/ppermute | solution.py:494
  84.1 2.1 %collective-permute-start.15 = (f32[8,2,64,128]{3,2,1,0:T(8,128)S(1)}, f32[8,2,64,128]{3,2,1,0:T(8,128)S(1)}, u32[]{:S(2)}, u32[]{:S(2)}) collective-permute-start(f32[8,2,64,128]{3,2,1,0:T(8,128)S(1)} %bitcast.50), channel_id=1, source_target_pairs={{0,1},{1,0},{2,3},{3,2},{4,5},{5,4},{6,7},{7,6},{8,9},{9,8},{10,11... | collective-permute-start | bytes 1572872 | tf_op jit(solution)/shard_map/ppermute | solution.py:498
  86.6 2.7 %collective-permute-done.24.refs_1_ = f32[2,64,1024]{2,1,0:T(8,128)S(1)} collective-permute-done((f32[2,64,1024]{2,1,0:T(8,128)S(1)}, f32[2,64,1024]{2,1,0:T(8,128)S(1)}, u32[]{:S(2)}, u32[]{:S(2)}) %collective-permute-start.24) | collective-permute-done | bytes 524320 | tf_op jit(solution)/shard_map/ppermute | solution.py:494
  89.6 4.7 %collective-permute-done.18.refs_4_ = f32[2,64,1024]{2,1,0:T(8,128)S(1)} collective-permute-done((f32[2,64,1024]{2,1,0:T(8,128)S(1)}, f32[2,64,1024]{2,1,0:T(8,128)S(1)}, u32[]{:S(2)}, u32[]{:S(2)}) %collective-permute-start.18) | collective-permute-done | bytes 524320 | tf_op jit(solution)/shard_map/ppermute | solution.py:494
  94.5 2.7 %collective-permute-start.17 = (f32[64,1024]{1,0:T(8,128)S(1)}, f32[64,1024]{1,0:T(8,128)S(1)}, u32[]{:S(2)}, u32[]{:S(2)}) collective-permute-start(f32[64,1024]{1,0:T(8,128)S(1)} %slice_bitcast_fusion.5), channel_id=1, source_target_pairs={{32,0},{48,16},{64,32},{80,48},{96,64},{112,80},{0,96},{16,112},{3... | collective-permute-start | bytes 786440 | tf_op jit(solution)/shard_map/ppermute | solution.py:494
  97.3 3.1 %collective-permute-start.28 = (f32[2,64,1024]{2,1,0:T(8,128)S(1)}, f32[2,64,1024]{2,1,0:T(8,128)S(1)}, u32[]{:S(2)}, u32[]{:S(2)}) collective-permute-start(f32[2,64,1024]{2,1,0:T(8,128)S(1)} %pad_maximum_fusion.3.refs_0_), channel_id=1, source_target_pairs={{0,1},{1,0},{2,3},{3,2},{4,5},{5,4},{6,7},{7,6},{8,9},{9,8},{10,11... | collective-permute-start | bytes 1572872 | tf_op jit(solution)/shard_map/ppermute | solution.py:498
  101.1 3.7 %collective-permute-start.29 = (f32[2,2,64,1024]{3,2,1,0:T(8,128)S(1)}, f32[2,2,64,1024]{3,2,1,0:T(8,128)S(1)}, u32[]{:S(2)}, u32[]{:S(2)}) collective-permute-start(f32[2,2,64,1024]{3,2,1,0:T(8,128)S(1)} %pad_maximum_fusion), channel_id=1, source_target_pairs={{0,1},{1,0},{2,3},{3,2},{4,5},{5,4},{6,7},{7,6},{8,9},{9,8},{10,11... | collective-permute-start | bytes 3145736 | tf_op jit(solution)/shard_map/ppermute | solution.py:498
  105.1 18.9 %inverse.1.inv_ref = f32[256,256]{1,0:T(8,128)S(1)} custom-call(f32[8,2,64,128]{3,2,1,0:T(8,128)S(1)} %bitcast.51, f32[8,2,64,128]{3,2,1,0:T(8,128)S(1)} %collective-permute-done.15.other_ref, s32[256,1]{1,0:T(8,128)S(1)} %fusion.7.rslot_ref.slot_ref, s32[1,256]{1,0:T(1,128)S(1)} %add_add_fusion.2.cslot_ref, f32[1,256]{1,0:T(1,128)S(1)} %copy-done.1), custom_call_target="tpu_custom_call" | custom-call | flops 18447998976 | bytes 4194304 | tf_op jit(solution)/shard_map/inverse/pallas_call | solution.py:330
  126.9 3.4 %collective-permute-done.22.er_ref = f32[2304,128]{1,0:T(8,128)S(1)} collective-permute-done((f32[2304,128]{1,0:T(8,128)S(1)}, f32[2304,128]{1,0:T(8,128)S(1)}, u32[]{:S(2)}, u32[]{:S(2)}) %collective-permute-start.22) | collective-permute-done | bytes 1179680 | tf_op jit(solution)/shard_map/ppermute | solution.py:494
  130.4 14.5 %update.1 = f32[2048,1024]{1,0:T(8,128)} custom-call(s32[2]{0:T(128)S(1)} %pad_add_fusion.place, f32[2048,1024]{1,0:T(8,128)S(1)} %bitcast.45, f32[1,1024]{1,0:T(1,128)S(1)} %dynamic-slice.proc_ref, f32[256,256]{1,0:T(8,128)S(1)} %inverse.1.inv_ref, f32[256,1024]{1,0:T(8,128)S(1)} %across.1.xc_ref, f32[2048,8]{1,0:T(8,128)S(1)} %copy.19.rc_ref, ...), custom_call_target="tpu_custom_call" | custom-call | flops 3221225472 | bytes 16777216 | tf_op jit(solution)/shard_map/update/pallas_call | solution.py:472
  (111 shorter events, 25.9 us)
Async XLA Ops:
  9.8 8.3 %collective-permute-start = (f32[32,1024]{1,0:T(8,128)}, f32[32,1024]{1,0:T(8,128)S(1)}, u32[]{:S(2)}, u32[]{:S(2)}) collective-permute-start(f32[32,1024]{1,0:T(8,128)} %get-tuple-element.34), channel_id=1, source_target_pairs={{112,0},{0,16},{16,32},{32,48},{48,64},{64,80},{80,96},{96,112},{1... | collective-permute-start | bytes 393224 | tf_op jit(solution)/shard_map/ppermute | solution.py:494
  11.1 7.4 %collective-permute-start.1 = (f32[32,1024]{1,0:T(8,128)}, f32[32,1024]{1,0:T(8,128)S(1)}, u32[]{:S(2)}, u32[]{:S(2)}) collective-permute-start(f32[32,1024]{1,0:T(8,128)} %get-tuple-element.30), channel_id=1, source_target_pairs={{16,0},{32,16},{48,32},{64,48},{80,64},{96,80},{112,96},{0,112},{1... | collective-permute-start | bytes 393224 | tf_op jit(solution)/shard_map/ppermute | solution.py:494
  21.2 7.3 %collective-permute-start.2 = (f32[64,128]{1,0:T(8,128)}, f32[64,128]{1,0:T(8,128)S(1)}, u32[]{:S(2)}, u32[]{:S(2)}) collective-permute-start(f32[64,128]{1,0:T(8,128)} %get-tuple-element.36), channel_id=1, source_target_pairs={{15,0},{0,1},{1,2},{2,3},{3,4},{4,5},{5,6},{6,7},{7,8},{8,9},{9,10... | collective-permute-start | bytes 98312 | tf_op jit(solution)/shard_map/ppermute | solution.py:494
  26.1 33.1 %collective-permute-start.9 = (f32[128,1024]{1,0:T(8,128)S(1)}, f32[128,1024]{1,0:T(8,128)S(1)}, u32[]{:S(2)}, u32[]{:S(2)}) collective-permute-start(f32[128,1024]{1,0:T(8,128)S(1)} %copy-done.13), channel_id=1, source_target_pairs={{16,0},{32,16},{48,32},{64,48},{80,64},{96,80},{112,96},{0,112},{1... | collective-permute-start | bytes 1572872 | tf_op jit(solution)/shard_map/ppermute | solution.py:494
  34.6 10.0 %collective-permute-start.7 = (f32[64,1024]{1,0:T(8,128)}, f32[64,1024]{1,0:T(8,128)S(1)}, u32[]{:S(2)}, u32[]{:S(2)}) collective-permute-start(f32[64,1024]{1,0:T(8,128)} %get-tuple-element.40), channel_id=1, source_target_pairs={{0,16},{16,0},{32,48},{48,32},{64,80},{80,64},{96,112},{112,96},{1... | collective-permute-start | bytes 786440 | tf_op jit(solution)/shard_map/ppermute | solution.py:498
  36.4 11.4 %collective-permute-start.4 = (f32[64,128]{1,0:T(8,128)}, f32[64,128]{1,0:T(8,128)S(1)}, u32[]{:S(2)}, u32[]{:S(2)}) collective-permute-start(f32[64,128]{1,0:T(8,128)} %get-tuple-element.39), channel_id=1, source_target_pairs={{4,0},{5,1},{6,2},{7,3},{8,4},{9,5},{10,6},{11,7},{12,8},{13,9},{1... | collective-permute-start | bytes 98312 | tf_op jit(solution)/shard_map/ppermute | solution.py:494
  38.3 20.9 %collective-permute-start.8 = (f32[64,1024]{1,0:T(8,128)}, f32[64,1024]{1,0:T(8,128)S(1)}, u32[]{:S(2)}, u32[]{:S(2)}) collective-permute-start(f32[64,1024]{1,0:T(8,128)} %get-tuple-element.40), channel_id=1, source_target_pairs={{0,0},{1,1},{2,16},{3,17},{4,36},{5,37},{6,52},{7,53},{8,72},{9,73... | collective-permute-start | bytes 786440 | tf_op jit(solution)/shard_map/ppermute | solution.py:550
  41.9 35.7 %collective-permute-start.20 = (f32[128,1024]{1,0:T(8,128)S(1)}, f32[128,1024]{1,0:T(8,128)S(1)}, u32[]{:S(2)}, u32[]{:S(2)}) collective-permute-start(f32[128,1024]{1,0:T(8,128)S(1)} %copy-done.12), channel_id=1, source_target_pairs={{112,0},{0,16},{16,32},{32,48},{48,64},{64,80},{80,96},{96,112},{1... | collective-permute-start | bytes 1572872 | tf_op jit(solution)/shard_map/ppermute | solution.py:494
  44.6 24.5 %collective-permute-start.23 = (f32[64,1024]{1,0:T(8,128)S(1)}, f32[64,1024]{1,0:T(8,128)S(1)}, u32[]{:S(2)}, u32[]{:S(2)}) collective-permute-start(f32[64,1024]{1,0:T(8,128)S(1)} %collective-permute-done.7), channel_id=1, source_target_pairs={{0,0},{1,1},{2,16},{3,17},{4,36},{5,37},{6,52},{7,53},{8,72},{9,73... | collective-permute-start | bytes 786440 | tf_op jit(solution)/shard_map/ppermute | solution.py:552
  63.5 7.8 %collective-permute-start.11 = (f32[2,64,128]{2,1,0:T(8,128)S(1)}, f32[2,64,128]{2,1,0:T(8,128)S(1)}, u32[]{:S(2)}, u32[]{:S(2)}) collective-permute-start(f32[2,64,128]{2,1,0:T(8,128)S(1)} %get-tuple-element.70), channel_id=1, source_target_pairs={{0,16},{16,0},{32,48},{48,32},{64,80},{80,64},{96,112},{112,96},{1... | collective-permute-start | bytes 196616 | tf_op jit(solution)/shard_map/ppermute | solution.py:498
  69.2 17.0 %collective-permute-start.26 = (f32[2,64,1024]{2,1,0:T(8,128)S(1)}, f32[2,64,1024]{2,1,0:T(8,128)S(1)}, u32[]{:S(2)}, u32[]{:S(2)}) collective-permute-start(f32[2,64,1024]{2,1,0:T(8,128)S(1)} %pad_maximum_fusion.3.refs_0_), channel_id=1, source_target_pairs={{12,0},{13,1},{14,2},{15,3},{0,4},{1,5},{2,6},{3,7},{4,8},{5,9},{6... | collective-permute-start | bytes 1572872 | tf_op jit(solution)/shard_map/ppermute | solution.py:494
  71.4 9.8 %collective-permute-start.13 = (f32[2,2,64,128]{3,2,1,0:T(8,128)S(1)}, f32[2,2,64,128]{3,2,1,0:T(8,128)S(1)}, u32[]{:S(2)}, u32[]{:S(2)}) collective-permute-start(f32[2,2,64,128]{3,2,1,0:T(8,128)S(1)} %get-tuple-element.68), channel_id=1, source_target_pairs={{64,0},{80,16},{96,32},{112,48},{0,64},{16,80},{32,96},{48,112},{6... | collective-permute-start | bytes 393224 | tf_op jit(solution)/shard_map/ppermute | solution.py:494
  77.6 11.7 %collective-permute-start.24 = (f32[2,64,1024]{2,1,0:T(8,128)S(1)}, f32[2,64,1024]{2,1,0:T(8,128)S(1)}, u32[]{:S(2)}, u32[]{:S(2)}) collective-permute-start(f32[2,64,1024]{2,1,0:T(8,128)S(1)} %pad_maximum_fusion.3.refs_0_), channel_id=1, source_target_pairs={{4,0},{5,1},{6,2},{7,3},{8,4},{9,5},{10,6},{11,7},{12,8},{13,9},{1... | collective-permute-start | bytes 1572872 | tf_op jit(solution)/shard_map/ppermute | solution.py:494
  81.2 13.1 %collective-permute-start.18 = (f32[2,64,1024]{2,1,0:T(8,128)S(1)}, f32[2,64,1024]{2,1,0:T(8,128)S(1)}, u32[]{:S(2)}, u32[]{:S(2)}) collective-permute-start(f32[2,64,1024]{2,1,0:T(8,128)S(1)} %pad_maximum_fusion.2.refs_0_), channel_id=1, source_target_pairs={{96,0},{112,16},{0,32},{16,48},{32,64},{48,80},{64,96},{80,112},{9... | collective-permute-start | bytes 1572872 | tf_op jit(solution)/shard_map/ppermute | solution.py:494
  81.3 13.2 %collective-permute-start.16 = (f32[2,64,1024]{2,1,0:T(8,128)S(1)}, f32[2,64,1024]{2,1,0:T(8,128)S(1)}, u32[]{:S(2)}, u32[]{:S(2)}) collective-permute-start(f32[2,64,1024]{2,1,0:T(8,128)S(1)} %pad_maximum_fusion.2.refs_0_), channel_id=1, source_target_pairs={{32,0},{48,16},{64,32},{80,48},{96,64},{112,80},{0,96},{16,112},{3... | collective-permute-start | bytes 1572872 | tf_op jit(solution)/shard_map/ppermute | solution.py:494
  84.1 16.5 %collective-permute-start.15 = (f32[8,2,64,128]{3,2,1,0:T(8,128)S(1)}, f32[8,2,64,128]{3,2,1,0:T(8,128)S(1)}, u32[]{:S(2)}, u32[]{:S(2)}) collective-permute-start(f32[8,2,64,128]{3,2,1,0:T(8,128)S(1)} %bitcast.50), channel_id=1, source_target_pairs={{0,1},{1,0},{2,3},{3,2},{4,5},{5,4},{6,7},{7,6},{8,9},{9,8},{10,11... | collective-permute-start | bytes 1572872 | tf_op jit(solution)/shard_map/ppermute | solution.py:498
  86.2 11.2 %collective-permute-start.27 = (f32[64,1024]{1,0:T(8,128)S(1)}, f32[64,1024]{1,0:T(8,128)S(1)}, u32[]{:S(2)}, u32[]{:S(2)}) collective-permute-start(f32[64,1024]{1,0:T(8,128)S(1)} %slice_bitcast_fusion.2), channel_id=1, source_target_pairs={{12,0},{13,1},{14,2},{15,3},{0,4},{1,5},{2,6},{3,7},{4,8},{5,9},{6... | collective-permute-start | bytes 786440 | tf_op jit(solution)/shard_map/ppermute | solution.py:494
  89.3 11.2 %collective-permute-start.25 = (f32[64,1024]{1,0:T(8,128)S(1)}, f32[64,1024]{1,0:T(8,128)S(1)}, u32[]{:S(2)}, u32[]{:S(2)}) collective-permute-start(f32[64,1024]{1,0:T(8,128)S(1)} %slice_bitcast_fusion.3), channel_id=1, source_target_pairs={{4,0},{5,1},{6,2},{7,3},{8,4},{9,5},{10,6},{11,7},{12,8},{13,9},{1... | collective-permute-start | bytes 786440 | tf_op jit(solution)/shard_map/ppermute | solution.py:494
  94.5 10.3 %collective-permute-start.17 = (f32[64,1024]{1,0:T(8,128)S(1)}, f32[64,1024]{1,0:T(8,128)S(1)}, u32[]{:S(2)}, u32[]{:S(2)}) collective-permute-start(f32[64,1024]{1,0:T(8,128)S(1)} %slice_bitcast_fusion.5), channel_id=1, source_target_pairs={{32,0},{48,16},{64,32},{80,48},{96,64},{112,80},{0,96},{16,112},{3... | collective-permute-start | bytes 786440 | tf_op jit(solution)/shard_map/ppermute | solution.py:494
  97.3 28.8 %collective-permute-start.28 = (f32[2,64,1024]{2,1,0:T(8,128)S(1)}, f32[2,64,1024]{2,1,0:T(8,128)S(1)}, u32[]{:S(2)}, u32[]{:S(2)}) collective-permute-start(f32[2,64,1024]{2,1,0:T(8,128)S(1)} %pad_maximum_fusion.3.refs_0_), channel_id=1, source_target_pairs={{0,1},{1,0},{2,3},{3,2},{4,5},{5,4},{6,7},{7,6},{8,9},{9,8},{10,11... | collective-permute-start | bytes 1572872 | tf_op jit(solution)/shard_map/ppermute | solution.py:498
  100.5 26.5 %collective-permute-start.21 = (f32[2304,128]{1,0:T(8,128)S(1)}, f32[2304,128]{1,0:T(8,128)S(1)}, u32[]{:S(2)}, u32[]{:S(2)}) collective-permute-start(f32[2304,128]{1,0:T(8,128)S(1)} %get-tuple-element.48), channel_id=1, source_target_pairs={{15,0},{0,1},{1,2},{2,3},{3,4},{4,5},{5,6},{6,7},{7,8},{8,9},{9,10... | collective-permute-start | bytes 3538952 | tf_op jit(solution)/shard_map/ppermute | solution.py:494
  100.5 29.8 %collective-permute-start.22 = (f32[2304,128]{1,0:T(8,128)S(1)}, f32[2304,128]{1,0:T(8,128)S(1)}, u32[]{:S(2)}, u32[]{:S(2)}) collective-permute-start(f32[2304,128]{1,0:T(8,128)S(1)} %get-tuple-element.50), channel_id=1, source_target_pairs={{1,0},{2,1},{3,2},{4,3},{5,4},{6,5},{7,6},{8,7},{9,8},{10,9},{11,1... | collective-permute-start | bytes 3538952 | tf_op jit(solution)/shard_map/ppermute | solution.py:494
  101.1 24.9 %collective-permute-start.29 = (f32[2,2,64,1024]{3,2,1,0:T(8,128)S(1)}, f32[2,2,64,1024]{3,2,1,0:T(8,128)S(1)}, u32[]{:S(2)}, u32[]{:S(2)}) collective-permute-start(f32[2,2,64,1024]{3,2,1,0:T(8,128)S(1)} %pad_maximum_fusion), channel_id=1, source_target_pairs={{0,1},{1,0},{2,3},{3,2},{4,5},{5,4},{6,7},{7,6},{8,9},{9,8},{10,11... | collective-permute-start | bytes 3145736 | tf_op jit(solution)/shard_map/ppermute | solution.py:498
  104.9 21.3 %collective-permute-start.30 = (f32[2,64,1024]{2,1,0:T(8,128)S(1)}, f32[2,64,1024]{2,1,0:T(8,128)S(1)}, u32[]{:S(2)}, u32[]{:S(2)}) collective-permute-start(f32[2,64,1024]{2,1,0:T(8,128)S(1)} %pad_maximum_fusion.4), channel_id=1, source_target_pairs={{0,1},{1,0},{2,3},{3,2},{4,5},{5,4},{6,7},{7,6},{8,9},{9,8},{10,11... | collective-permute-start | bytes 1572872 | tf_op jit(solution)/shard_map/ppermute | solution.py:498
  (23 other events, 236.8 us)

commit v4 on v3

--- a/solution.py
+++ b/solution.py
@@ -294,17 +294,17 @@
     return jnp.dot(a, b, precision=HI, preferred_element_type=F32)
 
 
+def sum_of(parts):
+    return parts[0] + (parts[1] + parts[2])
+
+
 def inverse_kernel(own_ref, other_ref, rslot_ref, cslot_ref, noise_ref, o_ref, s_ref):
     rows_in = ROWS * HALF
-    pick_rows = (lax.broadcasted_iota(jnp.int32, (M, rows_in), 1) == rslot_ref[...]).astype(F32)
-    total = jnp.zeros((M, M), F32)
-    for k, ref in enumerate((own_ref, other_ref)):
-        for h in range(2):
-            piece = ref[:, h].reshape(rows_in, NGY)
-            some = dot(pick_rows, piece)
-            base = (2 * k + h) * NGY
-            pick = lax.broadcasted_iota(jnp.int32, (NGY, M), 0) + base == cslot_ref[...]
-            total = total + dot(some, pick.astype(F32))
+    pick_rows = (lax.broadcasted_iota(jnp.int32, (M, rows_in), 1) == rslot_ref[...]).astype(BF16)
+    pieces = [ref[:, h].reshape(rows_in, NGY) for ref in (own_ref, other_ref) for h in range(2)]
+    some = sum_of([bdot(pick_rows, part) for part in three(jnp.concatenate(pieces, axis=1))])
+    pick = (lax.broadcasted_iota(jnp.int32, (4 * NGY, M), 0) == cslot_ref[...]).astype(BF16)
+    total = sum_of([bdot(part, pick) for part in three(some)])
     i0 = lax.broadcasted_iota(jnp.int32, (M, M), 0)
     i1 = lax.broadcasted_iota(jnp.int32, (M, M), 1)
     s_ref[...] = total + jnp.where(i0 == i1, noise_ref[...], 0.0)
@@ -357,23 +357,25 @@
     return jnp.concatenate([p[...].reshape(-1, p.shape[-1]) for p in refs], axis=0)
 
 
-def across_kernel(slot_ref, *refs):
+def across_kernel(slot_ref, inv_ref, *refs):
     pick = (lax.broadcasted_iota(jnp.int32, (M, SLOTS), 1) == slot_ref[...]).astype(BF16)
-    high, mid, low = three(joined(refs[:-1]))
-    refs[-1][...] = bdot(pick, high) + (bdot(pick, mid) + bdot(pick, low))
-
-
-def across(slot, parts):
+    rows = sum_of([bdot(pick, part) for part in three(joined(refs[:-2]))])
+    high, low = split(dot(inv_ref[...], rows))
+    refs[-2][...] = high
+    refs[-1][...] = low
+
+
+def across(slot, inv, parts):
     cols = parts[0].shape[-1]
     return pl.pallas_call(
         across_kernel,
-        out_shape=jax.ShapeDtypeStruct((M, cols), F32),
-        in_specs=vmem(1 + len(parts)),
-        out_specs=vmem(1)[0],
-        compiler_params=pltpu.CompilerParams(vmem_limit_bytes=14 << 20),
+        out_shape=(jax.ShapeDtypeStruct((M, cols), BF16), jax.ShapeDtypeStruct((M, cols), BF16)),
+        in_specs=vmem(2 + len(parts)),
+        out_specs=tuple(vmem(2)),
+        compiler_params=pltpu.CompilerParams(vmem_limit_bytes=16 << 20),
         cost_estimate=cost(6 * M * SLOTS * cols, 3 * SLOTS * cols * 4),
         name="across",
-    )(slot, *parts)
+    )(slot, inv, *parts)
 
 
 def strip_kernel(slot_ref, *refs):
@@ -397,8 +399,8 @@
 
 
 def update_kernel(
-    place, p_ref, proc_ref, inv_ref, xc_ref, rc_ref, cc_ref, up_ref, dn_ref, el_ref, er_ref,
-    oh_ref, ol_ref, ph_ref, pl_ref, o_ref, uh, ul, sh, sl,
+    place, p_ref, proc_ref, uh, ul, rc_ref, cc_ref, up_ref, dn_ref, el_ref, er_ref,
+    oh_ref, ol_ref, ph_ref, pl_ref, o_ref, sh, sl,
 ):
     h, j = pl.program_id(0), pl.program_id(1)
     steps = pl.num_programs(1)
@@ -407,12 +409,6 @@
     size, cols = o_ref.shape
     tiles, many = cols // NGY, size // NGY
     last = 2 * steps * many - 1
-
-    @pl.when((h == 0) & (j == 0))
-    def _():
-        high, low = split(dot(inv_ref[...], xc_ref[...]))
-        uh[...] = high
-        ul[...] = low
 
     rows = pl.ds(pl.multiple_of(j * size, size), size)
     for half, (hi_ref, lo_ref) in enumerate(((oh_ref, ol_ref), (ph_ref, pl_ref))):
@@ -462,7 +458,7 @@
             o_ref[some, :] = o_ref[some, :] + jnp.concatenate(rim, axis=1)
 
 
-def update(place, block, proc, inv, xc, row_coef, col_coef, rims, own, other):
+def update(place, block, proc, solved, row_coef, col_coef, rims, own, other):
     rows, cols = block.shape
     half = rows // 2
     size = 2 * NGY
@@ -478,8 +474,6 @@
             in_specs=vmem(4) + [few] + vmem(9),
             out_specs=tile,
             scratch_shapes=[
-                pltpu.VMEM((M, cols), BF16),
-                pltpu.VMEM((M, cols), BF16),
                 pltpu.VMEM((size, M), BF16),
                 pltpu.VMEM((size, M), BF16),
             ],
@@ -487,7 +481,7 @@
         compiler_params=pltpu.CompilerParams(vmem_limit_bytes=30 << 20),
         cost_estimate=cost(6 * rows * cols * M, 8 * rows * cols),
         name="update",
-    )(place, block, proc, inv, xc, row_coef, col_coef, *rims, *own, *other)
+    )(place, block, proc, *solved, row_coef, col_coef, *rims, *own, *other)
 
 
 def shift(x, axis, count, back):
@@ -595,13 +589,13 @@
         + (wc // 4) * WMAX
         + rank
     )
-    xc = across(row_slot[:, None], x_parts)
     own = strip(strip_slot[None], own)
     other = strip(strip_slot[None], other)
     inv = inverse(g, g_other, gram_slot[:, None], col_slot[None], noise)
+    solved = across(row_slot[:, None], inv, x_parts)
     rims = (up, dn, el, er)
     scalars = jnp.stack([c % 2, start[0]])
-    return update(scalars, block, col_coef[5:6], inv, xc, row_coef, col_coef[:5], rims, own, other)
+    return update(scalars, block, col_coef[5:6], solved, row_coef, col_coef[:5], rims, own, other)
 
 
 def solution(mesh):

time: 146 us -> 144 us (0.986)
  Pallas kernels: 49.3 us -> 47.3 us
    pallas_call x1, Pallas kernels: 18.9 us -> 16.8 us  [inverse(): pl.pallas_call(inverse_kernel, out_shape=jax.ShapeDtypeStruct((M, M), F32...]
  transfers between devices with their start and end apart: 31 -> 31, of which waited for: 10 -> 11; matrix products, arithmetic and copies ran while one was open for 4% -> 4% of each run, Pallas kernels for 16% -> 16%
where the time goes in v4:
time: 144 us
  starting transfers between devices  54.6 us (38%)
  Pallas kernels  47.3 us (33%)
  waiting for transfers between devices  34.2 us (24%)
  other arithmetic  3.78 us (3%)
  local copies, waits for them, and re-layouts  3.47 us (2%)
    ppermute x22, starting transfers between devices, shift(): lax.ppermute(x, axis, [((i + back) % count, i) for i in range(count)])  32.2 us
    ppermute x22, waiting for transfers between devices, shift(): lax.ppermute(x, axis, [((i + back) % count, i) for i in range(count)])  19.3 us
    pallas_call x1, Pallas kernels, inverse(): pl.pallas_call(inverse_kernel, out_shape=jax.ShapeDtypeStruct((M, M), F32...  16.8 us
    ppermute x7, starting transfers between devices, flip(): return lax.ppermute(x, axis, [(i, i ^ bit) for i in range(count)])  15.7 us
    pallas_call x1, Pallas kernels, update(): pl.pallas_call(update_kernel, out_shape=jax.ShapeDtypeStruct((rows, cols)...  13.5 us
    ppermute x1, waiting for transfers between devices, shards(): first = lax.ppermute(x, ('row', 'col'), turn)  10.6 us
    pallas_call x1, Pallas kernels, tables(): pl.pallas_call(table_kernel, out_shape=(jax.ShapeDtypeStruct((HALF, cols)...  9.12 us
    ppermute x7, waiting for transfers between devices, flip(): return lax.ppermute(x, axis, [(i, i ^ bit) for i in range(count)])  4.29 us
  transfers between devices with their start and end apart: 31, of which 11 were waited for; matrix products, arithmetic and copies ran while one was open for 4% of the time, Pallas kernels for 16%

profile of v4, /device:TPU:3, one launch (start us, length us, event | category | flops | bytes accessed | tf_op | source)
XLA Modules:
  0.0 143.9 jit_solution(11774512379088734715)
XLA Ops:
  0.7 9.1 %tables.1 = (f32[64,1024]{1,0:T(8,128)}, f32[32,1024]{1,0:T(8,128)}, f32[32,1024]{1,0:T(8,128)}, f32[64,128]{1,0:T(8,128)}, s32[1,128]{1,0:T(1,128)}, /*index=5*...) custom-call(s32[2]{0:T(128)} %pad_add_fusion.1.place, s32[1,256]{1,0:T(1,128)} %wells.1, ...), custom_call_target="tpu_custom_call" | custom-call | flops 1048576 | bytes 2097152 | tf_op jit(solution)/shard_map/tables/pallas_call | solution.py:123
  11.1 3.6 %collective-permute-start.1 = (f32[32,1024]{1,0:T(8,128)}, f32[32,1024]{1,0:T(8,128)S(1)}, u32[]{:S(2)}, u32[]{:S(2)}) collective-permute-start(f32[32,1024]{1,0:T(8,128)} %get-tuple-element.32), channel_id=1, source_target_pairs={{16,0},{32,16},{48,32},{64,48},{80,64},{96,80},{112,96},{0,112},{1... | collective-permute-start | bytes 393224 | tf_op jit(solution)/shard_map/ppermute | solution.py:488
  21.2 4.4 %collective-permute-start.2 = (f32[64,128]{1,0:T(8,128)}, f32[64,128]{1,0:T(8,128)S(1)}, u32[]{:S(2)}, u32[]{:S(2)}) collective-permute-start(f32[64,128]{1,0:T(8,128)} %get-tuple-element.39), channel_id=1, source_target_pairs={{15,0},{0,1},{1,2},{2,3},{3,4},{4,5},{5,6},{6,7},{7,8},{8,9},{9,10... | collective-permute-start | bytes 98312 | tf_op jit(solution)/shard_map/ppermute | solution.py:488
  28.4 2.2 %collective-permute-done.3.zr_ref = f32[64,128]{1,0:T(8,128)S(1)} collective-permute-done((f32[64,128]{1,0:T(8,128)}, f32[64,128]{1,0:T(8,128)S(1)}, u32[]{:S(2)}, u32[]{:S(2)}) %collective-permute-start.3) | collective-permute-done | bytes 32800 | tf_op jit(solution)/shard_map/ppermute | solution.py:488
  31.2 2.1 %well_cols.1 = (f32[64,1024]{1,0:T(8,128)}, f32[64,128]{1,0:T(8,128)}) custom-call(f32[64,1024]{1,0:T(8,128)} %get-tuple-element.37.z_ref, f32[64,128]{1,0:T(8,128)} %copy-done.8, f32[64,128]{1,0:T(8,128)} %copy-done.9, f32[5,1024]{1,0:T(8,128)} %constant_dynamic-slice_fusion.1.coef_ref.cc_ref, f32[64,128]{1,0:T(8,128)} %get-tuple-element.35.aux_ref, ...), custom_call_target="tpu_custom_call" | custom-call | flops 100663296 | bytes 1048576 | tf_op jit(solution)/shard_map/well_cols/pallas_call | solution.py:208
  38.3 3.5 %collective-permute-start.8 = (f32[64,1024]{1,0:T(8,128)}, f32[64,1024]{1,0:T(8,128)S(1)}, u32[]{:S(2)}, u32[]{:S(2)}) collective-permute-start(f32[64,1024]{1,0:T(8,128)} %get-tuple-element.43), channel_id=1, source_target_pairs={{0,0},{1,1},{2,16},{3,17},{4,36},{5,37},{6,52},{7,53},{8,72},{9,73... | collective-permute-start | bytes 786440 | tf_op jit(solution)/shard_map/ppermute | solution.py:544
  41.8 2.7 %collective-permute-start.20 = (f32[128,1024]{1,0:T(8,128)S(1)}, f32[128,1024]{1,0:T(8,128)S(1)}, u32[]{:S(2)}, u32[]{:S(2)}) collective-permute-start(f32[128,1024]{1,0:T(8,128)S(1)} %copy-done.12), channel_id=1, source_target_pairs={{112,0},{0,16},{16,32},{32,48},{48,64},{64,80},{80,96},{96,112},{1... | collective-permute-start | bytes 1572872 | tf_op jit(solution)/shard_map/ppermute | solution.py:488
  44.6 3.1 %collective-permute-start.23 = (f32[64,1024]{1,0:T(8,128)S(1)}, f32[64,1024]{1,0:T(8,128)S(1)}, u32[]{:S(2)}, u32[]{:S(2)}) collective-permute-start(f32[64,1024]{1,0:T(8,128)S(1)} %collective-permute-done.7), channel_id=1, source_target_pairs={{0,0},{1,1},{2,16},{3,17},{4,36},{5,37},{6,52},{7,53},{8,72},{9,73... | collective-permute-start | bytes 786440 | tf_op jit(solution)/shard_map/ppermute | solution.py:546
  48.5 10.6 %collective-permute-done.8 = f32[64,1024]{1,0:T(8,128)S(1)} collective-permute-done((f32[64,1024]{1,0:T(8,128)}, f32[64,1024]{1,0:T(8,128)S(1)}, u32[]{:S(2)}, u32[]{:S(2)}) %collective-permute-start.8) | collective-permute-done | bytes 262176 | tf_op jit(solution)/shard_map/ppermute | solution.py:544
  60.3 3.1 %collective-permute-done.10 = f32[64,128]{1,0:T(8,128)S(1)} collective-permute-done((f32[64,128]{1,0:T(8,128)S(1)}, f32[64,128]{1,0:T(8,128)S(1)}, u32[]{:S(2)}, u32[]{:S(2)}) %collective-permute-start.10) | collective-permute-done | bytes 32800 | tf_op jit(solution)/shard_map/ppermute | solution.py:492
  63.4 5.6 %collective-permute-start.11 = (f32[2,64,128]{2,1,0:T(8,128)S(1)}, f32[2,64,128]{2,1,0:T(8,128)S(1)}, u32[]{:S(2)}, u32[]{:S(2)}) collective-permute-start(f32[2,64,128]{2,1,0:T(8,128)S(1)} %get-tuple-element.74), channel_id=1, source_target_pairs={{0,16},{16,0},{32,48},{48,32},{64,80},{80,64},{96,112},{112,96},{1... | collective-permute-start | bytes 196616 | tf_op jit(solution)/shard_map/ppermute | solution.py:492
  71.4 4.1 %collective-permute-start.13 = (f32[2,2,64,128]{3,2,1,0:T(8,128)S(1)}, f32[2,2,64,128]{3,2,1,0:T(8,128)S(1)}, u32[]{:S(2)}, u32[]{:S(2)}) collective-permute-start(f32[2,2,64,128]{3,2,1,0:T(8,128)S(1)} %get-tuple-element.72), channel_id=1, source_target_pairs={{64,0},{80,16},{96,32},{112,48},{0,64},{16,80},{32,96},{48,112},{6... | collective-permute-start | bytes 393224 | tf_op jit(solution)/shard_map/ppermute | solution.py:488
  77.6 3.5 %collective-permute-done.13 = f32[2,2,64,128]{3,2,1,0:T(8,128)S(1)} collective-permute-done((f32[2,2,64,128]{3,2,1,0:T(8,128)S(1)}, f32[2,2,64,128]{3,2,1,0:T(8,128)S(1)}, u32[]{:S(2)}, u32[]{:S(2)}) %collective-permute-start.13) | collective-permute-done | bytes 131104 | tf_op jit(solution)/shard_map/ppermute | solution.py:488
  81.3 2.7 %collective-permute-start.16 = (f32[2,64,1024]{2,1,0:T(8,128)S(1)}, f32[2,64,1024]{2,1,0:T(8,128)S(1)}, u32[]{:S(2)}, u32[]{:S(2)}) collective-permute-start(f32[2,64,1024]{2,1,0:T(8,128)S(1)} %pad_maximum_fusion.2.refs_0_), channel_id=1, source_target_pairs={{32,0},{48,16},{64,32},{80,48},{96,64},{112,80},{0,96},{16,112},{3... | collective-permute-start | bytes 1572872 | tf_op jit(solution)/shard_map/ppermute | solution.py:488
  84.0 2.1 %collective-permute-start.15 = (f32[8,2,64,128]{3,2,1,0:T(8,128)S(1)}, f32[8,2,64,128]{3,2,1,0:T(8,128)S(1)}, u32[]{:S(2)}, u32[]{:S(2)}) collective-permute-start(f32[8,2,64,128]{3,2,1,0:T(8,128)S(1)} %bitcast.50), channel_id=1, source_target_pairs={{0,1},{1,0},{2,3},{3,2},{4,5},{5,4},{6,7},{7,6},{8,9},{9,8},{10,11... | collective-permute-start | bytes 1572872 | tf_op jit(solution)/shard_map/ppermute | solution.py:492
  86.6 2.6 %collective-permute-done.24.refs_1_ = f32[2,64,1024]{2,1,0:T(8,128)S(1)} collective-permute-done((f32[2,64,1024]{2,1,0:T(8,128)S(1)}, f32[2,64,1024]{2,1,0:T(8,128)S(1)}, u32[]{:S(2)}, u32[]{:S(2)}) %collective-permute-start.24) | collective-permute-done | bytes 524320 | tf_op jit(solution)/shard_map/ppermute | solution.py:488
  89.6 4.7 %collective-permute-done.18.refs_4_ = f32[2,64,1024]{2,1,0:T(8,128)S(1)} collective-permute-done((f32[2,64,1024]{2,1,0:T(8,128)S(1)}, f32[2,64,1024]{2,1,0:T(8,128)S(1)}, u32[]{:S(2)}, u32[]{:S(2)}) %collective-permute-start.18) | collective-permute-done | bytes 524320 | tf_op jit(solution)/shard_map/ppermute | solution.py:488
  94.4 2.7 %collective-permute-start.17 = (f32[64,1024]{1,0:T(8,128)S(1)}, f32[64,1024]{1,0:T(8,128)S(1)}, u32[]{:S(2)}, u32[]{:S(2)}) collective-permute-start(f32[64,1024]{1,0:T(8,128)S(1)} %slice_bitcast_fusion.5), channel_id=1, source_target_pairs={{32,0},{48,16},{64,32},{80,48},{96,64},{112,80},{0,96},{16,112},{3... | collective-permute-start | bytes 786440 | tf_op jit(solution)/shard_map/ppermute | solution.py:488
  97.3 3.1 %collective-permute-start.28 = (f32[2,64,1024]{2,1,0:T(8,128)S(1)}, f32[2,64,1024]{2,1,0:T(8,128)S(1)}, u32[]{:S(2)}, u32[]{:S(2)}) collective-permute-start(f32[2,64,1024]{2,1,0:T(8,128)S(1)} %pad_maximum_fusion.3.refs_0_), channel_id=1, source_target_pairs={{0,1},{1,0},{2,3},{3,2},{4,5},{5,4},{6,7},{7,6},{8,9},{9,8},{10,11... | collective-permute-start | bytes 1572872 | tf_op jit(solution)/shard_map/ppermute | solution.py:492
  101.1 3.7 %collective-permute-start.29 = (f32[2,2,64,1024]{3,2,1,0:T(8,128)S(1)}, f32[2,2,64,1024]{3,2,1,0:T(8,128)S(1)}, u32[]{:S(2)}, u32[]{:S(2)}) collective-permute-start(f32[2,2,64,1024]{3,2,1,0:T(8,128)S(1)} %pad_maximum_fusion), channel_id=1, source_target_pairs={{0,1},{1,0},{2,3},{3,2},{4,5},{5,4},{6,7},{7,6},{8,9},{9,8},{10,11... | collective-permute-start | bytes 3145736 | tf_op jit(solution)/shard_map/ppermute | solution.py:492
  105.1 16.8 %inverse.1.inv_ref = f32[256,256]{1,0:T(8,128)S(1)} custom-call(f32[8,2,64,128]{3,2,1,0:T(8,128)S(1)} %bitcast.51, f32[8,2,64,128]{3,2,1,0:T(8,128)S(1)} %collective-permute-done.15.other_ref, s32[256,1]{1,0:T(8,128)S(1)} %fusion.7.rslot_ref.slot_ref, s32[1,256]{1,0:T(1,128)S(1)} %add_add_fusion.2.cslot_ref, f32[1,256]{1,0:T(1,128)S(1)} %copy-done.1), custom_call_target="tpu_custom_call" | custom-call | flops 18447998976 | bytes 4194304 | tf_op jit(solution)/shard_map/inverse/pallas_call | solution.py:330
  122.6 2.4 %across.1 = (bf16[256,1024]{1,0:T(8,128)(2,1)S(1)}, bf16[256,1024]{1,0:T(8,128)(2,1)S(1)}) custom-call(s32[256,1]{1,0:T(8,128)S(1)} %fusion.7.rslot_ref.slot_ref, f32[256,256]{1,0:T(8,128)S(1)} %inverse.1.inv_ref, f32[2,64,1024]{2,1,0:T(8,128)S(1)} %pad_maximum_fusion.2.refs_0_, f32[2,64,1024]{2,1,0:T(8,128)S(1)} %collective-permute-done.16.refs_1_, ...), custom_call_target="tpu_custom_call" | custom-call | flops 805306368 | bytes 6291456 | tf_op jit(solution)/shard_map/across/pallas_call | solution.py:370
  126.2 4.1 %collective-permute-done.22.er_ref = f32[2304,128]{1,0:T(8,128)S(1)} collective-permute-done((f32[2304,128]{1,0:T(8,128)S(1)}, f32[2304,128]{1,0:T(8,128)S(1)}, u32[]{:S(2)}, u32[]{:S(2)}) %collective-permute-start.22) | collective-permute-done | bytes 1179680 | tf_op jit(solution)/shard_map/ppermute | solution.py:488
  130.3 13.5 %update.1 = f32[2048,1024]{1,0:T(8,128)} custom-call(s32[2]{0:T(128)S(1)} %pad_add_fusion.place, f32[2048,1024]{1,0:T(8,128)S(1)} %bitcast.45, f32[1,1024]{1,0:T(1,128)S(1)} %dynamic-slice.proc_ref, bf16[256,1024]{1,0:T(8,128)(2,1)S(1)} %get-tuple-element.48.uh, bf16[256,1024]{1,0:T(8,128)(2,1)S(1)} %get-tuple-element.49.ul, f32[2048,8]{1,0:T(8,128)S(1)} %copy.19.rc_ref, ...), custom_call_target="tpu_custom_call" | custom-call | flops 3221225472 | bytes 16777216 | tf_op jit(solution)/shard_map/update/pallas_call | solution.py:468
  (111 shorter events, 26.9 us)
Async XLA Ops:
  9.8 8.3 %collective-permute-start = (f32[32,1024]{1,0:T(8,128)}, f32[32,1024]{1,0:T(8,128)S(1)}, u32[]{:S(2)}, u32[]{:S(2)}) collective-permute-start(f32[32,1024]{1,0:T(8,128)} %get-tuple-element.36), channel_id=1, source_target_pairs={{112,0},{0,16},{16,32},{32,48},{48,64},{64,80},{80,96},{96,112},{1... | collective-permute-start | bytes 393224 | tf_op jit(solution)/shard_map/ppermute | solution.py:488
  11.1 7.4 %collective-permute-start.1 = (f32[32,1024]{1,0:T(8,128)}, f32[32,1024]{1,0:T(8,128)S(1)}, u32[]{:S(2)}, u32[]{:S(2)}) collective-permute-start(f32[32,1024]{1,0:T(8,128)} %get-tuple-element.32), channel_id=1, source_target_pairs={{16,0},{32,16},{48,32},{64,48},{80,64},{96,80},{112,96},{0,112},{1... | collective-permute-start | bytes 393224 | tf_op jit(solution)/shard_map/ppermute | solution.py:488
  21.2 7.3 %collective-permute-start.2 = (f32[64,128]{1,0:T(8,128)}, f32[64,128]{1,0:T(8,128)S(1)}, u32[]{:S(2)}, u32[]{:S(2)}) collective-permute-start(f32[64,128]{1,0:T(8,128)} %get-tuple-element.39), channel_id=1, source_target_pairs={{15,0},{0,1},{1,2},{2,3},{3,4},{4,5},{5,6},{6,7},{7,8},{8,9},{9,10... | collective-permute-start | bytes 98312 | tf_op jit(solution)/shard_map/ppermute | solution.py:488
  26.1 33.1 %collective-permute-start.9 = (f32[128,1024]{1,0:T(8,128)S(1)}, f32[128,1024]{1,0:T(8,128)S(1)}, u32[]{:S(2)}, u32[]{:S(2)}) collective-permute-start(f32[128,1024]{1,0:T(8,128)S(1)} %copy-done.13), channel_id=1, source_target_pairs={{16,0},{32,16},{48,32},{64,48},{80,64},{96,80},{112,96},{0,112},{1... | collective-permute-start | bytes 1572872 | tf_op jit(solution)/shard_map/ppermute | solution.py:488
  34.6 10.0 %collective-permute-start.7 = (f32[64,1024]{1,0:T(8,128)}, f32[64,1024]{1,0:T(8,128)S(1)}, u32[]{:S(2)}, u32[]{:S(2)}) collective-permute-start(f32[64,1024]{1,0:T(8,128)} %get-tuple-element.43), channel_id=1, source_target_pairs={{0,16},{16,0},{32,48},{48,32},{64,80},{80,64},{96,112},{112,96},{1... | collective-permute-start | bytes 786440 | tf_op jit(solution)/shard_map/ppermute | solution.py:492
  36.3 11.4 %collective-permute-start.4 = (f32[64,128]{1,0:T(8,128)}, f32[64,128]{1,0:T(8,128)S(1)}, u32[]{:S(2)}, u32[]{:S(2)}) collective-permute-start(f32[64,128]{1,0:T(8,128)} %get-tuple-element.42), channel_id=1, source_target_pairs={{4,0},{5,1},{6,2},{7,3},{8,4},{9,5},{10,6},{11,7},{12,8},{13,9},{1... | collective-permute-start | bytes 98312 | tf_op jit(solution)/shard_map/ppermute | solution.py:488
  38.3 20.9 %collective-permute-start.8 = (f32[64,1024]{1,0:T(8,128)}, f32[64,1024]{1,0:T(8,128)S(1)}, u32[]{:S(2)}, u32[]{:S(2)}) collective-permute-start(f32[64,1024]{1,0:T(8,128)} %get-tuple-element.43), channel_id=1, source_target_pairs={{0,0},{1,1},{2,16},{3,17},{4,36},{5,37},{6,52},{7,53},{8,72},{9,73... | collective-permute-start | bytes 786440 | tf_op jit(solution)/shard_map/ppermute | solution.py:544
  41.8 35.7 %collective-permute-start.20 = (f32[128,1024]{1,0:T(8,128)S(1)}, f32[128,1024]{1,0:T(8,128)S(1)}, u32[]{:S(2)}, u32[]{:S(2)}) collective-permute-start(f32[128,1024]{1,0:T(8,128)S(1)} %copy-done.12), channel_id=1, source_target_pairs={{112,0},{0,16},{16,32},{32,48},{48,64},{64,80},{80,96},{96,112},{1... | collective-permute-start | bytes 1572872 | tf_op jit(solution)/shard_map/ppermute | solution.py:488
  44.6 24.5 %collective-permute-start.23 = (f32[64,1024]{1,0:T(8,128)S(1)}, f32[64,1024]{1,0:T(8,128)S(1)}, u32[]{:S(2)}, u32[]{:S(2)}) collective-permute-start(f32[64,1024]{1,0:T(8,128)S(1)} %collective-permute-done.7), channel_id=1, source_target_pairs={{0,0},{1,1},{2,16},{3,17},{4,36},{5,37},{6,52},{7,53},{8,72},{9,73... | collective-permute-start | bytes 786440 | tf_op jit(solution)/shard_map/ppermute | solution.py:546
  63.4 7.8 %collective-permute-start.11 = (f32[2,64,128]{2,1,0:T(8,128)S(1)}, f32[2,64,128]{2,1,0:T(8,128)S(1)}, u32[]{:S(2)}, u32[]{:S(2)}) collective-permute-start(f32[2,64,128]{2,1,0:T(8,128)S(1)} %get-tuple-element.74), channel_id=1, source_target_pairs={{0,16},{16,0},{32,48},{48,32},{64,80},{80,64},{96,112},{112,96},{1... | collective-permute-start | bytes 196616 | tf_op jit(solution)/shard_map/ppermute | solution.py:492
  69.1 17.0 %collective-permute-start.26 = (f32[2,64,1024]{2,1,0:T(8,128)S(1)}, f32[2,64,1024]{2,1,0:T(8,128)S(1)}, u32[]{:S(2)}, u32[]{:S(2)}) collective-permute-start(f32[2,64,1024]{2,1,0:T(8,128)S(1)} %pad_maximum_fusion.3.refs_0_), channel_id=1, source_target_pairs={{12,0},{13,1},{14,2},{15,3},{0,4},{1,5},{2,6},{3,7},{4,8},{5,9},{6... | collective-permute-start | bytes 1572872 | tf_op jit(solution)/shard_map/ppermute | solution.py:488
  71.4 9.7 %collective-permute-start.13 = (f32[2,2,64,128]{3,2,1,0:T(8,128)S(1)}, f32[2,2,64,128]{3,2,1,0:T(8,128)S(1)}, u32[]{:S(2)}, u32[]{:S(2)}) collective-permute-start(f32[2,2,64,128]{3,2,1,0:T(8,128)S(1)} %get-tuple-element.72), channel_id=1, source_target_pairs={{64,0},{80,16},{96,32},{112,48},{0,64},{16,80},{32,96},{48,112},{6... | collective-permute-start | bytes 393224 | tf_op jit(solution)/shard_map/ppermute | solution.py:488
  77.5 11.7 %collective-permute-start.24 = (f32[2,64,1024]{2,1,0:T(8,128)S(1)}, f32[2,64,1024]{2,1,0:T(8,128)S(1)}, u32[]{:S(2)}, u32[]{:S(2)}) collective-permute-start(f32[2,64,1024]{2,1,0:T(8,128)S(1)} %pad_maximum_fusion.3.refs_0_), channel_id=1, source_target_pairs={{4,0},{5,1},{6,2},{7,3},{8,4},{9,5},{10,6},{11,7},{12,8},{13,9},{1... | collective-permute-start | bytes 1572872 | tf_op jit(solution)/shard_map/ppermute | solution.py:488
  81.2 13.1 %collective-permute-start.18 = (f32[2,64,1024]{2,1,0:T(8,128)S(1)}, f32[2,64,1024]{2,1,0:T(8,128)S(1)}, u32[]{:S(2)}, u32[]{:S(2)}) collective-permute-start(f32[2,64,1024]{2,1,0:T(8,128)S(1)} %pad_maximum_fusion.2.refs_0_), channel_id=1, source_target_pairs={{96,0},{112,16},{0,32},{16,48},{32,64},{48,80},{64,96},{80,112},{9... | collective-permute-start | bytes 1572872 | tf_op jit(solution)/shard_map/ppermute | solution.py:488
  81.3 13.1 %collective-permute-start.16 = (f32[2,64,1024]{2,1,0:T(8,128)S(1)}, f32[2,64,1024]{2,1,0:T(8,128)S(1)}, u32[]{:S(2)}, u32[]{:S(2)}) collective-permute-start(f32[2,64,1024]{2,1,0:T(8,128)S(1)} %pad_maximum_fusion.2.refs_0_), channel_id=1, source_target_pairs={{32,0},{48,16},{64,32},{80,48},{96,64},{112,80},{0,96},{16,112},{3... | collective-permute-start | bytes 1572872 | tf_op jit(solution)/shard_map/ppermute | solution.py:488
  84.0 16.5 %collective-permute-start.15 = (f32[8,2,64,128]{3,2,1,0:T(8,128)S(1)}, f32[8,2,64,128]{3,2,1,0:T(8,128)S(1)}, u32[]{:S(2)}, u32[]{:S(2)}) collective-permute-start(f32[8,2,64,128]{3,2,1,0:T(8,128)S(1)} %bitcast.50), channel_id=1, source_target_pairs={{0,1},{1,0},{2,3},{3,2},{4,5},{5,4},{6,7},{7,6},{8,9},{9,8},{10,11... | collective-permute-start | bytes 1572872 | tf_op jit(solution)/shard_map/ppermute | solution.py:492
  86.1 11.1 %collective-permute-start.27 = (f32[64,1024]{1,0:T(8,128)S(1)}, f32[64,1024]{1,0:T(8,128)S(1)}, u32[]{:S(2)}, u32[]{:S(2)}) collective-permute-start(f32[64,1024]{1,0:T(8,128)S(1)} %slice_bitcast_fusion.2), channel_id=1, source_target_pairs={{12,0},{13,1},{14,2},{15,3},{0,4},{1,5},{2,6},{3,7},{4,8},{5,9},{6... | collective-permute-start | bytes 786440 | tf_op jit(solution)/shard_map/ppermute | solution.py:488
  89.2 11.2 %collective-permute-start.25 = (f32[64,1024]{1,0:T(8,128)S(1)}, f32[64,1024]{1,0:T(8,128)S(1)}, u32[]{:S(2)}, u32[]{:S(2)}) collective-permute-start(f32[64,1024]{1,0:T(8,128)S(1)} %slice_bitcast_fusion.3), channel_id=1, source_target_pairs={{4,0},{5,1},{6,2},{7,3},{8,4},{9,5},{10,6},{11,7},{12,8},{13,9},{1... | collective-permute-start | bytes 786440 | tf_op jit(solution)/shard_map/ppermute | solution.py:488
  94.4 10.4 %collective-permute-start.17 = (f32[64,1024]{1,0:T(8,128)S(1)}, f32[64,1024]{1,0:T(8,128)S(1)}, u32[]{:S(2)}, u32[]{:S(2)}) collective-permute-start(f32[64,1024]{1,0:T(8,128)S(1)} %slice_bitcast_fusion.5), channel_id=1, source_target_pairs={{32,0},{48,16},{64,32},{80,48},{96,64},{112,80},{0,96},{16,112},{3... | collective-permute-start | bytes 786440 | tf_op jit(solution)/shard_map/ppermute | solution.py:488
  97.3 27.8 %collective-permute-start.28 = (f32[2,64,1024]{2,1,0:T(8,128)S(1)}, f32[2,64,1024]{2,1,0:T(8,128)S(1)}, u32[]{:S(2)}, u32[]{:S(2)}) collective-permute-start(f32[2,64,1024]{2,1,0:T(8,128)S(1)} %pad_maximum_fusion.3.refs_0_), channel_id=1, source_target_pairs={{0,1},{1,0},{2,3},{3,2},{4,5},{5,4},{6,7},{7,6},{8,9},{9,8},{10,11... | collective-permute-start | bytes 1572872 | tf_op jit(solution)/shard_map/ppermute | solution.py:492
  100.4 25.8 %collective-permute-start.21 = (f32[2304,128]{1,0:T(8,128)S(1)}, f32[2304,128]{1,0:T(8,128)S(1)}, u32[]{:S(2)}, u32[]{:S(2)}) collective-permute-start(f32[2304,128]{1,0:T(8,128)S(1)} %get-tuple-element.52), channel_id=1, source_target_pairs={{15,0},{0,1},{1,2},{2,3},{3,4},{4,5},{5,6},{6,7},{7,8},{8,9},{9,10... | collective-permute-start | bytes 3538952 | tf_op jit(solution)/shard_map/ppermute | solution.py:488
  100.5 29.8 %collective-permute-start.22 = (f32[2304,128]{1,0:T(8,128)S(1)}, f32[2304,128]{1,0:T(8,128)S(1)}, u32[]{:S(2)}, u32[]{:S(2)}) collective-permute-start(f32[2304,128]{1,0:T(8,128)S(1)} %get-tuple-element.54), channel_id=1, source_target_pairs={{1,0},{2,1},{3,2},{4,3},{5,4},{6,5},{7,6},{8,7},{9,8},{10,9},{11,1... | collective-permute-start | bytes 3538952 | tf_op jit(solution)/shard_map/ppermute | solution.py:488
  101.1 23.9 %collective-permute-start.29 = (f32[2,2,64,1024]{3,2,1,0:T(8,128)S(1)}, f32[2,2,64,1024]{3,2,1,0:T(8,128)S(1)}, u32[]{:S(2)}, u32[]{:S(2)}) collective-permute-start(f32[2,2,64,1024]{3,2,1,0:T(8,128)S(1)} %pad_maximum_fusion), channel_id=1, source_target_pairs={{0,1},{1,0},{2,3},{3,2},{4,5},{5,4},{6,7},{7,6},{8,9},{9,8},{10,11... | collective-permute-start | bytes 3145736 | tf_op jit(solution)/shard_map/ppermute | solution.py:492
  104.8 20.3 %collective-permute-start.30 = (f32[2,64,1024]{2,1,0:T(8,128)S(1)}, f32[2,64,1024]{2,1,0:T(8,128)S(1)}, u32[]{:S(2)}, u32[]{:S(2)}) collective-permute-start(f32[2,64,1024]{2,1,0:T(8,128)S(1)} %pad_maximum_fusion.4), channel_id=1, source_target_pairs={{0,1},{1,0},{2,3},{3,2},{4,5},{5,4},{6,7},{7,6},{8,9},{9,8},{10,11... | collective-permute-start | bytes 1572872 | tf_op jit(solution)/shard_map/ppermute | solution.py:492
  (23 other events, 237.7 us)

commit v5 on v4

--- a/solution.py
+++ b/solution.py
@@ -66,7 +66,7 @@
         count[home] = n + 1
         return carry
 
-    lax.fori_loop(0, M, put, 0, unroll=16)
+    lax.fori_loop(0, M, put, 0, unroll=64)
     for copy in copies:
         copy.wait()
 
@@ -107,7 +107,7 @@
         aux_ref[pl.ds(s, 1), :] = row
         return carry
 
-    lax.fori_loop(0, HALF, one, 0, unroll=4)
+    lax.fori_loop(0, HALF, one, 0, unroll=8)
     base = (c // 4) * WMAX
 
     def three(t, row):
@@ -200,7 +200,8 @@
     x = x + jnp.where(lane.astype(F32) == aux_ref[:, 3:4], aux_ref[:, 2:3], 0.0)
     x_ref[...] = x
     pick = lax.broadcasted_iota(jnp.int32, (cols, NGY), 0) == target_ref[...]
-    g_ref[...] = jnp.dot(x, pick.astype(F32), precision=HI, preferred_element_type=F32)
+    pick = pick.astype(BF16)
+    g_ref[...] = sum_of([bdot(part, pick) for part in three(x)])
 
 
 def well_cols(z, zl, zr, coef, aux, target):

time: 144 us -> 145 us (level)
  no operation moved by 1% of the time
where the time goes in v5:
time: 145 us; the launch traced here: 144 us
  starting transfers between devices  54.6 us (38%)
  Pallas kernels  47.3 us (33%)
  waiting for transfers between devices  34.4 us (24%)
  other arithmetic  3.78 us (3%)
  local copies, waits for them, and re-layouts  3.47 us (2%)
    ppermute x22, starting transfers between devices, shift(): lax.ppermute(x, axis, [((i + back) % count, i) for i in range(count)])  32.3 us
    ppermute x22, waiting for transfers between devices, shift(): lax.ppermute(x, axis, [((i + back) % count, i) for i in range(count)])  19.5 us
    pallas_call x1, Pallas kernels, inverse(): pl.pallas_call(inverse_kernel, out_shape=jax.ShapeDtypeStruct((M, M), F32...  16.8 us
    ppermute x7, starting transfers between devices, flip(): return lax.ppermute(x, axis, [(i, i ^ bit) for i in range(count)])  15.5 us
    pallas_call x1, Pallas kernels, update(): pl.pallas_call(update_kernel, out_shape=jax.ShapeDtypeStruct((rows, cols)...  13.5 us
    ppermute x1, waiting for transfers between devices, shards(): first = lax.ppermute(x, ('row', 'col'), turn)  10.6 us
    pallas_call x1, Pallas kernels, tables(): pl.pallas_call(table_kernel, out_shape=(jax.ShapeDtypeStruct((HALF, cols)...  9.16 us
    ppermute x7, waiting for transfers between devices, flip(): return lax.ppermute(x, axis, [(i, i ^ bit) for i in range(count)])  4.37 us
  transfers between devices with their start and end apart: 31, of which 11 were waited for; matrix products, arithmetic and copies ran while one was open for 4% of the time, Pallas kernels for 16%

profile of v5, /device:TPU:3, one launch (start us, length us, event | category | flops | bytes accessed | tf_op | source)
XLA Modules:
  0.0 144.0 jit_solution(14726320818058610827)
XLA Ops:
  0.7 9.2 %tables.1 = (f32[64,1024]{1,0:T(8,128)}, f32[32,1024]{1,0:T(8,128)}, f32[32,1024]{1,0:T(8,128)}, f32[64,128]{1,0:T(8,128)}, s32[1,128]{1,0:T(1,128)}, /*index=5*...) custom-call(s32[2]{0:T(128)} %pad_add_fusion.1.place, s32[1,256]{1,0:T(1,128)} %wells.1, ...), custom_call_target="tpu_custom_call" | custom-call | flops 1048576 | bytes 2097152 | tf_op jit(solution)/shard_map/tables/pallas_call | solution.py:123
  11.2 3.6 %collective-permute-start.1 = (f32[32,1024]{1,0:T(8,128)}, f32[32,1024]{1,0:T(8,128)S(1)}, u32[]{:S(2)}, u32[]{:S(2)}) collective-permute-start(f32[32,1024]{1,0:T(8,128)} %get-tuple-element.32), channel_id=1, source_target_pairs={{16,0},{32,16},{48,32},{64,48},{80,64},{96,80},{112,96},{0,112},{1... | collective-permute-start | bytes 393224 | tf_op jit(solution)/shard_map/ppermute | solution.py:489
  21.2 4.4 %collective-permute-start.2 = (f32[64,128]{1,0:T(8,128)}, f32[64,128]{1,0:T(8,128)S(1)}, u32[]{:S(2)}, u32[]{:S(2)}) collective-permute-start(f32[64,128]{1,0:T(8,128)} %get-tuple-element.39), channel_id=1, source_target_pairs={{15,0},{0,1},{1,2},{2,3},{3,4},{4,5},{5,6},{6,7},{7,8},{8,9},{9,10... | collective-permute-start | bytes 98312 | tf_op jit(solution)/shard_map/ppermute | solution.py:489
  28.5 2.2 %collective-permute-done.3.zr_ref = f32[64,128]{1,0:T(8,128)S(1)} collective-permute-done((f32[64,128]{1,0:T(8,128)}, f32[64,128]{1,0:T(8,128)S(1)}, u32[]{:S(2)}, u32[]{:S(2)}) %collective-permute-start.3) | collective-permute-done | bytes 32800 | tf_op jit(solution)/shard_map/ppermute | solution.py:489
  31.3 2.1 %well_cols.1 = (f32[64,1024]{1,0:T(8,128)}, f32[64,128]{1,0:T(8,128)}) custom-call(f32[64,1024]{1,0:T(8,128)} %get-tuple-element.37.z_ref, f32[64,128]{1,0:T(8,128)} %copy-done.8, f32[64,128]{1,0:T(8,128)} %copy-done.9, f32[5,1024]{1,0:T(8,128)} %constant_dynamic-slice_fusion.1.coef_ref.cc_ref, f32[64,128]{1,0:T(8,128)} %get-tuple-element.35.aux_ref, ...), custom_call_target="tpu_custom_call" | custom-call | flops 100663296 | bytes 1048576 | tf_op jit(solution)/shard_map/well_cols/pallas_call | solution.py:209
  38.2 3.5 %collective-permute-start.8 = (f32[64,1024]{1,0:T(8,128)}, f32[64,1024]{1,0:T(8,128)S(1)}, u32[]{:S(2)}, u32[]{:S(2)}) collective-permute-start(f32[64,1024]{1,0:T(8,128)} %get-tuple-element.43), channel_id=1, source_target_pairs={{0,0},{1,1},{2,16},{3,17},{4,36},{5,37},{6,52},{7,53},{8,72},{9,73... | collective-permute-start | bytes 786440 | tf_op jit(solution)/shard_map/ppermute | solution.py:545
  41.8 2.7 %collective-permute-start.20 = (f32[128,1024]{1,0:T(8,128)S(1)}, f32[128,1024]{1,0:T(8,128)S(1)}, u32[]{:S(2)}, u32[]{:S(2)}) collective-permute-start(f32[128,1024]{1,0:T(8,128)S(1)} %copy-done.12), channel_id=1, source_target_pairs={{112,0},{0,16},{16,32},{32,48},{48,64},{64,80},{80,96},{96,112},{1... | collective-permute-start | bytes 1572872 | tf_op jit(solution)/shard_map/ppermute | solution.py:489
  44.5 3.2 %collective-permute-start.23 = (f32[64,1024]{1,0:T(8,128)S(1)}, f32[64,1024]{1,0:T(8,128)S(1)}, u32[]{:S(2)}, u32[]{:S(2)}) collective-permute-start(f32[64,1024]{1,0:T(8,128)S(1)} %collective-permute-done.7), channel_id=1, source_target_pairs={{0,0},{1,1},{2,16},{3,17},{4,36},{5,37},{6,52},{7,53},{8,72},{9,73... | collective-permute-start | bytes 786440 | tf_op jit(solution)/shard_map/ppermute | solution.py:547
  48.5 10.6 %collective-permute-done.8 = f32[64,1024]{1,0:T(8,128)S(1)} collective-permute-done((f32[64,1024]{1,0:T(8,128)}, f32[64,1024]{1,0:T(8,128)S(1)}, u32[]{:S(2)}, u32[]{:S(2)}) %collective-permute-start.8) | collective-permute-done | bytes 262176 | tf_op jit(solution)/shard_map/ppermute | solution.py:545
  60.3 3.1 %collective-permute-done.10 = f32[64,128]{1,0:T(8,128)S(1)} collective-permute-done((f32[64,128]{1,0:T(8,128)S(1)}, f32[64,128]{1,0:T(8,128)S(1)}, u32[]{:S(2)}, u32[]{:S(2)}) %collective-permute-start.10) | collective-permute-done | bytes 32800 | tf_op jit(solution)/shard_map/ppermute | solution.py:493
  63.4 5.6 %collective-permute-start.11 = (f32[2,64,128]{2,1,0:T(8,128)S(1)}, f32[2,64,128]{2,1,0:T(8,128)S(1)}, u32[]{:S(2)}, u32[]{:S(2)}) collective-permute-start(f32[2,64,128]{2,1,0:T(8,128)S(1)} %get-tuple-element.74), channel_id=1, source_target_pairs={{0,16},{16,0},{32,48},{48,32},{64,80},{80,64},{96,112},{112,96},{1... | collective-permute-start | bytes 196616 | tf_op jit(solution)/shard_map/ppermute | solution.py:493
  71.3 4.1 %collective-permute-start.13 = (f32[2,2,64,128]{3,2,1,0:T(8,128)S(1)}, f32[2,2,64,128]{3,2,1,0:T(8,128)S(1)}, u32[]{:S(2)}, u32[]{:S(2)}) collective-permute-start(f32[2,2,64,128]{3,2,1,0:T(8,128)S(1)} %get-tuple-element.72), channel_id=1, source_target_pairs={{64,0},{80,16},{96,32},{112,48},{0,64},{16,80},{32,96},{48,112},{6... | collective-permute-start | bytes 393224 | tf_op jit(solution)/shard_map/ppermute | solution.py:489
  77.6 3.5 %collective-permute-done.13 = f32[2,2,64,128]{3,2,1,0:T(8,128)S(1)} collective-permute-done((f32[2,2,64,128]{3,2,1,0:T(8,128)S(1)}, f32[2,2,64,128]{3,2,1,0:T(8,128)S(1)}, u32[]{:S(2)}, u32[]{:S(2)}) %collective-permute-start.13) | collective-permute-done | bytes 131104 | tf_op jit(solution)/shard_map/ppermute | solution.py:489
  81.2 2.7 %collective-permute-start.16 = (f32[2,64,1024]{2,1,0:T(8,128)S(1)}, f32[2,64,1024]{2,1,0:T(8,128)S(1)}, u32[]{:S(2)}, u32[]{:S(2)}) collective-permute-start(f32[2,64,1024]{2,1,0:T(8,128)S(1)} %pad_maximum_fusion.2.refs_0_), channel_id=1, source_target_pairs={{32,0},{48,16},{64,32},{80,48},{96,64},{112,80},{0,96},{16,112},{3... | collective-permute-start | bytes 1572872 | tf_op jit(solution)/shard_map/ppermute | solution.py:489
  84.0 2.1 %collective-permute-start.15 = (f32[8,2,64,128]{3,2,1,0:T(8,128)S(1)}, f32[8,2,64,128]{3,2,1,0:T(8,128)S(1)}, u32[]{:S(2)}, u32[]{:S(2)}) collective-permute-start(f32[8,2,64,128]{3,2,1,0:T(8,128)S(1)} %bitcast.50), channel_id=1, source_target_pairs={{0,1},{1,0},{2,3},{3,2},{4,5},{5,4},{6,7},{7,6},{8,9},{9,8},{10,11... | collective-permute-start | bytes 1572872 | tf_op jit(solution)/shard_map/ppermute | solution.py:493
  86.5 2.6 %collective-permute-done.24.refs_1_ = f32[2,64,1024]{2,1,0:T(8,128)S(1)} collective-permute-done((f32[2,64,1024]{2,1,0:T(8,128)S(1)}, f32[2,64,1024]{2,1,0:T(8,128)S(1)}, u32[]{:S(2)}, u32[]{:S(2)}) %collective-permute-start.24) | collective-permute-done | bytes 524320 | tf_op jit(solution)/shard_map/ppermute | solution.py:489
  89.5 4.7 %collective-permute-done.18.refs_4_ = f32[2,64,1024]{2,1,0:T(8,128)S(1)} collective-permute-done((f32[2,64,1024]{2,1,0:T(8,128)S(1)}, f32[2,64,1024]{2,1,0:T(8,128)S(1)}, u32[]{:S(2)}, u32[]{:S(2)}) %collective-permute-start.18) | collective-permute-done | bytes 524320 | tf_op jit(solution)/shard_map/ppermute | solution.py:489
  94.4 2.9 %collective-permute-start.17 = (f32[64,1024]{1,0:T(8,128)S(1)}, f32[64,1024]{1,0:T(8,128)S(1)}, u32[]{:S(2)}, u32[]{:S(2)}) collective-permute-start(f32[64,1024]{1,0:T(8,128)S(1)} %slice_bitcast_fusion.5), channel_id=1, source_target_pairs={{32,0},{48,16},{64,32},{80,48},{96,64},{112,80},{0,96},{16,112},{3... | collective-permute-start | bytes 786440 | tf_op jit(solution)/shard_map/ppermute | solution.py:489
  97.4 3.1 %collective-permute-start.28 = (f32[2,64,1024]{2,1,0:T(8,128)S(1)}, f32[2,64,1024]{2,1,0:T(8,128)S(1)}, u32[]{:S(2)}, u32[]{:S(2)}) collective-permute-start(f32[2,64,1024]{2,1,0:T(8,128)S(1)} %pad_maximum_fusion.3.refs_0_), channel_id=1, source_target_pairs={{0,1},{1,0},{2,3},{3,2},{4,5},{5,4},{6,7},{7,6},{8,9},{9,8},{10,11... | collective-permute-start | bytes 1572872 | tf_op jit(solution)/shard_map/ppermute | solution.py:493
  101.2 3.7 %collective-permute-start.29 = (f32[2,2,64,1024]{3,2,1,0:T(8,128)S(1)}, f32[2,2,64,1024]{3,2,1,0:T(8,128)S(1)}, u32[]{:S(2)}, u32[]{:S(2)}) collective-permute-start(f32[2,2,64,1024]{3,2,1,0:T(8,128)S(1)} %pad_maximum_fusion), channel_id=1, source_target_pairs={{0,1},{1,0},{2,3},{3,2},{4,5},{5,4},{6,7},{7,6},{8,9},{9,8},{10,11... | collective-permute-start | bytes 3145736 | tf_op jit(solution)/shard_map/ppermute | solution.py:493
  105.0 16.8 %inverse.1.inv_ref = f32[256,256]{1,0:T(8,128)S(1)} custom-call(f32[8,2,64,128]{3,2,1,0:T(8,128)S(1)} %bitcast.51, f32[8,2,64,128]{3,2,1,0:T(8,128)S(1)} %collective-permute-done.15.other_ref, s32[256,1]{1,0:T(8,128)S(1)} %fusion.7.rslot_ref.slot_ref, s32[1,256]{1,0:T(1,128)S(1)} %add_add_fusion.2.cslot_ref, f32[1,256]{1,0:T(1,128)S(1)} %copy-done.1), custom_call_target="tpu_custom_call" | custom-call | flops 18447998976 | bytes 4194304 | tf_op jit(solution)/shard_map/inverse/pallas_call | solution.py:331
  122.6 2.4 %across.1 = (bf16[256,1024]{1,0:T(8,128)(2,1)S(1)}, bf16[256,1024]{1,0:T(8,128)(2,1)S(1)}) custom-call(s32[256,1]{1,0:T(8,128)S(1)} %fusion.7.rslot_ref.slot_ref, f32[256,256]{1,0:T(8,128)S(1)} %inverse.1.inv_ref, f32[2,64,1024]{2,1,0:T(8,128)S(1)} %pad_maximum_fusion.2.refs_0_, f32[2,64,1024]{2,1,0:T(8,128)S(1)} %collective-permute-done.16.refs_1_, ...), custom_call_target="tpu_custom_call" | custom-call | flops 805306368 | bytes 6291456 | tf_op jit(solution)/shard_map/across/pallas_call | solution.py:371
  126.3 4.1 %collective-permute-done.22.er_ref = f32[2304,128]{1,0:T(8,128)S(1)} collective-permute-done((f32[2304,128]{1,0:T(8,128)S(1)}, f32[2304,128]{1,0:T(8,128)S(1)}, u32[]{:S(2)}, u32[]{:S(2)}) %collective-permute-start.22) | collective-permute-done | bytes 1179680 | tf_op jit(solution)/shard_map/ppermute | solution.py:489
  130.5 13.5 %update.1 = f32[2048,1024]{1,0:T(8,128)} custom-call(s32[2]{0:T(128)S(1)} %pad_add_fusion.place, f32[2048,1024]{1,0:T(8,128)S(1)} %bitcast.45, f32[1,1024]{1,0:T(1,128)S(1)} %dynamic-slice.proc_ref, bf16[256,1024]{1,0:T(8,128)(2,1)S(1)} %get-tuple-element.48.uh, bf16[256,1024]{1,0:T(8,128)(2,1)S(1)} %get-tuple-element.49.ul, f32[2048,8]{1,0:T(8,128)S(1)} %copy.19.rc_ref, ...), custom_call_target="tpu_custom_call" | custom-call | flops 3221225472 | bytes 16777216 | tf_op jit(solution)/shard_map/update/pallas_call | solution.py:469
  (111 shorter events, 26.9 us)
Async XLA Ops:
  9.8 8.3 %collective-permute-start = (f32[32,1024]{1,0:T(8,128)}, f32[32,1024]{1,0:T(8,128)S(1)}, u32[]{:S(2)}, u32[]{:S(2)}) collective-permute-start(f32[32,1024]{1,0:T(8,128)} %get-tuple-element.36), channel_id=1, source_target_pairs={{112,0},{0,16},{16,32},{32,48},{48,64},{64,80},{80,96},{96,112},{1... | collective-permute-start | bytes 393224 | tf_op jit(solution)/shard_map/ppermute | solution.py:489
  11.2 7.4 %collective-permute-start.1 = (f32[32,1024]{1,0:T(8,128)}, f32[32,1024]{1,0:T(8,128)S(1)}, u32[]{:S(2)}, u32[]{:S(2)}) collective-permute-start(f32[32,1024]{1,0:T(8,128)} %get-tuple-element.32), channel_id=1, source_target_pairs={{16,0},{32,16},{48,32},{64,48},{80,64},{96,80},{112,96},{0,112},{1... | collective-permute-start | bytes 393224 | tf_op jit(solution)/shard_map/ppermute | solution.py:489
  21.2 7.3 %collective-permute-start.2 = (f32[64,128]{1,0:T(8,128)}, f32[64,128]{1,0:T(8,128)S(1)}, u32[]{:S(2)}, u32[]{:S(2)}) collective-permute-start(f32[64,128]{1,0:T(8,128)} %get-tuple-element.39), channel_id=1, source_target_pairs={{15,0},{0,1},{1,2},{2,3},{3,4},{4,5},{5,6},{6,7},{7,8},{8,9},{9,10... | collective-permute-start | bytes 98312 | tf_op jit(solution)/shard_map/ppermute | solution.py:489
  26.1 33.0 %collective-permute-start.9 = (f32[128,1024]{1,0:T(8,128)S(1)}, f32[128,1024]{1,0:T(8,128)S(1)}, u32[]{:S(2)}, u32[]{:S(2)}) collective-permute-start(f32[128,1024]{1,0:T(8,128)S(1)} %copy-done.13), channel_id=1, source_target_pairs={{16,0},{32,16},{48,32},{64,48},{80,64},{96,80},{112,96},{0,112},{1... | collective-permute-start | bytes 1572872 | tf_op jit(solution)/shard_map/ppermute | solution.py:489
  34.6 10.0 %collective-permute-start.7 = (f32[64,1024]{1,0:T(8,128)}, f32[64,1024]{1,0:T(8,128)S(1)}, u32[]{:S(2)}, u32[]{:S(2)}) collective-permute-start(f32[64,1024]{1,0:T(8,128)} %get-tuple-element.43), channel_id=1, source_target_pairs={{0,16},{16,0},{32,48},{48,32},{64,80},{80,64},{96,112},{112,96},{1... | collective-permute-start | bytes 786440 | tf_op jit(solution)/shard_map/ppermute | solution.py:493
  36.3 11.5 %collective-permute-start.4 = (f32[64,128]{1,0:T(8,128)}, f32[64,128]{1,0:T(8,128)S(1)}, u32[]{:S(2)}, u32[]{:S(2)}) collective-permute-start(f32[64,128]{1,0:T(8,128)} %get-tuple-element.42), channel_id=1, source_target_pairs={{4,0},{5,1},{6,2},{7,3},{8,4},{9,5},{10,6},{11,7},{12,8},{13,9},{1... | collective-permute-start | bytes 98312 | tf_op jit(solution)/shard_map/ppermute | solution.py:489
  38.2 20.9 %collective-permute-start.8 = (f32[64,1024]{1,0:T(8,128)}, f32[64,1024]{1,0:T(8,128)S(1)}, u32[]{:S(2)}, u32[]{:S(2)}) collective-permute-start(f32[64,1024]{1,0:T(8,128)} %get-tuple-element.43), channel_id=1, source_target_pairs={{0,0},{1,1},{2,16},{3,17},{4,36},{5,37},{6,52},{7,53},{8,72},{9,73... | collective-permute-start | bytes 786440 | tf_op jit(solution)/shard_map/ppermute | solution.py:545
  41.8 35.7 %collective-permute-start.20 = (f32[128,1024]{1,0:T(8,128)S(1)}, f32[128,1024]{1,0:T(8,128)S(1)}, u32[]{:S(2)}, u32[]{:S(2)}) collective-permute-start(f32[128,1024]{1,0:T(8,128)S(1)} %copy-done.12), channel_id=1, source_target_pairs={{112,0},{0,16},{16,32},{32,48},{48,64},{64,80},{80,96},{96,112},{1... | collective-permute-start | bytes 1572872 | tf_op jit(solution)/shard_map/ppermute | solution.py:489
  44.5 24.5 %collective-permute-start.23 = (f32[64,1024]{1,0:T(8,128)S(1)}, f32[64,1024]{1,0:T(8,128)S(1)}, u32[]{:S(2)}, u32[]{:S(2)}) collective-permute-start(f32[64,1024]{1,0:T(8,128)S(1)} %collective-permute-done.7), channel_id=1, source_target_pairs={{0,0},{1,1},{2,16},{3,17},{4,36},{5,37},{6,52},{7,53},{8,72},{9,73... | collective-permute-start | bytes 786440 | tf_op jit(solution)/shard_map/ppermute | solution.py:547
  63.4 7.8 %collective-permute-start.11 = (f32[2,64,128]{2,1,0:T(8,128)S(1)}, f32[2,64,128]{2,1,0:T(8,128)S(1)}, u32[]{:S(2)}, u32[]{:S(2)}) collective-permute-start(f32[2,64,128]{2,1,0:T(8,128)S(1)} %get-tuple-element.74), channel_id=1, source_target_pairs={{0,16},{16,0},{32,48},{48,32},{64,80},{80,64},{96,112},{112,96},{1... | collective-permute-start | bytes 196616 | tf_op jit(solution)/shard_map/ppermute | solution.py:493
  69.1 17.0 %collective-permute-start.26 = (f32[2,64,1024]{2,1,0:T(8,128)S(1)}, f32[2,64,1024]{2,1,0:T(8,128)S(1)}, u32[]{:S(2)}, u32[]{:S(2)}) collective-permute-start(f32[2,64,1024]{2,1,0:T(8,128)S(1)} %pad_maximum_fusion.3.refs_0_), channel_id=1, source_target_pairs={{12,0},{13,1},{14,2},{15,3},{0,4},{1,5},{2,6},{3,7},{4,8},{5,9},{6... | collective-permute-start | bytes 1572872 | tf_op jit(solution)/shard_map/ppermute | solution.py:489
  71.3 9.7 %collective-permute-start.13 = (f32[2,2,64,128]{3,2,1,0:T(8,128)S(1)}, f32[2,2,64,128]{3,2,1,0:T(8,128)S(1)}, u32[]{:S(2)}, u32[]{:S(2)}) collective-permute-start(f32[2,2,64,128]{3,2,1,0:T(8,128)S(1)} %get-tuple-element.72), channel_id=1, source_target_pairs={{64,0},{80,16},{96,32},{112,48},{0,64},{16,80},{32,96},{48,112},{6... | collective-permute-start | bytes 393224 | tf_op jit(solution)/shard_map/ppermute | solution.py:489
  77.5 11.7 %collective-permute-start.24 = (f32[2,64,1024]{2,1,0:T(8,128)S(1)}, f32[2,64,1024]{2,1,0:T(8,128)S(1)}, u32[]{:S(2)}, u32[]{:S(2)}) collective-permute-start(f32[2,64,1024]{2,1,0:T(8,128)S(1)} %pad_maximum_fusion.3.refs_0_), channel_id=1, source_target_pairs={{4,0},{5,1},{6,2},{7,3},{8,4},{9,5},{10,6},{11,7},{12,8},{13,9},{1... | collective-permute-start | bytes 1572872 | tf_op jit(solution)/shard_map/ppermute | solution.py:489
  81.1 13.1 %collective-permute-start.18 = (f32[2,64,1024]{2,1,0:T(8,128)S(1)}, f32[2,64,1024]{2,1,0:T(8,128)S(1)}, u32[]{:S(2)}, u32[]{:S(2)}) collective-permute-start(f32[2,64,1024]{2,1,0:T(8,128)S(1)} %pad_maximum_fusion.2.refs_0_), channel_id=1, source_target_pairs={{96,0},{112,16},{0,32},{16,48},{32,64},{48,80},{64,96},{80,112},{9... | collective-permute-start | bytes 1572872 | tf_op jit(solution)/shard_map/ppermute | solution.py:489
  81.2 13.1 %collective-permute-start.16 = (f32[2,64,1024]{2,1,0:T(8,128)S(1)}, f32[2,64,1024]{2,1,0:T(8,128)S(1)}, u32[]{:S(2)}, u32[]{:S(2)}) collective-permute-start(f32[2,64,1024]{2,1,0:T(8,128)S(1)} %pad_maximum_fusion.2.refs_0_), channel_id=1, source_target_pairs={{32,0},{48,16},{64,32},{80,48},{96,64},{112,80},{0,96},{16,112},{3... | collective-permute-start | bytes 1572872 | tf_op jit(solution)/shard_map/ppermute | solution.py:489
  84.0 16.7 %collective-permute-start.15 = (f32[8,2,64,128]{3,2,1,0:T(8,128)S(1)}, f32[8,2,64,128]{3,2,1,0:T(8,128)S(1)}, u32[]{:S(2)}, u32[]{:S(2)}) collective-permute-start(f32[8,2,64,128]{3,2,1,0:T(8,128)S(1)} %bitcast.50), channel_id=1, source_target_pairs={{0,1},{1,0},{2,3},{3,2},{4,5},{5,4},{6,7},{7,6},{8,9},{9,8},{10,11... | collective-permute-start | bytes 1572872 | tf_op jit(solution)/shard_map/ppermute | solution.py:493
  86.1 11.3 %collective-permute-start.27 = (f32[64,1024]{1,0:T(8,128)S(1)}, f32[64,1024]{1,0:T(8,128)S(1)}, u32[]{:S(2)}, u32[]{:S(2)}) collective-permute-start(f32[64,1024]{1,0:T(8,128)S(1)} %slice_bitcast_fusion.2), channel_id=1, source_target_pairs={{12,0},{13,1},{14,2},{15,3},{0,4},{1,5},{2,6},{3,7},{4,8},{5,9},{6... | collective-permute-start | bytes 786440 | tf_op jit(solution)/shard_map/ppermute | solution.py:489
  89.2 11.4 %collective-permute-start.25 = (f32[64,1024]{1,0:T(8,128)S(1)}, f32[64,1024]{1,0:T(8,128)S(1)}, u32[]{:S(2)}, u32[]{:S(2)}) collective-permute-start(f32[64,1024]{1,0:T(8,128)S(1)} %slice_bitcast_fusion.3), channel_id=1, source_target_pairs={{4,0},{5,1},{6,2},{7,3},{8,4},{9,5},{10,6},{11,7},{12,8},{13,9},{1... | collective-permute-start | bytes 786440 | tf_op jit(solution)/shard_map/ppermute | solution.py:489
  94.4 10.5 %collective-permute-start.17 = (f32[64,1024]{1,0:T(8,128)S(1)}, f32[64,1024]{1,0:T(8,128)S(1)}, u32[]{:S(2)}, u32[]{:S(2)}) collective-permute-start(f32[64,1024]{1,0:T(8,128)S(1)} %slice_bitcast_fusion.5), channel_id=1, source_target_pairs={{32,0},{48,16},{64,32},{80,48},{96,64},{112,80},{0,96},{16,112},{3... | collective-permute-start | bytes 786440 | tf_op jit(solution)/shard_map/ppermute | solution.py:489
  97.4 27.6 %collective-permute-start.28 = (f32[2,64,1024]{2,1,0:T(8,128)S(1)}, f32[2,64,1024]{2,1,0:T(8,128)S(1)}, u32[]{:S(2)}, u32[]{:S(2)}) collective-permute-start(f32[2,64,1024]{2,1,0:T(8,128)S(1)} %pad_maximum_fusion.3.refs_0_), channel_id=1, source_target_pairs={{0,1},{1,0},{2,3},{3,2},{4,5},{5,4},{6,7},{7,6},{8,9},{9,8},{10,11... | collective-permute-start | bytes 1572872 | tf_op jit(solution)/shard_map/ppermute | solution.py:493
  100.6 25.8 %collective-permute-start.21 = (f32[2304,128]{1,0:T(8,128)S(1)}, f32[2304,128]{1,0:T(8,128)S(1)}, u32[]{:S(2)}, u32[]{:S(2)}) collective-permute-start(f32[2304,128]{1,0:T(8,128)S(1)} %get-tuple-element.52), channel_id=1, source_target_pairs={{15,0},{0,1},{1,2},{2,3},{3,4},{4,5},{5,6},{6,7},{7,8},{8,9},{9,10... | collective-permute-start | bytes 3538952 | tf_op jit(solution)/shard_map/ppermute | solution.py:489
  100.6 29.8 %collective-permute-start.22 = (f32[2304,128]{1,0:T(8,128)S(1)}, f32[2304,128]{1,0:T(8,128)S(1)}, u32[]{:S(2)}, u32[]{:S(2)}) collective-permute-start(f32[2304,128]{1,0:T(8,128)S(1)} %get-tuple-element.54), channel_id=1, source_target_pairs={{1,0},{2,1},{3,2},{4,3},{5,4},{6,5},{7,6},{8,7},{9,8},{10,9},{11,1... | collective-permute-start | bytes 3538952 | tf_op jit(solution)/shard_map/ppermute | solution.py:489
  101.2 23.7 %collective-permute-start.29 = (f32[2,2,64,1024]{3,2,1,0:T(8,128)S(1)}, f32[2,2,64,1024]{3,2,1,0:T(8,128)S(1)}, u32[]{:S(2)}, u32[]{:S(2)}) collective-permute-start(f32[2,2,64,1024]{3,2,1,0:T(8,128)S(1)} %pad_maximum_fusion), channel_id=1, source_target_pairs={{0,1},{1,0},{2,3},{3,2},{4,5},{5,4},{6,7},{7,6},{8,9},{9,8},{10,11... | collective-permute-start | bytes 3145736 | tf_op jit(solution)/shard_map/ppermute | solution.py:493
  104.9 20.1 %collective-permute-start.30 = (f32[2,64,1024]{2,1,0:T(8,128)S(1)}, f32[2,64,1024]{2,1,0:T(8,128)S(1)}, u32[]{:S(2)}, u32[]{:S(2)}) collective-permute-start(f32[2,64,1024]{2,1,0:T(8,128)S(1)} %pad_maximum_fusion.4), channel_id=1, source_target_pairs={{0,1},{1,0},{2,3},{3,2},{4,5},{5,4},{6,7},{7,6},{8,9},{9,8},{10,11... | collective-permute-start | bytes 1572872 | tf_op jit(solution)/shard_map/ppermute | solution.py:493
  (23 other events, 237.9 us)
